TPU v7x, 128 devices: a whole 4x4x4 slice. The times are simulated.
128 devices in a mesh: dp: 8 (over x, core), seq: 16 (over y, z).
Axes of the slice: x: 4, y: 4, z: 4, core: 2. Of those that a mesh axis runs over, the one named last changes fastest.
Arguments:
- q_raw: bfloat16 [8, 2048, 4096], P('dp', 'seq'), may hold values from -64 to 64
- k_raw: bfloat16 [8, 2048, 4096], P('dp', 'seq'), may hold values from -64 to 64
- values: bfloat16 [8, 2048, 4096], P('dp', 'seq'), may hold values from -6 to 6
- grad_out: bfloat16 [8, 2048, 4096], P('dp', 'seq'), may hold values from -6 to 6
- q_gain: float32 [4096], replicated, may hold values from 0.1 to 1.9
- k_gain: float32 [4096], replicated, may hold values from 0.1 to 1.9
- lengths: int32 [8, 6], P('dp'), may hold values from 1 to 682, 2048 in all within a row
- positions: int32 [8, 3, 2048], P('dp', None, 'seq'), may hold values from 0 to 63
Outputs:
- attended: bfloat16 [8, 2048, 4096], P('dp', 'seq')
- grad_q: bfloat16 [8, 2048, 4096], P('dp', 'seq')
- grad_k: bfloat16 [8, 2048, 4096], P('dp', 'seq')
- grad_v: bfloat16 [8, 2048, 4096], P('dp', 'seq')
- grad_q_gain: float32 [4096], replicated
- grad_k_gain: float32 [4096], replicated
Inputs may be any that keep to these rules, and one draw needn't show every extreme that they name: `lengths`: the clips of a bucket lie end to end and fill its 2048 tokens.
All inputs are finite; a program needn't handle non-finite values.
Results may differ from a plain program's by a relative error of at most 0.012.
The roundings to bfloat16 on the way count: a program that leaves them out, or rounds other values in their place, can miss the bound.
Values may be sent and summed in bfloat16 or wider, within the bound.
No kernel may reach another device: no remote copies, remote signals or barrier semaphores. Data moves between devices by JAX's collectives and lax.ppermute only.
A program may use at most 128 MiB of HBM per device.

v0:
```python
import jax
import jax.numpy as jnp
from jax import lax
from jax.sharding import PartitionSpec as P

HEAD_DIM = 128


epsilon = 1e-06


def in_one_piece(arrays, axis, split_dim, concat_dim, along):
    ends, at = ([], 0)
    for a in arrays[:-1]:
        at += a.shape[along]
        ends.append(at)
    both = jnp.concatenate(arrays, axis=along)
    return tuple(
        jnp.split(
            lax.all_to_all(both, axis, split_axis=split_dim, concat_axis=concat_dim, tiled=True),
            ends,
            axis=along,
        )
    )


def in_order(pieces, dim):
    lengths = list(pieces.shape[1:])
    lengths[dim] *= pieces.shape[0]
    return jnp.moveaxis(pieces, 0, dim).reshape(lengths)


def sent_to_all(value, axis):
    count = lax.axis_size(axis)
    return lax.all_to_all(
        jnp.broadcast_to(value[None], (count, *value.shape)), axis, 0, 0, tiled=True
    )


def gather_directly(value, axis, dim):
    return in_order(sent_to_all(value, axis), dim)


def taken_together(value, axis):
    return sent_to_all(value, axis).sum(axis=0)


def packed_total(arrays, axis):
    ends = [0]
    for a in arrays:
        ends.append(ends[-1] + a.size)
    so_far = taken_together(jnp.concatenate([a.ravel() for a in arrays]), axis)
    return tuple((so_far[b:e].reshape(a.shape) for a, b, e in zip(arrays, ends, ends[1:])))


def in_blocks(value, dim, count):
    lengths = value.shape
    pieces = value.reshape(*lengths[:dim], count, lengths[dim] // count, *lengths[dim + 1 :])
    return jnp.moveaxis(pieces, dim, 0)


def piece_ends(length, count):
    step = length // count
    if step >= 8:
        step -= step % 8
    return [step * k for k in range(1, count)]


def exchange_in_pieces(value, axis, pieces, split_dim, concat_dim):
    blocks = in_blocks(value, split_dim, lax.axis_size(axis))
    split_at = max(range(1, max(2, blocks.ndim - 1)), key=lambda d: blocks.shape[d])
    finished = []
    for slab in jnp.split(blocks, piece_ends(blocks.shape[split_at], pieces), axis=split_at):
        if slab.size:
            finished.append(lax.all_to_all(slab, axis, split_axis=0, concat_axis=0, tiled=True))
    return in_order(jnp.concatenate(finished, axis=split_at), concat_dim)


def product(form, left, right):
    return jnp.einsum(form, left, right, preferred_element_type=jnp.float32)


def segment_ids(clip_lengths, tokens):
    boundary = jnp.cumsum(clip_lengths)
    places = jnp.arange(tokens, dtype=jnp.int32)
    return jnp.sum((boundary[None, :] <= places[:, None]).astype(jnp.int32), axis=1)


def rope_tables(position_rows, head_dim):
    half = head_dim // 2
    sixth = head_dim // 6
    first = half - 2 * sixth
    pairs = jnp.arange(half, dtype=jnp.int32)
    section = (pairs >= first).astype(jnp.int32) + (pairs >= first + sixth).astype(jnp.int32)
    begin = jnp.where(section == 0, 0, jnp.where(section == 1, first, first + sixth))
    number = jnp.where(section == 0, first, sixth)
    freqs = 10000.0 ** (-(pairs - begin).astype(jnp.float32) / number.astype(jnp.float32))
    picker = (section[None, :] == jnp.arange(3, dtype=jnp.int32)[:, None]).astype(
        jnp.float32
    ) * freqs[None, :]
    angle = lax.dot_general(
        position_rows.astype(jnp.float32),
        picker,
        (((0,), (0,)), ((), ())),
        precision=lax.Precision.HIGHEST,
    )
    cosine = jnp.cos(angle)
    sine = jnp.sin(angle)
    return (jnp.concatenate([cosine, cosine], axis=-1), jnp.concatenate([sine, sine], axis=-1))


def rotate_pairs(inputs, cosine, sine):
    half = inputs.shape[-1] // 2
    partner = jnp.concatenate([-inputs[..., half:], inputs[..., :half]], axis=-1)
    return inputs * cosine[:, None, :] + partner * sine[:, None, :]


def rotate_back(grads, cosine, sine):
    half = grads.shape[-1] // 2
    turned = grads * sine[:, None, :]
    return grads * cosine[:, None, :] + jnp.concatenate(
        [turned[..., half:], -turned[..., :half]], axis=-1
    )


def attention_forward(query, keys, value_rows, segment, block, window, reach):
    count = query.shape[0]
    scale = query.shape[2] ** (-0.5)

    def one_block(index_block):
        start = index_block * block
        key_start = jnp.clip(start - reach, 0, count - window)
        query_block = lax.dynamic_slice_in_dim(query, start, block, 0)
        key_window = lax.dynamic_slice_in_dim(keys, key_start, window, 0)
        value_window = lax.dynamic_slice_in_dim(value_rows, key_start, window, 0)
        query_clip = lax.dynamic_slice_in_dim(segment, start, block, 0)
        key_clip = lax.dynamic_slice_in_dim(segment, key_start, window, 0)
        scores = product("qhd,khd->hqk", query_block, key_window) * scale
        live = (query_clip[:, None] == key_clip[None, :])[None]
        scores = jnp.where(live, scores, -1e30)
        highest = jnp.max(scores, axis=-1, keepdims=True)
        expon = jnp.exp(scores - highest)
        totals = jnp.sum(expon, axis=-1, keepdims=True)
        weights = (expon / totals).astype(jnp.bfloat16)
        output = product("hqk,khd->qhd", weights, value_window)
        return (output, (highest + jnp.log(totals))[..., 0])

    outputs, logsum = lax.map(one_block, jnp.arange(count // block, dtype=jnp.int32))
    return (outputs.reshape(query.shape), logsum)


def attention_backward(
    query, keys, value_rows, context, cotangent, logsum, segment, block, window, reach
):
    count = query.shape[0]
    scale = query.shape[2] ** (-0.5)
    delta = jnp.sum(cotangent.astype(jnp.float32) * context.astype(jnp.float32), axis=-1)

    def one_block(carry, inputs):
        key_acc, value_acc = carry
        index_block, block_logsum = inputs
        start = index_block * block
        key_start = jnp.clip(start - reach, 0, count - window)
        query_block = lax.dynamic_slice_in_dim(query, start, block, 0)
        cot_block = lax.dynamic_slice_in_dim(cotangent, start, block, 0)
        delta_block = lax.dynamic_slice_in_dim(delta, start, block, 0)
        key_window = lax.dynamic_slice_in_dim(keys, key_start, window, 0)
        value_window = lax.dynamic_slice_in_dim(value_rows, key_start, window, 0)
        query_clip = lax.dynamic_slice_in_dim(segment, start, block, 0)
        key_clip = lax.dynamic_slice_in_dim(segment, key_start, window, 0)
        scores = product("qhd,khd->hqk", query_block, key_window) * scale
        live = (query_clip[:, None] == key_clip[None, :])[None]
        probs = jnp.where(live, jnp.exp(scores - block_logsum[:, :, None]), 0.0)
        prob_half = probs.astype(jnp.bfloat16)
        value_grad = product("hqk,qhd->khd", prob_half, cot_block)
        dprob = product("qhd,khd->hqk", cot_block, value_window)
        dscore = (probs * (dprob - jnp.transpose(delta_block)[:, :, None]) * scale).astype(
            jnp.bfloat16
        )
        query_grad = product("hqk,khd->qhd", dscore, key_window)
        key_grad = product("hqk,qhd->khd", dscore, query_block)
        key_acc = lax.dynamic_update_slice_in_dim(
            key_acc,
            lax.dynamic_slice_in_dim(key_acc, key_start, window, 0) + key_grad,
            key_start,
            0,
        )
        value_acc = lax.dynamic_update_slice_in_dim(
            value_acc,
            lax.dynamic_slice_in_dim(value_acc, key_start, window, 0) + value_grad,
            key_start,
            0,
        )
        return ((key_acc, value_acc), query_grad)

    zeros = jnp.zeros(query.shape, jnp.float32)
    indices = jnp.arange(count // block, dtype=jnp.int32)
    (key_acc, value_acc), query_grads = lax.scan(one_block, (zeros, zeros), (indices, logsum))
    return (query_grads.reshape(query.shape), key_acc, value_acc)


def on_device(q_raw, k_raw, values, grad_out, q_gain, k_gain, lengths, positions):
    members = lax.axis_size("seq")
    replicas = lax.axis_size("dp")
    tok_dev = q_raw.shape[1]
    feature = q_raw.shape[2]
    tokens = tok_dev * members
    share = feature // members
    local_heads = share // HEAD_DIM
    reach = tokens // 3
    block = min(512, tokens)
    window = min(tokens, block + 2 * reach)
    segment = segment_ids(lengths[0], tokens)
    sent = (q_raw, k_raw, values)
    got_query, got_key, got_value = in_one_piece((sent[0], sent[1], sent[2]), "seq", 2, 1, 0)
    every_position = gather_directly(positions, "seq", 2)
    cosine, sine = rope_tables(every_position[0], HEAD_DIM)
    query_float = got_query[0].astype(jnp.float32)
    key_float = got_key[0].astype(jnp.float32)
    query_total, key_total = packed_total(
        (jnp.sum(query_float * query_float, axis=-1), jnp.sum(key_float * key_float, axis=-1)),
        "seq",
    )
    query_scale = lax.rsqrt(query_total / feature + epsilon)
    key_scale = lax.rsqrt(key_total / feature + epsilon)
    offset = lax.axis_index("seq") * share
    query_gain = lax.dynamic_slice_in_dim(q_gain, offset, share)
    key_gain = lax.dynamic_slice_in_dim(k_gain, offset, share)
    query_hat = query_float * query_scale[:, None]
    key_hat = key_float * key_scale[:, None]
    query_heads = rotate_pairs(
        (query_hat * query_gain).reshape(tokens, local_heads, HEAD_DIM), cosine, sine
    ).astype(jnp.bfloat16)
    key_heads = rotate_pairs(
        (key_hat * key_gain).reshape(tokens, local_heads, HEAD_DIM), cosine, sine
    ).astype(jnp.bfloat16)
    value_heads = got_value[0].reshape(tokens, local_heads, HEAD_DIM)
    context, logsum = attention_forward(
        query_heads, key_heads, value_heads, segment, block, window, reach
    )
    context_half = context.astype(jnp.bfloat16)
    attended = exchange_in_pieces(context_half.reshape(1, tokens, share), "seq", 2, 1, 2)
    cotangent = lax.all_to_all(grad_out, "seq", split_axis=2, concat_axis=1, tiled=True)[0].reshape(
        tokens, local_heads, HEAD_DIM
    )
    query_grad, key_grad, value_grad = attention_backward(
        query_heads,
        key_heads,
        value_heads,
        context_half,
        cotangent,
        logsum,
        segment,
        block,
        window,
        reach,
    )
    query_half = query_grad.astype(jnp.bfloat16)
    key_half = key_grad.astype(jnp.bfloat16)
    value_half = value_grad.astype(jnp.bfloat16).reshape(1, tokens, share)
    query_back = rotate_back(
        lax.optimization_barrier(query_half).astype(jnp.float32), cosine, sine
    ).reshape(tokens, share)
    key_back = rotate_back(
        lax.optimization_barrier(key_half).astype(jnp.float32), cosine, sine
    ).reshape(tokens, share)
    query_part = jnp.sum(query_back * query_hat, axis=0)
    key_part = jnp.sum(key_back * key_hat, axis=0)
    query_lift = query_back * query_gain
    key_lift = key_back * key_gain
    query_inner, key_inner = packed_total(
        (jnp.sum(query_lift * query_hat, axis=-1), jnp.sum(key_lift * key_hat, axis=-1)), "seq"
    )
    query_input = query_scale[:, None] * (query_lift - query_hat * (query_inner / feature)[:, None])
    key_input = key_scale[:, None] * (key_lift - key_hat * (key_inner / feature)[:, None])
    sent_back = (
        query_input.astype(jnp.bfloat16).reshape(1, tokens, share),
        key_input.astype(jnp.bfloat16).reshape(1, tokens, share),
        value_half,
    )
    back_query, back_key, back_value = in_one_piece(
        (sent_back[0], sent_back[1], sent_back[2]), "seq", 1, 2, 0
    )
    summed = taken_together(jnp.stack([query_part, key_part]), "dp")
    gains = gather_directly(summed / replicas, "seq", 1)
    return (attended, back_query, back_key, back_value, gains[0], gains[1])


def solution(mesh):
    return jax.shard_map(
        on_device,
        mesh=mesh,
        in_specs=(
            P("dp", "seq", None),
            P("dp", "seq", None),
            P("dp", "seq", None),
            P("dp", "seq", None),
            P(),
            P(),
            P("dp", None),
            P("dp", None, "seq"),
        ),
        out_specs=(
            P("dp", "seq", None),
            P("dp", "seq", None),
            P("dp", "seq", None),
            P("dp", "seq", None),
            P(),
            P(),
        ),
        check_vma=False,
    )
```

profile of v0, /device:TPU:0, one launch (start us, length us, event | category | flops | bytes accessed | tf_op | source)
XLA Modules:
  0.0 491.4 jit_solution(15827931555533931733)
XLA Ops:
  1.9 8.1 %all-to-all-start.2 = ((s32[16,1,3,128]{3,1,2,0:T(1,128)}), s32[16,1,3,128]{3,1,2,0:T(1,128)S(1)}, u32[]{:S(2)}, u32[]{:S(2)}) async-start(s32[16,1,3,128]{3,1,2,0:T(1,128)} %broadcast_in_dim.134), calls=%async_computation.2 | async-start | bytes 49152 | tf_op jit(solution)/shard_map/all_to_all | solution.py:35
  10.1 5.0 %copy.206 = bf16[1,128,4096]{1,0,2:T(2,128)(2,1)S(1)} copy(bf16[1,128,4096]{2,1,0:T(8,128)(2,1)} %param.15) | data formatting | bytes 2097152 | tf_op args[3]
  15.6 22.4 %reduce.8 = bf16[4096,128]{1,0:T(8,128)(2,1)S(1)} reduce(bf16[4096,1,128]{2,1,0:T(2,128)(2,1)S(1)} %bitcast.147, bf16[]{:T(256)} %broadcast.352), dimensions={1}, to_apply=%bitcast.109.reduce_sub_computation | reduce | bytes 2097154
  39.1 7.2 %all-to-all-start.5 = ((bf16[16,2,16384]{2,1,0:T(2,128)(2,1)}), bf16[16,2,16384]{2,1,0:T(2,128)(2,1)S(1)}, u32[]{:S(2)}, u32[]{:S(2)}) async-start(bf16[16,2,16384]{2,1,0:T(2,128)(2,1)} %reshape.513), calls=%async_computation.5 | async-start | bytes 2097152 | tf_op jit(solution)/shard_map/all_to_all | solution.py:243
  46.4 5.0 %copy.189 = bf16[1,128,4096]{1,0,2:T(2,128)(2,1)S(1)} copy(bf16[1,128,4096]{2,1,0:T(8,128)(2,1)} %param.12) | data formatting | bytes 2097152 | tf_op args[0]
  51.4 5.5 %copy.190 = bf16[1,128,4096]{1,0,2:T(2,128)(2,1)} copy(bf16[1,128,4096]{2,1,0:T(8,128)(2,1)} %param.13) | data formatting | bytes 2097152 | tf_op args[1]
  56.9 5.5 %copy.191 = bf16[1,128,4096]{1,0,2:T(2,128)(2,1)} copy(bf16[1,128,4096]{2,1,0:T(8,128)(2,1)} %param.14) | data formatting | bytes 2097152 | tf_op args[2]
  62.4 9.4 %pad_maximum_fusion = bf16[3,128,4096]{1,0,2:T(4,128)(2,1)} fusion(bf16[1,128,4096]{1,0,2:T(2,128)(2,1)} %copy.191, bf16[1,128,4096]{1,0,2:T(2,128)(2,1)} %copy.190, bf16[1,128,4096]{1,0,2:T(2,128)(2,1)S(1)} %copy.189), kind=kLoop, calls=%fused_computation.47 | loop fusion | flops 9437184 | bytes 6291456 | tf_op jit(solution)/shard_map/concatenate | solution.py:17
  71.9 7.9 %all-to-all-start = ((bf16[3,128,4096]{1,0,2:T(4,128)(2,1)}), bf16[3,128,4096]{1,0,2:T(4,128)(2,1)}, u32[]{:S(2)}, u32[]{:S(2)}) async-start(bf16[3,128,4096]{1,0,2:T(4,128)(2,1)} %pad_maximum_fusion), calls=%async_computation | async-start | bytes 8388608 | tf_op jit(solution)/shard_map/all_to_all | solution.py:20
  89.5 45.0 %all-to-all-done = bf16[3,128,4096]{1,0,2:T(4,128)(2,1)} async-done(((bf16[3,128,4096]{1,0,2:T(4,128)(2,1)}), bf16[3,128,4096]{1,0,2:T(4,128)(2,1)}, u32[]{:S(2)}, u32[]{:S(2)}) %all-to-all-start) | async-done | bytes 3145760 | tf_op jit(solution)/shard_map/all_to_all | solution.py:20
  138.4 5.1 %all-to-all-start.1 = ((f32[16,1,4096]{2,1,0:T(1,128)}), f32[16,1,4096]{2,1,0:T(1,128)S(1)}, u32[]{:S(2)}, u32[]{:S(2)}) async-start(f32[16,1,4096]{2,1,0:T(1,128)} %broadcast_in_dim.131), calls=%async_computation.1 | async-start | bytes 524288 | tf_op jit(solution)/shard_map/all_to_all | solution.py:35
  154.4 4.9 copy.194
  171.4 41.7 %while.30 = (s32[]{:T(128)}, bf16[4,512,2,128]{1,3,2,0:T(8,128)(2,1)S(1)}, f32[4,2,512]{2,1,0:T(2,128)S(1)}, s32[4]{0:T(128)S(1)}, bf16[2048,2,128]{2,0,1:T(8,12...) while((s32[]{:T(128)}, ...), condition=%wide.region_8.9_spmd, body=%wide.region_5.8_spmd.sunk | while | flops 1007576064 | bytes 33882388 | solution.py:148
  217.9 120.5 %while.31 = (s32[]{:T(128)}, f32[2048,2,128]{2,0,1:T(8,128)}, f32[2048,2,128]{2,0,1:T(8,128)}, bf16[4,512,2,128]{3,1,0,2:T(8,128)(2,1)}, s32[4]{0:T(128)S(1)}, /...) while((s32[]{:T(128)}, f32[2048,2,128]{2,0,1:T(8,128)}, ...), condition=%wide.region_11.12_spmd, body=%wide.region_10.11_spmd.sunk | while | flops 2481963008 | bytes 90323368 | solution.py:198
  229.5 5.9 %dynamic_update_slice.44 = f32[2048,2,128]{2,0,1:T(8,128)} dynamic-update-slice(f32[2048,2,128]{2,0,1:T(8,128)} %get-tuple-element.685, f32[1876,2,128]{2,0,1:T(8,128)S(1)} %fusion.113, s32[]{:T(128)S(6)} %min.16, s32[]{:T(128)} %constant.141.clone.1..sunk.1, s32[]{:T(128)} %constant.141.clone.1..sunk.1) | dynamic-update-slice | bytes 3842052 | tf_op jit(solution)/shard_map/while/body/eval_jaxpr/dynamic_update_slice | solution.py:188
  241.6 5.9 %dynamic_update_slice.43 = f32[2048,2,128]{2,0,1:T(8,128)} dynamic-update-slice(f32[2048,2,128]{2,0,1:T(8,128)} %get-tuple-element.684, f32[1876,2,128]{2,0,1:T(8,128)S(1)} %fusion.112, s32[]{:T(128)S(6)} %min.16, s32[]{:T(128)} %constant.141.clone.1..sunk.1, s32[]{:T(128)} %constant.141.clone.1..sunk.1) | dynamic-update-slice | bytes 3842052 | tf_op jit(solution)/shard_map/while/body/eval_jaxpr/dynamic_update_slice | solution.py:182
  259.7 5.9 %dynamic_update_slice.44 = f32[2048,2,128]{2,0,1:T(8,128)} dynamic-update-slice(f32[2048,2,128]{2,0,1:T(8,128)} %get-tuple-element.685, f32[1876,2,128]{2,0,1:T(8,128)S(1)} %fusion.113, s32[]{:T(128)S(6)} %min.16, s32[]{:T(128)} %constant.141.clone.1..sunk.1, s32[]{:T(128)} %constant.141.clone.1..sunk.1) | dynamic-update-slice | bytes 3842052 | tf_op jit(solution)/shard_map/while/body/eval_jaxpr/dynamic_update_slice | solution.py:188
  271.8 5.9 %dynamic_update_slice.43 = f32[2048,2,128]{2,0,1:T(8,128)} dynamic-update-slice(f32[2048,2,128]{2,0,1:T(8,128)} %get-tuple-element.684, f32[1876,2,128]{2,0,1:T(8,128)S(1)} %fusion.112, s32[]{:T(128)S(6)} %min.16, s32[]{:T(128)} %constant.141.clone.1..sunk.1, s32[]{:T(128)} %constant.141.clone.1..sunk.1) | dynamic-update-slice | bytes 3842052 | tf_op jit(solution)/shard_map/while/body/eval_jaxpr/dynamic_update_slice | solution.py:182
  285.4 4.4 multiply_convert_fusion.2
  289.8 5.8 %dynamic_update_slice.44 = f32[2048,2,128]{2,0,1:T(8,128)} dynamic-update-slice(f32[2048,2,128]{2,0,1:T(8,128)} %get-tuple-element.685, f32[1876,2,128]{2,0,1:T(8,128)S(1)} %fusion.113, s32[]{:T(128)S(6)} %min.16, s32[]{:T(128)} %constant.141.clone.1..sunk.1, s32[]{:T(128)} %constant.141.clone.1..sunk.1) | dynamic-update-slice | bytes 3842052 | tf_op jit(solution)/shard_map/while/body/eval_jaxpr/dynamic_update_slice | solution.py:188
  301.9 5.8 %dynamic_update_slice.43 = f32[2048,2,128]{2,0,1:T(8,128)} dynamic-update-slice(f32[2048,2,128]{2,0,1:T(8,128)} %get-tuple-element.684, f32[1876,2,128]{2,0,1:T(8,128)S(1)} %fusion.112, s32[]{:T(128)S(6)} %min.16, s32[]{:T(128)} %constant.141.clone.1..sunk.1, s32[]{:T(128)} %constant.141.clone.1..sunk.1) | dynamic-update-slice | bytes 3842052 | tf_op jit(solution)/shard_map/while/body/eval_jaxpr/dynamic_update_slice | solution.py:182
  319.8 5.8 %dynamic_update_slice.44 = f32[2048,2,128]{2,0,1:T(8,128)} dynamic-update-slice(f32[2048,2,128]{2,0,1:T(8,128)} %get-tuple-element.685, f32[1876,2,128]{2,0,1:T(8,128)S(1)} %fusion.113, s32[]{:T(128)S(6)} %min.16, s32[]{:T(128)} %constant.141.clone.1..sunk.1, s32[]{:T(128)} %constant.141.clone.1..sunk.1) | dynamic-update-slice | bytes 3842052 | tf_op jit(solution)/shard_map/while/body/eval_jaxpr/dynamic_update_slice | solution.py:188
  331.9 5.8 %dynamic_update_slice.43 = f32[2048,2,128]{2,0,1:T(8,128)} dynamic-update-slice(f32[2048,2,128]{2,0,1:T(8,128)} %get-tuple-element.684, f32[1876,2,128]{2,0,1:T(8,128)S(1)} %fusion.112, s32[]{:T(128)S(6)} %min.16, s32[]{:T(128)} %constant.141.clone.1..sunk.1, s32[]{:T(128)} %constant.141.clone.1..sunk.1) | dynamic-update-slice | bytes 3842052 | tf_op jit(solution)/shard_map/while/body/eval_jaxpr/dynamic_update_slice | solution.py:182
  349.7 9.4 %all_to_all.82 = f32[8,2,256]{2,1,0:T(2,128)S(1)} all-to-all(f32[8,2,256]{2,1,0:T(2,128)S(1)} %broadcast_in_dim.137), channel_id=1, replica_groups=mesh['dp'=8,'seq'=16] {'dp'}, dimensions={0} | all-to-all | bytes 32768 | tf_op jit(solution)/shard_map/all_to_all | solution.py:35
  359.8 7.3 %all-to-all-start.9 = ((f32[16,2,256]{2,1,0:T(2,128)}), f32[16,2,256]{2,1,0:T(2,128)S(1)}, u32[]{:S(2)}, u32[]{:S(2)}) async-start(f32[16,2,256]{2,1,0:T(2,128)} %broadcast_in_dim.138), calls=%async_computation.9 | async-start | bytes 65536 | tf_op jit(solution)/shard_map/all_to_all | solution.py:35
  368.6 6.1 %all-to-all-done.9 = f32[16,2,256]{2,1,0:T(2,128)S(1)} async-done(((f32[16,2,256]{2,1,0:T(2,128)}), f32[16,2,256]{2,1,0:T(2,128)S(1)}, u32[]{:S(2)}, u32[]{:S(2)}) %all-to-all-start.9) | async-done | bytes 32800 | tf_op jit(solution)/shard_map/all_to_all | solution.py:35
  380.2 7.4 %all-to-all-done.6 = f32[16,1,4096]{2,1,0:T(1,128)S(1)} async-done(((f32[16,1,4096]{2,1,0:T(1,128)}), f32[16,1,4096]{2,1,0:T(1,128)S(1)}, u32[]{:S(2)}, u32[]{:S(2)}) %all-to-all-start.6) | async-done | bytes 262176 | tf_op jit(solution)/shard_map/all_to_all | solution.py:35
  405.5 7.4 %all-to-all-start.4 = ((bf16[16,1,64,256]{3,2,1,0:T(8,128)(2,1)}), bf16[16,1,64,256]{3,2,1,0:T(8,128)(2,1)}, u32[]{:S(2)}, u32[]{:S(2)}) async-start(bf16[16,1,64,256]{3,2,1,0:T(8,128)(2,1)} %get-tuple-element.486), calls=%async_computation.4 | async-start | bytes 1048576 | tf_op jit(solution)/shard_map/all_to_all | solution.py:75
  412.9 4.7 fusion.47
  418.0 4.8 copy.222
  423.0 7.2 %all-to-all-start.7 = ((bf16[3,2048,256]{2,0,1:T(4,128)(2,1)}), bf16[3,2048,256]{2,0,1:T(4,128)(2,1)}, u32[]{:S(2)}, u32[]{:S(2)}) async-start(bf16[3,2048,256]{2,0,1:T(4,128)(2,1)} %copy.222), calls=%async_computation.7 | async-start | bytes 8388608 | tf_op jit(solution)/shard_map/all_to_all | solution.py:20
  434.7 45.4 %all-to-all-done.7 = bf16[3,2048,256]{2,0,1:T(4,128)(2,1)} async-done(((bf16[3,2048,256]{2,0,1:T(4,128)(2,1)}), bf16[3,2048,256]{2,0,1:T(4,128)(2,1)}, u32[]{:S(2)}, u32[]{:S(2)}) %all-to-all-start.7) | async-done | bytes 3145760 | tf_op jit(solution)/shard_map/all_to_all | solution.py:20
  (274 shorter events, 200.9 us)
Async XLA Ops:
  1.9 37.2 %all-to-all-start.2 = ((s32[16,1,3,128]{3,1,2,0:T(1,128)}), s32[16,1,3,128]{3,1,2,0:T(1,128)S(1)}, u32[]{:S(2)}, u32[]{:S(2)}) async-start(s32[16,1,3,128]{3,1,2,0:T(1,128)} %broadcast_in_dim.134), calls=%async_computation.2 | async-start | bytes 49152 | tf_op jit(solution)/shard_map/all_to_all | solution.py:35
  39.1 32.7 %all-to-all-start.5 = ((bf16[16,2,16384]{2,1,0:T(2,128)(2,1)}), bf16[16,2,16384]{2,1,0:T(2,128)(2,1)S(1)}, u32[]{:S(2)}, u32[]{:S(2)}) async-start(bf16[16,2,16384]{2,1,0:T(2,128)(2,1)} %reshape.513), calls=%async_computation.5 | async-start | bytes 2097152 | tf_op jit(solution)/shard_map/all_to_all | solution.py:243
  71.9 8.0 %copy-start.32 = (s32[1,6]{1,0:T(1,128)S(1)}, s32[1,6]{1,0:T(1,128)}, u32[]{:S(2)}) copy-start(s32[1,6]{1,0:T(1,128)} %param.18) | copy-start | bytes 76
  71.9 62.6 %all-to-all-start = ((bf16[3,128,4096]{1,0,2:T(4,128)(2,1)}), bf16[3,128,4096]{1,0,2:T(4,128)(2,1)}, u32[]{:S(2)}, u32[]{:S(2)}) async-start(bf16[3,128,4096]{1,0,2:T(4,128)(2,1)} %pad_maximum_fusion), calls=%async_computation | async-start | bytes 8388608 | tf_op jit(solution)/shard_map/all_to_all | solution.py:20
  80.9 83.7 %copy-start.28 = (f32[2,128]{1,0:T(2,128)}, f32[2,128]{1,0:T(2,128)S(1)}, u32[]{:S(2)}) copy-start(f32[2,128]{1,0:T(2,128)S(1)} %dynamic-slice_bitcast_fusion.2) | copy-start | bytes 3076
  81.6 83.0 %copy-start.30 = (f32[2,128]{1,0:T(2,128)}, f32[2,128]{1,0:T(2,128)S(1)}, u32[]{:S(2)}) copy-start(f32[2,128]{1,0:T(2,128)S(1)} %dynamic-slice_bitcast_fusion.3) | copy-start | bytes 3076
  138.4 23.6 %all-to-all-start.1 = ((f32[16,1,4096]{2,1,0:T(1,128)}), f32[16,1,4096]{2,1,0:T(1,128)S(1)}, u32[]{:S(2)}, u32[]{:S(2)}) async-start(f32[16,1,4096]{2,1,0:T(1,128)} %broadcast_in_dim.131), calls=%async_computation.1 | async-start | bytes 524288 | tf_op jit(solution)/shard_map/all_to_all | solution.py:35
  146.6 3.5 copy-start.7
  154.4 10.2 %copy-start.2 = (f32[2048,2,128]{0,2,1:T(8,128)}, f32[2048,2,128]{0,2,1:T(8,128)S(1)}, u32[]{:S(2)}) copy-start(f32[2048,2,128]{0,2,1:T(8,128)S(1)} %reshape.509) | copy-start | bytes 6291460
  162.2 2.4 copy-start.24
  162.2 2.4 copy-start.26
  168.3 3.0 copy-start.16
  235.4 3.2 copy-start
  265.6 3.2 copy-start
  280.9 2.3 copy-start.12
  295.7 3.2 copy-start
  325.7 3.2 copy-start
  338.4 2.4 copy-start.1
  343.8 2.7 copy-start.5
  343.8 2.7 copy-start.29
  343.8 2.7 copy-start.31
  346.6 20.6 %copy-start.18 = (bf16[4,512,2,128]{1,3,2,0:T(8,128)(2,1)S(1)}, bf16[4,512,2,128]{1,3,2,0:T(8,128)(2,1)}, u32[]{:S(2)}) copy-start(bf16[4,512,2,128]{1,3,2,0:T(8,128)(2,1)} %copy-done.17) | copy-start | bytes 3145732
  359.8 14.9 %all-to-all-start.9 = ((f32[16,2,256]{2,1,0:T(2,128)}), f32[16,2,256]{2,1,0:T(2,128)S(1)}, u32[]{:S(2)}, u32[]{:S(2)}) async-start(f32[16,2,256]{2,1,0:T(2,128)} %broadcast_in_dim.138), calls=%async_computation.9 | async-start | bytes 65536 | tf_op jit(solution)/shard_map/all_to_all | solution.py:35
  375.6 12.0 %all-to-all-start.6 = ((f32[16,1,4096]{2,1,0:T(1,128)}), f32[16,1,4096]{2,1,0:T(1,128)S(1)}, u32[]{:S(2)}, u32[]{:S(2)}) async-start(f32[16,1,4096]{2,1,0:T(1,128)} %broadcast_in_dim.136), calls=%async_computation.6 | async-start | bytes 524288 | tf_op jit(solution)/shard_map/all_to_all | solution.py:35
  387.6 17.9 %all-to-all-start.3 = ((bf16[16,1,64,256]{3,2,1,0:T(8,128)(2,1)}), bf16[16,1,64,256]{3,2,1,0:T(8,128)(2,1)S(1)}, u32[]{:S(2)}, u32[]{:S(2)}) async-start(bf16[16,1,64,256]{3,2,1,0:T(8,128)(2,1)} %get-tuple-element.485), calls=%async_computation.3 | async-start | bytes 1048576 | tf_op jit(solution)/shard_map/all_to_all | solution.py:75
  393.1 3.1 copy-start.6
  400.9 3.1 copy-start.13
  405.5 12.1 %copy-start.20 = (bf16[16,1,64,256]{3,2,1,0:T(8,128)(2,1)}, bf16[16,1,64,256]{3,2,1,0:T(8,128)(2,1)S(1)}, u32[]{:S(2)}) copy-start(bf16[16,1,64,256]{3,2,1,0:T(8,128)(2,1)S(1)} %all-to-all-done.3) | copy-start | bytes 1572868
  405.5 17.5 %all-to-all-start.4 = ((bf16[16,1,64,256]{3,2,1,0:T(8,128)(2,1)}), bf16[16,1,64,256]{3,2,1,0:T(8,128)(2,1)}, u32[]{:S(2)}, u32[]{:S(2)}) async-start(bf16[16,1,64,256]{3,2,1,0:T(8,128)(2,1)} %get-tuple-element.486), calls=%async_computation.4 | async-start | bytes 1048576 | tf_op jit(solution)/shard_map/all_to_all | solution.py:75
  412.9 4.8 copy-start.19
  422.8 9.5 %copy-start.21 = (bf16[16,1,64,256]{3,2,1,0:T(8,128)(2,1)S(1)}, bf16[16,1,64,256]{3,2,1,0:T(8,128)(2,1)}, u32[]{:S(2)}) copy-start(bf16[16,1,64,256]{3,2,1,0:T(8,128)(2,1)} %copy-done.20) | copy-start | bytes 1572868
  423.0 57.1 %all-to-all-start.7 = ((bf16[3,2048,256]{2,0,1:T(4,128)(2,1)}), bf16[3,2048,256]{2,0,1:T(4,128)(2,1)}, u32[]{:S(2)}, u32[]{:S(2)}) async-start(bf16[3,2048,256]{2,0,1:T(4,128)(2,1)} %copy.222), calls=%async_computation.7 | async-start | bytes 8388608 | tf_op jit(solution)/shard_map/all_to_all | solution.py:20
  (25 other events, 47.2 us)
where the time goes:
time: 501 us; the launch traced here: 491 us
  local copies, waits for them, and re-layouts  158 us (32%)
  waiting for transfers between devices  104 us (21%)
  matrix products  85.7 us (17%)
  other arithmetic  67.7 us (14%)
  starting transfers between devices  57.7 us (12%)
  blocking collectives  9.44 us (2%)
  loops' own time  6.48 us (1%)
    all_to_all x2, waiting for transfers between devices, in_one_piece(): lax.all_to_all(both, axis, split_axis=split_dim, concat_axis=concat_dim,...  90.4 us
    dot_general x28, matrix products, product(): return jnp.einsum(form, left, right, preferred_element_type=jnp.float32)  83.3 us
    unnamed x69, local copies, waits for them, and re-layouts  36.2 us
    all_to_all x4, starting transfers between devices, sent_to_all(): lax.all_to_all(jnp.broadcast_to(value[None], (count, *value.shape)), axis...  24 us
    dynamic_update_slice x4, local copies, waits for them, and re-layouts, one_block(): lax.dynamic_update_slice_in_dim(key_acc, lax.dynamic_slice_in_dim(key_acc...  23.4 us
    dynamic_update_slice x4, local copies, waits for them, and re-layouts, one_block(): lax.dynamic_update_slice_in_dim(value_acc, lax.dynamic_slice_in_dim(value...  23.4 us
    unnamed x2, other arithmetic  22.7 us
    all_to_all x2, starting transfers between devices, in_one_piece(): lax.all_to_all(both, axis, split_axis=split_dim, concat_axis=concat_dim,...  15.1 us
  transfers between devices with their start and end apart: 9, of which 5 were waited for; matrix products, arithmetic and copies ran while one was open for 23% of the time, Pallas kernels for 0%

commit v1 on v0

v1 whole, which is shorter than its diff:
```python
import functools
import math

import jax
import jax.numpy as jnp
import numpy as np
from jax import lax
from jax.experimental import pallas as pl
from jax.experimental.pallas import tpu as pltpu
from jax.sharding import PartitionSpec as P

HEAD_DIM = 128
HALF = HEAD_DIM // 2
EPSILON = 1e-06
APART = float(2**20)
QUERY_TILE = 256
KEY_STEP = 512
SLAB = 4 * HEAD_DIM
F32 = jnp.float32
BF16 = jnp.bfloat16


def frequency_row():
    sixth = HEAD_DIM // 6
    first = HALF - 2 * sixth
    pairs = np.arange(HALF)
    section = (pairs >= first).astype(int) + (pairs >= first + sixth).astype(int)
    begin = np.array([0, first, first + sixth])[section]
    count = np.array([first, sixth, sixth])[section]
    freqs = 10000.0 ** (-(pairs - begin) / count)
    return np.tile(freqs, 2)[None].astype(np.float32), (first, first + sixth)


def rotary_tables(rows, freqs):
    _, (second, third) = frequency_row()
    columns = rows.T
    tokens = columns.shape[0]
    lane = lax.broadcasted_iota(jnp.int32, (tokens, HEAD_DIM), 1)
    pair = lane & (HALF - 1)
    place = jnp.where(
        pair < second, columns[:, 0:1], jnp.where(pair < third, columns[:, 1:2], columns[:, 2:3])
    )
    angle = place * freqs
    return jnp.cos(angle), jnp.where(lane < HALF, -jnp.sin(angle), jnp.sin(angle))


def send_kernel(q_ref, k_ref, v_ref, g_ref, qg_ref, kg_ref, pos_ref, freq_ref, out_ref, cos_ref, sin_ref, qs_ref, ks_ref):
    tokens, feature = q_ref.shape
    rows = jnp.concatenate(
        [pos_ref[...].astype(F32), jnp.zeros((13, tokens), F32)], axis=0
    )
    cosine, sine = rotary_tables(rows, freq_ref[...])
    cos_ref[...] = cosine
    sin_ref[...] = sine
    members = out_ref.shape[0]
    local = feature // members // HEAD_DIM
    scales = []
    for ref, scale_ref in ((q_ref, qs_ref), (k_ref, ks_ref)):
        total = jnp.zeros((tokens, HEAD_DIM), F32)
        for h in range(feature // HEAD_DIM):
            part = ref[:, h * HEAD_DIM : (h + 1) * HEAD_DIM].astype(F32)
            total = total + part * part
        scale = lax.rsqrt(jnp.sum(total, axis=-1, keepdims=True) / feature + EPSILON)
        scale = jnp.broadcast_to(scale, (tokens, HEAD_DIM))
        scale_ref[...] = scale
        scales.append(scale)
    packed_rows = rows.astype(BF16)

    def one(j, carry):
        for h in range(local):
            at = pl.ds(pl.multiple_of((j * local + h) * HEAD_DIM, HEAD_DIM), HEAD_DIM)
            for a, (ref, gain_ref, scale_ref) in enumerate(((q_ref, qg_ref, qs_ref), (k_ref, kg_ref, ks_ref))):
                x = ref[:, at].astype(F32) * scale_ref[...] * gain_ref[:, at]
                turned = x * cos_ref[...] + pltpu.roll(x, HALF, 1) * sin_ref[...]
                out_ref[j, h * SLAB + a * tokens : h * SLAB + (a + 1) * tokens, :] = turned.astype(BF16)
            out_ref[j, h * SLAB + 2 * tokens : h * SLAB + 3 * tokens, :] = v_ref[:, at]
            out_ref[j, h * SLAB + 3 * tokens : h * SLAB + 4 * tokens, :] = g_ref[:, at]
        out_ref[j, local * SLAB : local * SLAB + 16, :] = packed_rows
        return carry

    lax.fori_loop(0, members, one, 0)


def dot(left, right, contract):
    return lax.dot_general(left, right, ((contract[0], contract[1]), ((), ())), preferred_element_type=F32)


def attention_kernel(len_ref, x_ref, freq_ref, out_ref, part_ref, kt, vt, keymask, querymask, s_ref, dk, dv):
    members = x_ref.shape[0]
    tok = HEAD_DIM
    tokens = members * tok
    local = (x_ref.shape[1] - 16) // SLAB
    clips = len_ref.shape[0]
    scale = HEAD_DIM ** (-0.5)
    factor = scale * math.log2(math.e)

    ends = []
    so_far = 0
    for c in range(clips):
        so_far = so_far + len_ref[c]
        ends.append(so_far)

    def masks(i, carry):
        token = lax.broadcasted_iota(jnp.int32, (tok, HEAD_DIM), 0) + i * tok
        lane = lax.broadcasted_iota(jnp.int32, (tok, HEAD_DIM), 1)
        clip = jnp.zeros((tok, HEAD_DIM), jnp.int32)
        for c in range(clips):
            clip = clip + (token >= ends[c]).astype(jnp.int32)
        own = clip == lane
        at = pl.ds(pl.multiple_of(i * tok, tok), tok)
        keymask[at, :] = jnp.where(own, -APART, 0.0).astype(BF16)
        querymask[at, :] = jnp.where(own, 0.0, 1.0).astype(BF16)
        for h in range(local):
            kt[h, :, at] = x_ref[i, h * SLAB + tok : h * SLAB + 2 * tok, :].T
            vt[h, :, at] = x_ref[i, h * SLAB + 2 * tok : h * SLAB + 3 * tok, :].T
            dk[h, at, :] = jnp.zeros((tok, HEAD_DIM), F32)
            dv[h, at, :] = jnp.zeros((tok, HEAD_DIM), F32)
        return carry

    lax.fori_loop(0, members, masks, 0)

    per = QUERY_TILE // tok
    step = KEY_STEP // tok

    def tile(i, carry):
        q0 = i * QUERY_TILE
        first, last = jnp.int32(0), jnp.int32(tokens)
        for c in range(clips):
            first = jnp.where(ends[c] <= q0, ends[c], first)
        for c in reversed(range(clips)):
            last = jnp.where(ends[c] >= q0 + QUERY_TILE, ends[c], last)
        low = first // tok
        count = (last - low * tok + KEY_STEP - 1) // KEY_STEP
        low = jnp.minimum(low, members - count * step)

        def block(h, a, start, number):
            return x_ref[pl.ds(start, number), h * SLAB + a * tok : h * SLAB + (a + 1) * tok, :].reshape(
                number * tok, HEAD_DIM
            )

        q_at = pl.ds(pl.multiple_of(q0, QUERY_TILE), QUERY_TILE)
        query_mask = querymask[q_at, :]
        queries = [block(h, 0, i * per, per) for h in range(local)]
        cots = [block(h, 3, i * per, per) for h in range(local)]
        wide = [jnp.concatenate([queries[h], query_mask], axis=1) for h in range(local)]

        def scores(j, highest):
            k0 = low + j * step
            k_at = pl.ds(pl.multiple_of(k0 * tok, tok), KEY_STEP)
            s_at = pl.ds(pl.multiple_of(j * KEY_STEP, KEY_STEP), KEY_STEP)
            key_mask = keymask[k_at, :]
            new = []
            for h in range(local):
                keys = jnp.concatenate([block(h, 1, k0, step), key_mask], axis=1)
                s = dot(keys, wide[h], ((1,), (1,)))
                s_ref[h, s_at, :] = s
                new.append(jnp.maximum(highest[h], jnp.max(s.reshape(KEY_STEP // 8, 8, QUERY_TILE), axis=0)))
            return tuple(new)

        lowest = jnp.full((8, QUERY_TILE), -4.0 * APART, F32)
        highest = lax.fori_loop(0, count, scores, (lowest,) * local)
        highest = [jnp.max(m, axis=0, keepdims=True) for m in highest]

        def forward(j, sums):
            k0 = low + j * step
            k_at = pl.ds(pl.multiple_of(k0 * tok, tok), KEY_STEP)
            s_at = pl.ds(pl.multiple_of(j * KEY_STEP, KEY_STEP), KEY_STEP)
            totals, outs = [], []
            for h in range(local):
                e = jnp.exp2((s_ref[h, s_at, :] - highest[h]) * factor)
                s_ref[h, s_at, :] = e
                totals.append(sums[0][h] + jnp.sum(e.reshape(KEY_STEP // 8, 8, QUERY_TILE), axis=0))
                outs.append(sums[1][h] + dot(vt[h, :, k_at], e.astype(BF16), ((1,), (0,))))
            return tuple(totals), tuple(outs)

        zero8 = jnp.zeros((8, QUERY_TILE), F32)
        zero_t = jnp.zeros((HEAD_DIM, QUERY_TILE), F32)
        totals, outs = lax.fori_loop(0, count, forward, ((zero8,) * local, (zero_t,) * local))
        inverse, deltas, cot_t = [], [], []
        for h in range(local):
            inv = 1.0 / jnp.sum(totals[h], axis=0, keepdims=True)
            attended = (outs[h] * inv).astype(BF16)
            turned = cots[h].T
            deltas.append(jnp.sum(attended.astype(F32) * turned.astype(F32), axis=0, keepdims=True))
            inverse.append(inv)
            cot_t.append(turned)
            out_ref[pl.ds(i * per, per), h * SLAB : h * SLAB + tok, :] = attended.T.reshape(per, tok, HEAD_DIM)

        def backward(j, sums):
            k0 = low + j * step
            k_at = pl.ds(pl.multiple_of(k0 * tok, tok), KEY_STEP)
            s_at = pl.ds(pl.multiple_of(j * KEY_STEP, KEY_STEP), KEY_STEP)
            new = []
            for h in range(local):
                prob = s_ref[h, s_at, :] * inverse[h]
                dprob = dot(block(h, 2, k0, step), cot_t[h], ((1,), (0,)))
                dscore = (prob * (dprob - deltas[h])).astype(BF16)
                dv[h, k_at, :] += dot(prob.astype(BF16), cots[h], ((1,), (0,)))
                dk[h, k_at, :] += dot(dscore, queries[h], ((1,), (0,)))
                new.append(sums[h] + dot(kt[h, :, k_at], dscore, ((1,), (0,))))
            return tuple(new)

        dq = lax.fori_loop(0, count, backward, (zero_t,) * local)
        for h in range(local):
            dq_tile = (dq[h] * scale).astype(BF16)
            out_ref[pl.ds(i * per, per), h * SLAB + tok : h * SLAB + 2 * tok, :] = dq_tile.T.reshape(
                per, tok, HEAD_DIM
            )
        return carry

    lax.fori_loop(0, tokens // QUERY_TILE, tile, 0)

    def finish(i, sums):
        at = pl.ds(pl.multiple_of(i * tok, tok), tok)
        cosine, sine = rotary_tables(x_ref[i, local * SLAB : local * SLAB + 16, :].astype(F32), freq_ref[...])
        new = []
        for h in range(local):
            dk_tile = (dk[h, at, :] * scale).astype(BF16)
            out_ref[i, h * SLAB + 2 * tok : h * SLAB + 3 * tok, :] = dk_tile
            out_ref[i, h * SLAB + 3 * tok : h * SLAB + 4 * tok, :] = dv[h, at, :].astype(BF16)
            dq_tile = out_ref[i, h * SLAB + tok : h * SLAB + 2 * tok, :]
            for a, grad in ((0, dq_tile), (1, dk_tile)):
                g = grad.astype(F32)
                p = x_ref[i, h * SLAB + a * tok : h * SLAB + (a + 1) * tok, :].astype(F32)
                g = g * cosine - pltpu.roll(g, HALF, 1) * sine
                p = p * cosine - pltpu.roll(p, HALF, 1) * sine
                new.append(sums[2 * h + a] + jnp.sum((g * p).reshape(tok // 8, 8, HEAD_DIM), axis=0))
        return tuple(new)

    sums = lax.fori_loop(0, members, finish, (jnp.zeros((8, HEAD_DIM), F32),) * (2 * local))
    part_ref[...] = jnp.concatenate(
        [jnp.sum(s, axis=0, keepdims=True) for s in sums] + [jnp.zeros((8 - 2 * local, HEAD_DIM), F32)], axis=0
    )


def receive_kernel(y_ref, q_ref, k_ref, qg_ref, kg_ref, cos_ref, sin_ref, qs_ref, ks_ref, att_ref, gq_ref, gk_ref, gv_ref, lift_q, lift_k):
    tokens, feature = q_ref.shape
    members = y_ref.shape[0]
    local = feature // members // HEAD_DIM
    groups = ((q_ref, qg_ref, qs_ref, gq_ref, lift_q), (k_ref, kg_ref, ks_ref, gk_ref, lift_k))

    def first(j, sums):
        sums = list(sums)
        for h in range(local):
            at = pl.ds(pl.multiple_of((j * local + h) * HEAD_DIM, HEAD_DIM), HEAD_DIM)
            att_ref[:, at] = y_ref[j, h * SLAB : h * SLAB + tokens, :]
            gv_ref[:, at] = y_ref[j, h * SLAB + 3 * tokens : h * SLAB + 4 * tokens, :]
            for a, (raw_ref, gain_ref, scale_ref, _, lift_ref) in enumerate(groups):
                g = y_ref[j, h * SLAB + (a + 1) * tokens : h * SLAB + (a + 2) * tokens, :].astype(F32)
                g = g * cos_ref[...] - pltpu.roll(g, HALF, 1) * sin_ref[...]
                lift = g * gain_ref[:, at]
                lift_ref[:, at] = lift
                sums[a] = sums[a] + lift * (raw_ref[:, at].astype(F32) * scale_ref[...])
        return tuple(sums)

    zero = jnp.zeros((tokens, HEAD_DIM), F32)
    sums = lax.fori_loop(0, members, first, (zero, zero))
    inner = [jnp.sum(s, axis=-1, keepdims=True) / feature for s in sums]

    def second(j, carry):
        for h in range(local):
            at = pl.ds(pl.multiple_of((j * local + h) * HEAD_DIM, HEAD_DIM), HEAD_DIM)
            for a, (raw_ref, _, scale_ref, grad_ref, lift_ref) in enumerate(groups):
                hat = raw_ref[:, at].astype(F32) * scale_ref[...]
                grad_ref[:, at] = (scale_ref[...] * (lift_ref[:, at] - hat * inner[a])).astype(BF16)
        return carry

    lax.fori_loop(0, members, second, 0)


def on_device(q_raw, k_raw, values, grad_out, q_gain, k_gain, lengths, positions):
    members = lax.axis_size("seq")
    replicas = lax.axis_size("dp")
    _, tok, feature = q_raw.shape
    local = feature // members // HEAD_DIM
    tokens = tok * members
    vmem = pl.BlockSpec(memory_space=pltpu.VMEM)
    smem = pl.BlockSpec(memory_space=pltpu.SMEM)
    freqs = jnp.asarray(frequency_row()[0])
    shape = jax.ShapeDtypeStruct
    wide = shape((tok, HEAD_DIM), F32)

    packet, cosine, sine, q_scale, k_scale = pl.pallas_call(
        send_kernel,
        out_shape=(shape((members, local * SLAB + 16, HEAD_DIM), BF16), wide, wide, wide, wide),
        in_specs=[vmem] * 8,
        out_specs=(vmem,) * 5,
        compiler_params=pltpu.CompilerParams(vmem_limit_bytes=48 << 20),
        cost_estimate=pl.CostEstimate(flops=40 << 20, bytes_accessed=9 << 20, transcendentals=0),
        name="send",
    )(q_raw[0], k_raw[0], values[0], grad_out[0], q_gain[None], k_gain[None], positions[0], freqs)

    got = lax.all_to_all(packet, "seq", 0, 0, tiled=True)

    back, part = pl.pallas_call(
        attention_kernel,
        out_shape=(shape((members, local * SLAB, HEAD_DIM), BF16), shape((8, HEAD_DIM), F32)),
        in_specs=[smem, vmem, vmem],
        out_specs=(vmem,) * 2,
        scratch_shapes=[
            pltpu.VMEM((local, HEAD_DIM, tokens), BF16),
            pltpu.VMEM((local, HEAD_DIM, tokens), BF16),
            pltpu.VMEM((tokens, HEAD_DIM), BF16),
            pltpu.VMEM((tokens, HEAD_DIM), BF16),
            pltpu.VMEM((local, tokens, QUERY_TILE), F32),
            pltpu.VMEM((local, tokens, HEAD_DIM), F32),
            pltpu.VMEM((local, tokens, HEAD_DIM), F32),
        ],
        compiler_params=pltpu.CompilerParams(vmem_limit_bytes=48 << 20),
        cost_estimate=pl.CostEstimate(flops=12 << 30, bytes_accessed=9 << 20, transcendentals=1 << 22),
        name="attention",
    )(lengths[0], got, freqs)

    returned = lax.all_to_all(back, "seq", 0, 0, tiled=True)

    for distance in (1, 2, 4):
        part = part + lax.ppermute(part, "dp", [(i, i ^ distance) for i in range(replicas)])
    mine = lax.broadcasted_iota(jnp.int32, (members, 1, 1), 0) == lax.axis_index("seq")
    every = jnp.where(mine, part[None], 0.0)
    for distance in (1, 2, 4, 8):
        every = every + lax.ppermute(every, "seq", [(i, i ^ distance) for i in range(members)])
    gains = every[:, : 2 * local].reshape(members, local, 2, HEAD_DIM)
    gain_out = [gains[:, :, a].reshape(feature) / (gain * replicas) for a, gain in enumerate((q_gain, k_gain))]

    outs = pl.pallas_call(
        receive_kernel,
        out_shape=(shape((tok, feature), BF16),) * 4,
        in_specs=[vmem] * 9,
        out_specs=(vmem,) * 4,
        scratch_shapes=[pltpu.VMEM((tok, feature), F32)] * 2,
        compiler_params=pltpu.CompilerParams(vmem_limit_bytes=48 << 20),
        cost_estimate=pl.CostEstimate(flops=40 << 20, bytes_accessed=10 << 20, transcendentals=0),
        name="receive",
    )(returned, q_raw[0], k_raw[0], q_gain[None], k_gain[None], cosine, sine, q_scale, k_scale)
    return tuple(o[None] for o in outs) + tuple(gain_out)


def solution(mesh):
    tokens_split = P("dp", "seq", None)
    return jax.shard_map(
        on_device,
        mesh=mesh,
        in_specs=(tokens_split,) * 4 + (P(), P(), P("dp", None), P("dp", None, "seq")),
        out_specs=(tokens_split,) * 4 + (P(), P()),
        check_vma=False,
    )
```

time: 501 us -> 199 us (0.40); the launches traced: 491 us -> 198 us
  local copies, waits for them, and re-layouts: 158 us -> 9.73 us
  matrix products: 85.7 us -> 0 us
  other arithmetic: 67.7 us -> 0.91 us
  blocking collectives: 9.44 us -> 60.5 us
  Pallas kernels: 0 us -> 49.9 us
  waiting for transfers between devices: 104 us -> 59.8 us
  starting transfers between devices: 57.7 us -> 16.3 us
  loops' own time: 6.48 us -> 0 us
    all_to_all x9 -> x1, waiting for transfers between devices: 104 us -> 0.01 us  [on_device(): returned = lax.all_to_all(back, 'seq', 0, 0, tiled=True)]
    dot_general x29 -> x0, matrix products: 85.7 us -> none  [the longest x28 83.3 us: product(): return jnp.einsum(form, left, right, preferred_element_type=jnp.float32)]
    ppermute x0 -> x7, waiting for transfers between devices: none -> 59.8 us  [the longest x4 52.5 us: on_device(): lax.ppermute(every, 'seq', [(i, i ^ distance) for i in range(members)])]
    all_to_all x9 -> x1, starting transfers between devices: 57.7 us -> 4.69 us  [on_device(): returned = lax.all_to_all(back, 'seq', 0, 0, tiled=True)]
    all_to_all x1, blocking collectives: 9.44 us -> 60.5 us  [on_device(): got = lax.all_to_all(packet, 'seq', 0, 0, tiled=True)]
    dynamic_update_slice x16 -> x0, local copies, waits for them, and re-layouts: 50.4 us -> none  [the longest x4 23.4 us: one_block(): lax.dynamic_update_slice_in_dim(key_acc, lax.dynamic_slice_in_dim(key_acc...]
    pallas_call x0 -> x3, Pallas kernels: none -> 49.9 us  [the longest x1 35.8 us: on_device(): pl.pallas_call(attention_kernel, out_shape=(shape((members, local * SLAB,...]
    unnamed x69 -> x27, local copies, waits for them, and re-layouts: 36.2 us -> 9.7 us
  transfers between devices with their start and end apart: 9 -> 8, of which waited for: 5 -> 7; matrix products, arithmetic and copies ran while one was open for 23% -> 0% of each run, Pallas kernels for 0% -> 0%
where the time goes in v1:
time: 199 us; the launch traced here: 198 us
  blocking collectives  60.5 us (30%)
  waiting for transfers between devices  59.8 us (30%)
  Pallas kernels  49.9 us (25%)
  starting transfers between devices  16.3 us (8%)
  local copies, waits for them, and re-layouts  9.73 us (5%)
    all_to_all x1, blocking collectives, on_device(): got = lax.all_to_all(packet, 'seq', 0, 0, tiled=True)  60.5 us
    ppermute x4, waiting for transfers between devices, on_device(): lax.ppermute(every, 'seq', [(i, i ^ distance) for i in range(members)])  52.5 us
    pallas_call x1, Pallas kernels, on_device(): pl.pallas_call(attention_kernel, out_shape=(shape((members, local * SLAB,...  35.8 us
    unnamed x27, local copies, waits for them, and re-layouts  9.7 us
    pallas_call x1, Pallas kernels, on_device(): pl.pallas_call(receive_kernel, out_shape=(shape((tok, feature), BF16),) *...  8.57 us
    ppermute x4, starting transfers between devices, on_device(): lax.ppermute(every, 'seq', [(i, i ^ distance) for i in range(members)])  8.24 us
    ppermute x3, waiting for transfers between devices, on_device(): lax.ppermute(part, 'dp', [(i, i ^ distance) for i in range(replicas)])  7.34 us
    pallas_call x1, Pallas kernels, on_device(): pl.pallas_call(send_kernel, out_shape=(shape((members, local * SLAB + 16,...  5.6 us
  transfers between devices with their start and end apart: 8, of which 7 were waited for; matrix products, arithmetic and copies ran while one was open for 0% of the time, Pallas kernels for 0%

profile of v1, /device:TPU:0, one launch (start us, length us, event | category | flops | bytes accessed | tf_op | source)
XLA Modules:
  0.0 197.9 jit_solution(14401336950925004679)
XLA Ops:
  0.6 0.7 copy.17
  1.3 1.2 copy-done.1
  2.5 1.2 copy-done.3
  3.8 1.2 copy-done.5
  5.0 1.2 copy-done.6
  6.2 0.7 copy-done.7
  6.9 0.7 copy-done.9
  7.7 0.7 copy-done.11
  8.3 5.6 %send.1 = (bf16[16,1040,128]{2,1,0:T(8,128)(2,1)}, f32[128,128]{1,0:T(8,128)S(1)}, f32[128,128]{1,0:T(8,128)S(1)}, f32[128,128]{1,0:T(8,128)S(1)}, f32[128,128]{1,0:T(8,128)S(1)}) custom-call(bf16[128,4096]{1,0:T(8,128)(2,1)S(1)} %bitcast.17, bf16[128,4096]{1,0:T(8,128)(2,1)S(1)} %bitcast.19, bf16[128,4096]{1,0:T(8,128)(2,1)S(1)} %bitcast.21, ...), custom_call_target="tpu_custom_call" | custom-call | flops 41943040 | bytes 9437184 | tf_op jit(solution)/shard_map/send/pallas_call | solution.py:283
  13.9 60.5 %all_to_all.10.x_ref = bf16[16,1040,128]{2,1,0:T(8,128)(2,1)} all-to-all(bf16[16,1040,128]{2,1,0:T(8,128)(2,1)} %get-tuple-element.17), channel_id=1, replica_groups=mesh['dp'=8,'seq'=16] {'seq'}, dimensions={0} | all-to-all | bytes 8519680 | tf_op jit(solution)/shard_map/all_to_all | solution.py:293
  74.4 35.8 %attention.1 = (bf16[16,1024,128]{2,1,0:T(8,128)(2,1)S(1)}, f32[8,128]{1,0:T(8,128)S(1)}) custom-call(s32[6]{0:T(128)S(1)} %bitcast.28, bf16[16,1040,128]{2,1,0:T(8,128)(2,1)} %all_to_all.10.x_ref, f32[1,128]{1,0:T(1,128)S(1)} %copy-done.11), custom_call_target="tpu_custom_call" | custom-call | flops 12884901888 | bytes 9437184 | tf_op jit(solution)/shard_map/attention/pallas_call | solution.py:295
  110.2 2.0 %copy-done = bf16[16,1024,128]{2,1,0:T(8,128)(2,1)} copy-done((bf16[16,1024,128]{2,1,0:T(8,128)(2,1)}, bf16[16,1024,128]{2,1,0:T(8,128)(2,1)S(1)}, u32[]{:S(2)}) %copy-start) | copy-done | bytes 4194328
  112.2 4.7 %all-to-all-start.1 = ((bf16[16,1024,128]{2,1,0:T(8,128)(2,1)}), bf16[16,1024,128]{2,1,0:T(8,128)(2,1)}, u32[]{:S(2)}, u32[]{:S(2)}) async-start(bf16[16,1024,128]{2,1,0:T(8,128)(2,1)} %copy-done), calls=%async_computation.1 | async-start | bytes 8388608 | tf_op jit(solution)/shard_map/all_to_all | solution.py:314
  116.9 1.2 collective-permute-start
  118.1 0.8 collective-permute-done
  118.9 0.8 collective-permute-start.1
  119.7 2.8 %collective-permute-done.1 = f32[8,128]{1,0:T(8,128)S(1)} collective-permute-done((f32[8,128]{1,0:T(8,128)S(1)}, f32[8,128]{1,0:T(8,128)S(1)}, u32[]{:S(2)}, u32[]{:S(2)}) %collective-permute-start.1) | collective-permute-done | bytes 4128 | tf_op jit(solution)/shard_map/ppermute | solution.py:317
  122.6 1.4 collective-permute-start.2
  124.0 3.7 %collective-permute-done.2 = f32[8,128]{1,0:T(8,128)S(1)} collective-permute-done((f32[8,128]{1,0:T(8,128)S(1)}, f32[8,128]{1,0:T(8,128)S(1)}, u32[]{:S(2)}, u32[]{:S(2)}) %collective-permute-start.2) | collective-permute-done | bytes 4128 | tf_op jit(solution)/shard_map/ppermute | solution.py:317
  127.7 0.1 broadcast_select_fusion
  127.8 1.5 collective-permute-start.3
  129.2 35.0 %collective-permute-done.3 = f32[16,8,128]{2,1,0:T(8,128)S(1)} collective-permute-done((f32[16,8,128]{2,1,0:T(8,128)S(1)}, f32[16,8,128]{2,1,0:T(8,128)S(1)}, u32[]{:S(2)}, u32[]{:S(2)}) %collective-permute-start.3) | collective-permute-done | bytes 65568 | tf_op jit(solution)/shard_map/ppermute | solution.py:321
  164.3 0.1 fusion
  164.4 0.1 collective-permute-start.4
  164.4 12.3 %collective-permute-done.4 = f32[16,8,128]{2,1,0:T(8,128)S(1)} collective-permute-done((f32[16,8,128]{2,1,0:T(8,128)S(1)}, f32[16,8,128]{2,1,0:T(8,128)S(1)}, u32[]{:S(2)}, u32[]{:S(2)}) %collective-permute-start.4) | collective-permute-done | bytes 65568 | tf_op jit(solution)/shard_map/ppermute | solution.py:321
  176.7 0.1 fusion.2
  176.8 1.4 collective-permute-start.5
  178.3 2.9 %collective-permute-done.5 = f32[16,8,128]{2,1,0:T(8,128)S(1)} collective-permute-done((f32[16,8,128]{2,1,0:T(8,128)S(1)}, f32[16,8,128]{2,1,0:T(8,128)S(1)}, u32[]{:S(2)}, u32[]{:S(2)}) %collective-permute-start.5) | collective-permute-done | bytes 65568 | tf_op jit(solution)/shard_map/ppermute | solution.py:321
  181.2 5.2 %collective-permute-start.6 = (f32[16,8,128]{2,1,0:T(8,128)S(1)}, f32[16,8,128]{2,1,0:T(8,128)S(1)}, u32[]{:S(2)}, u32[]{:S(2)}) collective-permute-start(f32[16,8,128]{2,1,0:T(8,128)S(1)} %add.26), channel_id=1, source_target_pairs={{0,8},{1,9},{2,10},{3,11},{4,12},{5,13},{6,14},{7,15},{8,0},{9,1},... | collective-permute-start | bytes 196616 | tf_op jit(solution)/shard_map/ppermute | solution.py:321
  186.4 2.2 %collective-permute-done.6 = f32[16,8,128]{2,1,0:T(8,128)S(1)} collective-permute-done((f32[16,8,128]{2,1,0:T(8,128)S(1)}, f32[16,8,128]{2,1,0:T(8,128)S(1)}, u32[]{:S(2)}, u32[]{:S(2)}) %collective-permute-start.6) | collective-permute-done | bytes 65568 | tf_op jit(solution)/shard_map/ppermute | solution.py:321
  188.7 0.6 multiply_divide_fusion
  189.4 8.6 %receive.1 = (bf16[128,4096]{1,0:T(8,128)(2,1)}, bf16[128,4096]{1,0:T(8,128)(2,1)}, bf16[128,4096]{1,0:T(8,128)(2,1)}, bf16[128,4096]{1,0:T(8,128)(2,1)}) custom-call(bf16[16,1024,128]{2,1,0:T(8,128)(2,1)} %all-to-all-done.1.y_ref, bf16[128,4096]{1,0:T(8,128)(2,1)S(1)} %bitcast.18, bf16[128,4096]{1,0:T(8,128)(2,1)S(1)} %bitcast.20, f32[1,4096]{1,0:T(1,128)S(1)} %bitcast.24, ...), custom_call_target="tpu_custom_call" | custom-call | flops 41943040 | bytes 10485760 | tf_op jit(solution)/shard_map/receive/pallas_call | solution.py:325
  (26 shorter events, 0.1 us)
Async XLA Ops:
  1.3 1.2 copy-start.1
  2.5 1.2 copy-start.3
  3.8 1.2 copy-start.5
  5.0 1.2 copy-start.6
  6.2 0.7 copy-start.7
  6.9 0.7 copy-start.9
  7.7 0.7 copy-start.11
  13.9 60.5 %copy-start.12 = (s32[1,6]{1,0:T(1,128)S(1)}, s32[1,6]{1,0:T(1,128)}, u32[]{:S(2)}) copy-start(s32[1,6]{1,0:T(1,128)} %param.15) | copy-start | bytes 76
  110.2 2.0 %copy-start = (bf16[16,1024,128]{2,1,0:T(8,128)(2,1)}, bf16[16,1024,128]{2,1,0:T(8,128)(2,1)S(1)}, u32[]{:S(2)}) copy-start(bf16[16,1024,128]{2,1,0:T(8,128)(2,1)S(1)} %get-tuple-element.18) | copy-start | bytes 12582916
  112.2 76.5 %copy-start.8 = (f32[4096]{0:T(1024)S(1)}, f32[4096]{0:T(1024)}, u32[]{:S(2)}) copy-start(f32[4096]{0:T(1024)} %param.13) | copy-start | bytes 49156
  112.2 76.5 %copy-start.10 = (f32[4096]{0:T(1024)S(1)}, f32[4096]{0:T(1024)}, u32[]{:S(2)}) copy-start(f32[4096]{0:T(1024)} %param.14) | copy-start | bytes 49156
  112.2 77.1 %copy-start.2 = (bf16[1,128,4096]{2,1,0:T(8,128)(2,1)S(1)}, bf16[1,128,4096]{2,1,0:T(8,128)(2,1)}, u32[]{:S(2)}) copy-start(bf16[1,128,4096]{2,1,0:T(8,128)(2,1)} %param.9) | copy-start | bytes 3145732
  112.2 77.1 %copy-start.4 = (bf16[1,128,4096]{2,1,0:T(8,128)(2,1)S(1)}, bf16[1,128,4096]{2,1,0:T(8,128)(2,1)}, u32[]{:S(2)}) copy-start(bf16[1,128,4096]{2,1,0:T(8,128)(2,1)} %param.10) | copy-start | bytes 3145732
  112.2 77.1 %all-to-all-start.1 = ((bf16[16,1024,128]{2,1,0:T(8,128)(2,1)}), bf16[16,1024,128]{2,1,0:T(8,128)(2,1)}, u32[]{:S(2)}, u32[]{:S(2)}) async-start(bf16[16,1024,128]{2,1,0:T(8,128)(2,1)} %copy-done), calls=%async_computation.1 | async-start | bytes 8388608 | tf_op jit(solution)/shard_map/all_to_all | solution.py:314
  116.9 2.0 %collective-permute-start = (f32[8,128]{1,0:T(8,128)S(1)}, f32[8,128]{1,0:T(8,128)S(1)}, u32[]{:S(2)}, u32[]{:S(2)}) collective-permute-start(f32[8,128]{1,0:T(8,128)S(1)} %get-tuple-element.27), channel_id=1, source_target_pairs={{0,16},{16,0},{32,48},{48,32},{64,80},{80,64},{96,112},{112,96},{1... | collective-permute-start | bytes 12296 | tf_op jit(solution)/shard_map/ppermute | solution.py:317
  118.9 3.6 %collective-permute-start.1 = (f32[8,128]{1,0:T(8,128)S(1)}, f32[8,128]{1,0:T(8,128)S(1)}, u32[]{:S(2)}, u32[]{:S(2)}) collective-permute-start(f32[8,128]{1,0:T(8,128)S(1)} %add.21), channel_id=1, source_target_pairs={{0,32},{16,48},{32,0},{48,16},{64,96},{80,112},{96,64},{112,80},{1... | collective-permute-start | bytes 12296 | tf_op jit(solution)/shard_map/ppermute | solution.py:317
  122.6 5.1 %collective-permute-start.2 = (f32[8,128]{1,0:T(8,128)S(1)}, f32[8,128]{1,0:T(8,128)S(1)}, u32[]{:S(2)}, u32[]{:S(2)}) collective-permute-start(f32[8,128]{1,0:T(8,128)S(1)} %add.22), channel_id=1, source_target_pairs={{0,64},{16,80},{32,96},{48,112},{64,0},{80,16},{96,32},{112,48},{1... | collective-permute-start | bytes 12296 | tf_op jit(solution)/shard_map/ppermute | solution.py:317
  127.8 36.5 %collective-permute-start.3 = (f32[16,8,128]{2,1,0:T(8,128)S(1)}, f32[16,8,128]{2,1,0:T(8,128)S(1)}, u32[]{:S(2)}, u32[]{:S(2)}) collective-permute-start(f32[16,8,128]{2,1,0:T(8,128)S(1)} %broadcast_select_fusion), channel_id=1, source_target_pairs={{0,1},{1,0},{2,3},{3,2},{4,5},{5,4},{6,7},{7,6},{8,9},{9,8},{10,11... | collective-permute-start | bytes 196616 | tf_op jit(solution)/shard_map/ppermute | solution.py:321
  164.4 12.4 %collective-permute-start.4 = (f32[16,8,128]{2,1,0:T(8,128)S(1)}, f32[16,8,128]{2,1,0:T(8,128)S(1)}, u32[]{:S(2)}, u32[]{:S(2)}) collective-permute-start(f32[16,8,128]{2,1,0:T(8,128)S(1)} %fusion), channel_id=1, source_target_pairs={{0,2},{1,3},{2,0},{3,1},{4,6},{5,7},{6,4},{7,5},{8,10},{9,11},{10,... | collective-permute-start | bytes 196616 | tf_op jit(solution)/shard_map/ppermute | solution.py:321
  176.8 4.3 %collective-permute-start.5 = (f32[16,8,128]{2,1,0:T(8,128)S(1)}, f32[16,8,128]{2,1,0:T(8,128)S(1)}, u32[]{:S(2)}, u32[]{:S(2)}) collective-permute-start(f32[16,8,128]{2,1,0:T(8,128)S(1)} %fusion.2), channel_id=1, source_target_pairs={{0,4},{1,5},{2,6},{3,7},{4,0},{5,1},{6,2},{7,3},{8,12},{9,13},{10,... | collective-permute-start | bytes 196616 | tf_op jit(solution)/shard_map/ppermute | solution.py:321
  181.2 7.5 %collective-permute-start.6 = (f32[16,8,128]{2,1,0:T(8,128)S(1)}, f32[16,8,128]{2,1,0:T(8,128)S(1)}, u32[]{:S(2)}, u32[]{:S(2)}) collective-permute-start(f32[16,8,128]{2,1,0:T(8,128)S(1)} %add.26), channel_id=1, source_target_pairs={{0,8},{1,9},{2,10},{3,11},{4,12},{5,13},{6,14},{7,15},{8,0},{9,1},... | collective-permute-start | bytes 196616 | tf_op jit(solution)/shard_map/ppermute | solution.py:321

commit v2 on v1

v2 whole, which is shorter than its diff:
```python
import functools
import math

import jax
import jax.numpy as jnp
import numpy as np
from jax import lax
from jax.experimental import pallas as pl
from jax.experimental.pallas import tpu as pltpu
from jax.sharding import PartitionSpec as P

HEAD_DIM = 128
HALF = HEAD_DIM // 2
EPSILON = 1e-06
APART = float(2**20)
QUERY_TILE = 256
KEY_STEP = 512
SLAB = 4 * HEAD_DIM
F32 = jnp.float32
BF16 = jnp.bfloat16


GRID = 64


def rotary_table():
    sixth = HEAD_DIM // 6
    first = HALF - 2 * sixth
    table = np.zeros((3, GRID, HEAD_DIM))
    begin = 0
    for section, count in enumerate((first, sixth, sixth)):
        freqs = 10000.0 ** (-np.arange(count) / count)
        angle = np.arange(GRID)[:, None] * freqs[None]
        table[section, :, begin : begin + count] = np.cos(angle)
        table[section, :, HALF + begin : HALF + begin + count] = np.sin(angle)
        begin += count
    rest = table.reshape(3 * GRID, HEAD_DIM)
    terms = []
    for _ in range(3):
        terms.append(rest.astype(np.float32).astype(jnp.bfloat16))
        rest = rest - terms[-1].astype(np.float64)
    return np.concatenate(terms, axis=1)


def dot(left, right, contract):
    return lax.dot_general(left, right, ((contract[0], contract[1]), ((), ())), preferred_element_type=F32)


def rotary(rows, table):
    tokens = rows[0].shape[1]
    terms = dot(picks_of(rows), table, ((0,), (0,)))
    both = terms[:, :HEAD_DIM] + terms[:, HEAD_DIM : 2 * HEAD_DIM] + terms[:, 2 * HEAD_DIM :]
    other = pltpu.roll(both, HALF, 1)
    lower = lax.broadcasted_iota(jnp.int32, (tokens, HEAD_DIM), 1) < HALF
    return jnp.where(lower, both, other), jnp.where(lower, -other, both)


def double_table():
    sixth = HEAD_DIM // 6
    first = HALF - 2 * sixth
    table = np.zeros((3, GRID, 2, 2, HALF))
    begin = 0
    for section, count in enumerate((first, sixth, sixth)):
        angle = 2 * np.arange(GRID)[:, None] * 10000.0 ** (-np.arange(count) / count)[None]
        at = slice(begin, begin + count)
        table[section, :, 0, 0, at], table[section, :, 0, 1, at] = np.cos(angle), -np.cos(angle)
        table[section, :, 1, 0, at] = table[section, :, 1, 1, at] = np.sin(angle)
        begin += count
    table = table.reshape(3 * GRID, 2 * HEAD_DIM)
    high = table.astype(np.float32).astype(jnp.bfloat16)
    return np.concatenate([high, (table - high.astype(np.float64)).astype(np.float32).astype(jnp.bfloat16)], axis=1)


def picks_of(rows):
    number = lax.broadcasted_iota(jnp.int32, (GRID, rows[0].shape[1]), 0).astype(F32)
    return jnp.concatenate([jnp.where(number == row, 1.0, 0.0) for row in rows], axis=0).astype(BF16)


def columns(block):
    return pl.ds(pl.multiple_of(block * HEAD_DIM, HEAD_DIM), HEAD_DIM)


def send_kernel(q_hbm, k_hbm, v_hbm, g_hbm, qg_hbm, kg_hbm, pos_hbm, table_hbm, out_hbm, aside_ref, raw, gains, pos_ref, table_ref, stage, place, in_sem, small_sem, through_sem, out_sem, place_sem):
    tokens, feature = q_hbm.shape
    members = out_hbm.shape[0]
    local = feature // members // HEAD_DIM
    small = [
        pltpu.make_async_copy(source, target, small_sem.at[a])
        for a, (source, target) in enumerate(
            ((pos_hbm, pos_ref), (table_hbm, table_ref), (qg_hbm, gains.at[0]), (kg_hbm, gains.at[1]))
        )
    ]
    reads = [pltpu.make_async_copy(ref, raw.at[a], in_sem.at[a]) for a, ref in enumerate((q_hbm, k_hbm, v_hbm, g_hbm))]
    for copy in reads[:1] + small + reads[1:]:
        copy.start()
    small[0].wait()
    small[1].wait()
    rows = [pos_ref[a].astype(F32) for a in range(3)]
    aside_ref[0], aside_ref[1] = rotary(rows, table_ref[...])
    place[...] = jnp.concatenate(rows + [jnp.zeros((13, tokens), F32)], axis=0).astype(BF16)
    places = [
        pltpu.make_async_copy(place, out_hbm.at[j, local * SLAB : local * SLAB + 16, :], place_sem.at[j])
        for j in range(members)
    ]
    for copy in places:
        copy.start()
    for a in range(2):
        reads[a].wait()
        total = jnp.zeros((tokens, HEAD_DIM), F32)
        for h in range(feature // HEAD_DIM):
            part = raw[a, :, h * HEAD_DIM : (h + 1) * HEAD_DIM].astype(F32)
            total = total + part * part
        scale = lax.rsqrt(jnp.sum(total, axis=-1, keepdims=True) / feature + EPSILON)
        aside_ref[2 + a] = jnp.broadcast_to(scale, (tokens, HEAD_DIM))
    small[2].wait()
    small[3].wait()
    through = []
    for a in (2, 3):
        reads[a].wait()
        for j in range(members):
            for h in range(local):
                at = (j * local + h) * HEAD_DIM
                through.append(
                    pltpu.make_async_copy(
                        raw.at[a, :, at : at + HEAD_DIM],
                        out_hbm.at[j, h * SLAB + a * tokens : h * SLAB + (a + 1) * tokens, :],
                        through_sem.at[(j * local + h) * 2 + a - 2],
                    )
                )
                through[-1].start()

    def packet(j, h):
        return pltpu.make_async_copy(
            stage.at[j, h], out_hbm.at[j, h * SLAB : h * SLAB + 2 * tokens, :], out_sem.at[j, h]
        )

    def one(j, carry):
        for h in range(local):
            at = columns(j * local + h)
            for a in range(2):
                x = raw[a, :, at].astype(F32) * aside_ref[2 + a] * gains[a, :, at]
                turned = x * aside_ref[0] + pltpu.roll(x, HALF, 1) * aside_ref[1]
                stage[j, h, a * tokens : (a + 1) * tokens, :] = turned.astype(BF16)
            packet(j, h).start()
        return carry

    lax.fori_loop(0, members, one, 0, unroll=2)
    for copy in through + places:
        copy.wait()
    for j in range(members):
        for h in range(local):
            packet(j, h).wait()


def attention_kernel(len_ref, x_hbm, table_ref, out_hbm, x_ref, out_ref, qt, kt, vt, gt, keymask, s_ref, dk, dv, cos_ref, sin_ref, part_ref, in_sem, out_sem, part_sem):
    members = x_ref.shape[0]
    tok = HEAD_DIM
    tokens = members * tok
    local = (x_ref.shape[1] - 16) // SLAB
    clips = len_ref.shape[0]
    scale = HEAD_DIM ** (-0.5)
    factor = scale * math.log2(math.e)

    def read(i):
        return pltpu.make_async_copy(x_hbm.at[i], x_ref.at[i], in_sem.at[i])

    def start(i, carry):
        read(i).start()
        return carry

    lax.fori_loop(0, members, start, 0)
    ends = []
    so_far = 0
    for c in range(clips):
        so_far = so_far + len_ref[c]
        ends.append(so_far)

    def masks(i, carry):
        token = lax.broadcasted_iota(jnp.int32, (tok, HEAD_DIM), 0) + i * tok
        lane = lax.broadcasted_iota(jnp.int32, (tok, HEAD_DIM), 1)
        clip = jnp.zeros((tok, HEAD_DIM), jnp.int32)
        for c in range(clips):
            clip = clip + (token >= ends[c]).astype(jnp.int32)
        own = clip == lane
        at = pl.ds(pl.multiple_of(i * tok, tok), tok)
        keymask[at, :] = jnp.where(own, -APART, 0.0).astype(BF16)
        token = lax.broadcasted_iota(jnp.int32, (HEAD_DIM, tok), 1) + i * tok
        lane = lax.broadcasted_iota(jnp.int32, (HEAD_DIM, tok), 0)
        clip = jnp.zeros((HEAD_DIM, tok), jnp.int32)
        for c in range(clips):
            clip = clip + (token >= ends[c]).astype(jnp.int32)
        apart = jnp.where(clip == lane, 0.0, 1.0).astype(BF16)
        read(i).wait()
        rows = x_ref[i, local * SLAB : local * SLAB + 16, :].astype(F32)
        terms = dot(picks_of([rows[a : a + 1] for a in range(3)]), table_ref[...], ((0,), (0,)))
        both = terms[:, : 2 * HEAD_DIM] + terms[:, 2 * HEAD_DIM :]
        cos_ref[at, :], sin_ref[at, :] = both[:, :HEAD_DIM], both[:, HEAD_DIM:]
        for h in range(local):
            qt[h, :HEAD_DIM, at] = x_ref[i, h * SLAB : h * SLAB + tok, :].T
            qt[h, HEAD_DIM:, at] = apart
            gt[h, :, at] = x_ref[i, h * SLAB + 3 * tok : h * SLAB + 4 * tok, :].T
            kt[h, :, at] = x_ref[i, h * SLAB + tok : h * SLAB + 2 * tok, :].T
            vt[h, :, at] = x_ref[i, h * SLAB + 2 * tok : h * SLAB + 3 * tok, :].T
            dk[h, at, :] = jnp.zeros((tok, HEAD_DIM), F32)
            dv[h, at, :] = jnp.zeros((tok, HEAD_DIM), F32)
        return carry

    lax.fori_loop(0, members, masks, 0)

    per = QUERY_TILE // tok
    step = KEY_STEP // tok

    def tile(i, carry):
        q0 = i * QUERY_TILE
        first, last = jnp.int32(0), jnp.int32(tokens)
        for c in range(clips):
            first = jnp.where(ends[c] <= q0, ends[c], first)
        for c in reversed(range(clips)):
            last = jnp.where(ends[c] >= q0 + QUERY_TILE, ends[c], last)
        low = first // tok
        count = (last - low * tok + KEY_STEP - 1) // KEY_STEP
        low = jnp.minimum(low, members - count * step)

        def block(h, a, start, number):
            return x_ref[pl.ds(start, number), h * SLAB + a * tok : h * SLAB + (a + 1) * tok, :].reshape(
                number * tok, HEAD_DIM
            )

        q_at = pl.ds(pl.multiple_of(q0, QUERY_TILE), QUERY_TILE)
        queries = [block(h, 0, i * per, per) for h in range(local)]
        cots = [block(h, 3, i * per, per) for h in range(local)]


        def whole(number, heads):
            k0 = [low + j * step for j in range(number)]
            k_at = [pl.ds(pl.multiple_of(k * tok, tok), KEY_STEP) for k in k0]
            s, highest = {}, {}
            for h in heads:
                for j in range(number):
                    keys = jnp.concatenate([block(h, 1, k0[j], step), keymask[k_at[j], :]], axis=1)
                    s[h, j] = dot(keys, qt[h, :, q_at], ((1,), (0,)))
                    m = jnp.max(s[h, j].reshape(KEY_STEP // 8, 8, QUERY_TILE), axis=0)
                    highest[h] = m if j == 0 else jnp.maximum(highest[h], m)
            e, total, out = {}, {}, {}
            for h in heads:
                top = jnp.max(highest[h], axis=0, keepdims=True)
                for j in range(number):
                    e[h, j] = jnp.exp2((s[h, j] - top) * factor)
                    t = jnp.sum(e[h, j].reshape(KEY_STEP // 8, 8, QUERY_TILE), axis=0)
                    o = dot(vt[h, :, k_at[j]], e[h, j].astype(BF16), ((1,), (0,)))
                    total[h] = t if j == 0 else total[h] + t
                    out[h] = o if j == 0 else out[h] + o
            for h in heads:
                inv = 1.0 / jnp.sum(total[h], axis=0, keepdims=True)
                attended = (out[h] * inv).astype(BF16)
                delta = jnp.sum(attended.astype(F32) * gt[h, :, q_at].astype(F32), axis=0, keepdims=True)
                out_ref[pl.ds(i * per, per), h * SLAB : h * SLAB + tok, :] = attended.T.reshape(per, tok, HEAD_DIM)
                for j in range(number):
                    prob = e[h, j] * inv
                    dprob = dot(block(h, 2, k0[j], step), gt[h, :, q_at], ((1,), (0,)))
                    dscore = (prob * (dprob - delta)).astype(BF16)
                    dv[h, k_at[j], :] += dot(prob.astype(BF16), cots[h], ((1,), (0,)))
                    dk[h, k_at[j], :] += dot(dscore, queries[h], ((1,), (0,)))
                    d = dot(kt[h, :, k_at[j]], dscore, ((1,), (0,)))
                    dq = d if j == 0 else dq + d
                dq_tile = (dq * scale).astype(BF16)
                out_ref[pl.ds(i * per, per), h * SLAB + tok : h * SLAB + 2 * tok, :] = dq_tile.T.reshape(
                    per, tok, HEAD_DIM
                )

        for number in range(1, tokens // KEY_STEP + 1):

            @pl.when(count == number)
            def _():
                whole(number, range(local))

        return carry

    lax.fori_loop(0, tokens // QUERY_TILE, tile, 0)

    def write(i):
        return pltpu.make_async_copy(out_ref.at[i], out_hbm.at[i, : local * SLAB, :], out_sem.at[i])

    def finish(i, sums):
        at = pl.ds(pl.multiple_of(i * tok, tok), tok)
        cosine, sine = cos_ref[at, :], sin_ref[at, :]
        new = []
        for h in range(local):
            dk_tile = (dk[h, at, :] * scale).astype(BF16)
            out_ref[i, h * SLAB + 2 * tok : h * SLAB + 3 * tok, :] = dk_tile
            out_ref[i, h * SLAB + 3 * tok : h * SLAB + 4 * tok, :] = dv[h, at, :].astype(BF16)
        write(i).start()
        for h in range(local):
            for a, row in ((0, 1), (1, 2)):
                g = out_ref[i, h * SLAB + row * tok : h * SLAB + (row + 1) * tok, :].astype(F32)
                p = x_ref[i, h * SLAB + a * tok : h * SLAB + (a + 1) * tok, :].astype(F32)
                straight = g * p
                across = straight * cosine + g * pltpu.roll(p, HALF, 1) * sine
                plain, turned = sums[2 * h + a]
                new.append(
                    (
                        plain + jnp.sum(straight.reshape(tok // 8, 8, HEAD_DIM), axis=0),
                        turned + jnp.sum(across.reshape(tok // 8, 8, HEAD_DIM), axis=0),
                    )
                )
        return tuple(new)

    zero = jnp.zeros((8, HEAD_DIM), F32)
    sums = lax.fori_loop(0, members, finish, ((zero, zero),) * (2 * local))
    plain, turned = (jnp.concatenate([jnp.sum(s[n], axis=0, keepdims=True) for s in sums], axis=0) for n in range(2))
    plain = plain + pltpu.roll(plain, HALF, 1)
    turned = turned + pltpu.roll(turned, HALF, 1)
    lower = lax.broadcasted_iota(jnp.int32, plain.shape, 1) < HALF
    rest = 0.5 * (plain + jnp.where(lower, turned, -turned))
    terms = []
    for _ in range(3):
        terms.append(rest.astype(BF16).astype(F32))
        rest = rest - terms[-1]
    terms.append(jnp.zeros((16 - 6 * local, HEAD_DIM), F32))
    part_ref[...] = jnp.concatenate(terms, axis=0).astype(BF16)
    parts = [
        pltpu.make_async_copy(part_ref, out_hbm.at[i, local * SLAB : local * SLAB + 16, :], part_sem.at[i])
        for i in range(members)
    ]
    for copy in parts:
        copy.start()
    for i in range(members):
        write(i).wait()
        parts[i].wait()


def spread_kernel(y_hbm, att_hbm, gv_hbm, sem):
    tokens, feature = att_hbm.shape
    members = y_hbm.shape[0]
    local = feature // members // HEAD_DIM
    copies = []
    for j in range(members):
        for h in range(local):
            for a, (ref, row) in enumerate(((att_hbm, 0), (gv_hbm, 3))):
                at = (j * local + h) * HEAD_DIM
                copies.append(
                    pltpu.make_async_copy(
                        y_hbm.at[j, h * SLAB + row * tokens : h * SLAB + (row + 1) * tokens, :],
                        ref.at[:, at : at + HEAD_DIM],
                        sem.at[(j * local + h) * 2 + a],
                    )
                )
                copies[-1].start()
    for copy in copies:
        copy.wait()


def norm_kernel(which, y_ref, raw_ref, gain_ref, aside_ref, grad_hbm, lift_ref, stage, sem):
    tokens, feature = raw_ref.shape
    members = y_ref.shape[0]
    local = feature // members // HEAD_DIM
    parts = sem.shape[0]

    def first(j, total):
        for h in range(local):
            at = columns(j * local + h)
            g = y_ref[j, h * SLAB + (which + 1) * tokens : h * SLAB + (which + 2) * tokens, :].astype(F32)
            g = g * aside_ref[0] - pltpu.roll(g, HALF, 1) * aside_ref[1]
            lift = g * gain_ref[:, at]
            lift_ref[:, at] = lift
            total = total + lift * (raw_ref[:, at].astype(F32) * aside_ref[2 + which])
        return total

    total = lax.fori_loop(0, members, first, jnp.zeros((tokens, HEAD_DIM), F32), unroll=2)
    inner = jnp.sum(total, axis=-1, keepdims=True) / feature
    width = feature // parts
    copies = []
    for part in range(parts):
        for block in range(part * width // HEAD_DIM, (part + 1) * width // HEAD_DIM):
            at = slice(block * HEAD_DIM, (block + 1) * HEAD_DIM)
            hat = raw_ref[:, at].astype(F32) * aside_ref[2 + which]
            stage[:, at] = (aside_ref[2 + which] * (lift_ref[:, at] - hat * inner)).astype(BF16)
        at = slice(part * width, (part + 1) * width)
        copies.append(pltpu.make_async_copy(stage.at[:, at], grad_hbm.at[:, at], sem.at[part]))
        copies[-1].start()
    for copy in copies:
        copy.wait()


def on_device(q_raw, k_raw, values, grad_out, q_gain, k_gain, lengths, positions):
    members = lax.axis_size("seq")
    replicas = lax.axis_size("dp")
    _, tok, feature = q_raw.shape
    local = feature // members // HEAD_DIM
    tokens = tok * members
    vmem = pl.BlockSpec(memory_space=pltpu.VMEM)
    smem = pl.BlockSpec(memory_space=pltpu.SMEM)
    hbm = pl.BlockSpec(memory_space=pltpu.HBM)
    sems = pltpu.SemaphoreType.DMA
    table = jnp.asarray(rotary_table())
    shape = jax.ShapeDtypeStruct
    wide = shape((tok, HEAD_DIM), F32)
    whole = shape((members, local * SLAB + 16, HEAD_DIM), BF16)
    params = pltpu.CompilerParams(vmem_limit_bytes=48 << 20)

    packet, aside = pl.pallas_call(
        send_kernel,
        out_shape=(whole, shape((4, tok, HEAD_DIM), F32)),
        in_specs=[hbm] * 8,
        out_specs=(hbm, vmem),
        scratch_shapes=[
            pltpu.VMEM((4, tok, feature), BF16),
            pltpu.VMEM((2, 1, feature), F32),
            pltpu.VMEM((3, 1, tok), jnp.int32),
            pltpu.VMEM(table.shape, BF16),
            pltpu.VMEM((members, local, 2 * tok, HEAD_DIM), BF16),
            pltpu.VMEM((16, tok), BF16),
            sems((4,)),
            sems((4,)),
            sems((members * local * 2,)),
            sems((members, local)),
            sems((members,)),
        ],
        compiler_params=pltpu.CompilerParams(vmem_limit_bytes=60 << 20),
        cost_estimate=pl.CostEstimate(flops=40 << 20, bytes_accessed=9 << 20, transcendentals=0),
        name="send",
    )(q_raw[0], k_raw[0], values[0], grad_out[0], q_gain[None], k_gain[None], jnp.transpose(positions, (1, 0, 2)), table)

    got = lax.all_to_all(packet, "seq", 0, 0, tiled=True)

    back = pl.pallas_call(
        attention_kernel,
        out_shape=whole,
        in_specs=[smem, hbm, vmem],
        out_specs=hbm,
        scratch_shapes=[
            pltpu.VMEM((members, local * SLAB + 16, HEAD_DIM), BF16),
            pltpu.VMEM((members, local * SLAB, HEAD_DIM), BF16),
            pltpu.VMEM((local, 2 * HEAD_DIM, tokens), BF16),
            pltpu.VMEM((local, HEAD_DIM, tokens), BF16),
            pltpu.VMEM((local, HEAD_DIM, tokens), BF16),
            pltpu.VMEM((local, HEAD_DIM, tokens), BF16),
            pltpu.VMEM((tokens, HEAD_DIM), BF16),
            pltpu.VMEM((local, tokens, QUERY_TILE), F32),
            pltpu.VMEM((local, tokens, HEAD_DIM), F32),
            pltpu.VMEM((local, tokens, HEAD_DIM), F32),
            pltpu.VMEM((tokens, HEAD_DIM), F32),
            pltpu.VMEM((tokens, HEAD_DIM), F32),
            pltpu.VMEM((16, HEAD_DIM), BF16),
            sems((members,)),
            sems((members,)),
            sems((members,)),
        ],
        compiler_params=params,
        cost_estimate=pl.CostEstimate(flops=12 << 30, bytes_accessed=9 << 20, transcendentals=1 << 22),
        name="attention",
    )(lengths[0], got, jnp.asarray(double_table()))

    returned = lax.all_to_all(back, "seq", 0, 0, tiled=True)

    sums = sum(
        returned[:, local * SLAB + 2 * local * t : local * SLAB + 2 * local * (t + 1)].astype(F32) for t in range(3)
    )

    def add(value, distance):
        return value + lax.ppermute(value, "dp", [(i, i ^ distance) for i in range(replicas)])

    def norm(returned, which, raw, gain):
        return pl.pallas_call(
            functools.partial(norm_kernel, which),
            out_shape=shape((tok, feature), BF16),
            in_specs=[vmem] * 4,
            out_specs=hbm,
            scratch_shapes=[pltpu.VMEM((tok, feature), F32), pltpu.VMEM((tok, feature), BF16), sems((4,))],
            compiler_params=pltpu.CompilerParams(vmem_limit_bytes=24 << 20),
            cost_estimate=pl.CostEstimate(flops=20 << 20, bytes_accessed=4 << 20, transcendentals=0),
            name="receive",
        )(returned, raw[0], gain[None], aside)

    added = add(sums, 1)
    attended, grad_v = pl.pallas_call(
        spread_kernel,
        out_shape=(shape((tok, feature), BF16),) * 2,
        in_specs=[hbm],
        out_specs=(hbm, hbm),
        scratch_shapes=[sems((members * local * 2,))],
        compiler_params=params,
        cost_estimate=pl.CostEstimate(flops=0, bytes_accessed=8 << 20, transcendentals=0),
        name="receive_spread",
    )(returned)
    added, attended, grad_v, returned = lax.optimization_barrier((added, attended, grad_v, returned))
    sums = add(added, 2)
    grad_q = norm(returned, 0, q_raw, q_gain)
    sums, grad_q, returned = lax.optimization_barrier((sums, grad_q, returned))
    sums = add(sums, 4)
    grad_k = norm(returned, 1, k_raw, k_gain)
    gains = sums.reshape(members, local, 2, HEAD_DIM)
    gain_out = [gains[:, :, a].reshape(feature) / (gain * replicas) for a, gain in enumerate((q_gain, k_gain))]
    return tuple(o[None] for o in (attended, grad_q, grad_k, grad_v)) + tuple(gain_out)


def solution(mesh):
    tokens_split = P("dp", "seq", None)
    return jax.shard_map(
        on_device,
        mesh=mesh,
        in_specs=(tokens_split,) * 4 + (P(), P(), P("dp", None), P("dp", None, "seq")),
        out_specs=(tokens_split,) * 4 + (P(), P()),
        check_vma=False,
    )
```

time: 199 us -> 161 us (0.81)
  waiting for transfers between devices: 59.8 us -> 0.9 us
  blocking collectives: 60.5 us -> 115 us
  starting transfers between devices: 16.3 us -> 4.68 us
  Pallas kernels: 49.9 us -> 39.1 us
  local copies, waits for them, and re-layouts: 9.73 us -> 0.06 us
    ppermute x7 -> x3, waiting for transfers between devices: 59.8 us -> 0.9 us  [add(): lax.ppermute(value, 'dp', [(i, i ^ distance) for i in range(replicas)])]
    all_to_all x0 -> x1, blocking collectives: none -> 54 us  [on_device(): returned = lax.all_to_all(back, 'seq', 0, 0, tiled=True)]
    pallas_call x3 -> x5, Pallas kernels: 49.9 us -> 39.1 us  [the longest x1 25.7 us: on_device(): pl.pallas_call(attention_kernel, out_shape=whole, in_specs=[smem, hbm, vm...]
    unnamed x27 -> x14, local copies, waits for them, and re-layouts: 9.7 us -> 0.04 us
    ppermute x7 -> x3, starting transfers between devices: 11.6 us -> 4.68 us  [add(): lax.ppermute(value, 'dp', [(i, i ^ distance) for i in range(replicas)])]
    all_to_all x1 -> x0, starting transfers between devices: 4.69 us -> none  [on_device(): returned = lax.all_to_all(back, 'seq', 0, 0, tiled=True)]
  transfers between devices with their start and end apart: 8 -> 3, of which waited for: 7 -> 1; matrix products, arithmetic and copies ran while one was open for 0% -> 0% of each run, Pallas kernels for 0% -> 4%
where the time goes in v2:
time: 161 us
  blocking collectives  115 us (71%)
  Pallas kernels  39.1 us (24%)
  starting transfers between devices  4.68 us (3%)
    all_to_all x1, blocking collectives, on_device(): got = lax.all_to_all(packet, 'seq', 0, 0, tiled=True)  60.5 us
    all_to_all x1, blocking collectives, on_device(): returned = lax.all_to_all(back, 'seq', 0, 0, tiled=True)  54 us
    pallas_call x1, Pallas kernels, on_device(): pl.pallas_call(attention_kernel, out_shape=whole, in_specs=[smem, hbm, vm...  25.7 us
    pallas_call x1, Pallas kernels, on_device(): pl.pallas_call(send_kernel, out_shape=(whole, shape((4, tok, HEAD_DIM), F...  6.63 us
    pallas_call x2, Pallas kernels, norm(): pl.pallas_call(functools.partial(norm_kernel, which), out_shape=shape((to...  4.94 us
    ppermute x3, starting transfers between devices, add(): lax.ppermute(value, 'dp', [(i, i ^ distance) for i in range(replicas)])  4.68 us
  transfers between devices with their start and end apart: 3, of which 1 were waited for; matrix products, arithmetic and copies ran while one was open for 0% of the time, Pallas kernels for 4%

profile of v2, /device:TPU:0, one launch (start us, length us, event | category | flops | bytes accessed | tf_op | source)
XLA Modules:
  0.0 160.7 jit_solution(2466895638793876344)
XLA Ops:
  0.6 6.6 %send.1 = (bf16[16,1040,128]{2,1,0:T(8,128)(2,1)}, f32[4,128,128]{2,1,0:T(8,128)}) custom-call(bf16[128,4096]{1,0:T(8,128)(2,1)} %bitcast.15, bf16[128,4096]{1,0:T(8,128)(2,1)} %bitcast.17, bf16[128,4096]{1,0:T(8,128)(2,1)} %bitcast.24, bf16[128,4096]{1,0:T(8,128)(2,1)} %bitcast.25, f32[1,4096]{1,0:T(1,128)} %bitcast.19, f32[1,4096]{1,0:T(1,128)} %bitcast.21, ...), custom_call_target="tpu_custom_call" | custom-call | flops 41943040 | bytes 9437184 | tf_op jit(solution)/shard_map/send/pallas_call | solution.py:401
  7.3 0.0 copy-start.5
  7.3 0.0 copy-start.6
  7.3 60.5 %all_to_all.10.x_hbm = bf16[16,1040,128]{2,1,0:T(8,128)(2,1)} all-to-all(bf16[16,1040,128]{2,1,0:T(8,128)(2,1)} %get-tuple-element.17), channel_id=1, replica_groups=mesh['dp'=8,'seq'=16] {'seq'}, dimensions={0} | all-to-all | bytes 8519680 | tf_op jit(solution)/shard_map/all_to_all | solution.py:424
  67.8 0.0 copy-done.5
  67.8 0.0 copy-done.6
  67.8 25.7 %attention.1 = bf16[16,1040,128]{2,1,0:T(8,128)(2,1)S(1)} custom-call(s32[6]{0:T(128)S(1)} %bitcast.23, bf16[16,1040,128]{2,1,0:T(8,128)(2,1)} %all_to_all.10.x_hbm, bf16[192,512]{1,0:T(8,128)(2,1)S(1)} %copy-done.6), custom_call_target="tpu_custom_call" | custom-call | flops 12884901888 | bytes 9437184 | tf_op jit(solution)/shard_map/attention/pallas_call | solution.py:426
  93.5 54.0 %all_to_all.11.y_hbm.y_ref = bf16[16,1040,128]{2,1,0:T(8,128)(2,1)S(1)} all-to-all(bf16[16,1040,128]{2,1,0:T(8,128)(2,1)S(1)} %attention.1), channel_id=1, replica_groups=mesh['dp'=8,'seq'=16] {'seq'}, dimensions={0} | all-to-all | bytes 8519680 | tf_op jit(solution)/shard_map/all_to_all | solution.py:454
  147.5 0.0 copy-start
  147.5 0.0 copy-start.2
  147.5 0.0 copy-start.3
  147.5 0.1 collective-permute-start
  147.6 1.9 %receive_spread.1 = (bf16[128,4096]{1,0:T(8,128)(2,1)}, bf16[128,4096]{1,0:T(8,128)(2,1)}) custom-call(bf16[16,1040,128]{2,1,0:T(8,128)(2,1)S(1)} %all_to_all.11.y_hbm.y_ref), custom_call_target="tpu_custom_call" | custom-call | bytes 8388608 | tf_op jit(solution)/shard_map/receive_spread/pallas_call | solution.py:476
  149.4 0.0 copy-start.1
  149.5 0.0 copy-start.4
  149.5 0.0 collective-permute-done
  149.5 2.5 %collective-permute-start.1 = (f32[16,4,128]{2,1,0:T(4,128)S(1)}, f32[16,4,128]{2,1,0:T(4,128)S(1)}, u32[]{:S(2)}, u32[]{:S(2)}) collective-permute-start(f32[16,4,128]{2,1,0:T(4,128)S(1)} %fusion.1), channel_id=1, source_target_pairs={{0,32},{16,48},{32,0},{48,16},{64,96},{80,112},{96,64},{112,80},{1... | collective-permute-start | bytes 98312 | tf_op jit(solution)/shard_map/ppermute | solution.py:461
  152.0 0.0 copy-done
  152.0 0.0 copy-done.2
  152.0 0.0 copy-done.3
  152.0 2.5 %receive.2 = bf16[128,4096]{1,0:T(8,128)(2,1)} custom-call(bf16[16,1040,128]{2,1,0:T(8,128)(2,1)S(1)} %all_to_all.11.y_hbm.y_ref, bf16[128,4096]{1,0:T(8,128)(2,1)S(1)} %bitcast.16, f32[1,4096]{1,0:T(1,128)S(1)} %bitcast.20, f32[4,128,128]{2,1,0:T(8,128)S(1)} %copy-done.2), custom_call_target="tpu_custom_call" | custom-call | flops 20971520 | bytes 4194304 | tf_op jit(solution)/shard_map/receive/pallas_call | solution.py:464
  154.5 0.0 collective-permute-done.1
  154.5 2.1 %collective-permute-start.2 = (f32[16,4,128]{2,1,0:T(4,128)S(1)}, f32[16,4,128]{2,1,0:T(4,128)S(1)}, u32[]{:S(2)}, u32[]{:S(2)}) collective-permute-start(f32[16,4,128]{2,1,0:T(4,128)S(1)} %add.18), channel_id=1, source_target_pairs={{0,64},{16,80},{32,96},{48,112},{64,0},{80,16},{96,32},{112,48},{1... | collective-permute-start | bytes 98312 | tf_op jit(solution)/shard_map/ppermute | solution.py:461
  156.6 0.0 copy-done.1
  156.6 0.0 copy-done.4
  156.6 2.5 %receive.3 = bf16[128,4096]{1,0:T(8,128)(2,1)} custom-call(bf16[16,1040,128]{2,1,0:T(8,128)(2,1)S(1)} %all_to_all.11.y_hbm.y_ref, bf16[128,4096]{1,0:T(8,128)(2,1)S(1)} %bitcast.18, f32[1,4096]{1,0:T(1,128)S(1)} %bitcast.22, f32[4,128,128]{2,1,0:T(8,128)S(1)} %copy-done.2), custom_call_target="tpu_custom_call" | custom-call | flops 20971520 | bytes 4194304 | tf_op jit(solution)/shard_map/receive/pallas_call | solution.py:464
  159.1 0.9 collective-permute-done.2
  160.0 0.6 multiply_divide_fusion
  (5 shorter events, 0.1 us)
Async XLA Ops:
  7.3 60.6 %copy-start.5 = (s32[1,6]{1,0:T(1,128)S(1)}, s32[1,6]{1,0:T(1,128)}, u32[]{:S(2)}) copy-start(s32[1,6]{1,0:T(1,128)} %param.16) | copy-start | bytes 76
  7.3 60.6 %copy-start.6 = (bf16[192,512]{1,0:T(8,128)(2,1)S(1)}, bf16[192,512]{1,0:T(8,128)(2,1)}, u32[]{:S(2)}) copy-start(bf16[192,512]{1,0:T(8,128)(2,1)} %constant.7.clone.table_ref) | copy-start | bytes 589828
  147.5 4.5 %copy-start = (bf16[1,128,4096]{2,1,0:T(8,128)(2,1)S(1)}, bf16[1,128,4096]{2,1,0:T(8,128)(2,1)}, u32[]{:S(2)}) copy-start(bf16[1,128,4096]{2,1,0:T(8,128)(2,1)} %param.10) | copy-start | bytes 3145732
  147.5 4.5 %copy-start.2 = (f32[4,128,128]{2,1,0:T(8,128)S(1)}, f32[4,128,128]{2,1,0:T(8,128)}, u32[]{:S(2)}) copy-start(f32[4,128,128]{2,1,0:T(8,128)} %get-tuple-element.23.aside_ref) | copy-start | bytes 786436
  147.5 4.5 %copy-start.3 = (f32[4096]{0:T(1024)S(1)}, f32[4096]{0:T(1024)}, u32[]{:S(2)}) copy-start(f32[4096]{0:T(1024)} %param.14) | copy-start | bytes 49156
  147.5 2.0 %collective-permute-start = (f32[16,4,128]{2,1,0:T(4,128)S(1)}, f32[16,4,128]{2,1,0:T(4,128)S(1)}, u32[]{:S(2)}, u32[]{:S(2)}) collective-permute-start(f32[16,4,128]{2,1,0:T(4,128)S(1)} %convert_add_fusion), channel_id=1, source_target_pairs={{0,16},{16,0},{32,48},{48,32},{64,80},{80,64},{96,112},{112,96},{1... | collective-permute-start | bytes 98312 | tf_op jit(solution)/shard_map/ppermute | solution.py:461
  149.4 7.2 %copy-start.1 = (bf16[1,128,4096]{2,1,0:T(8,128)(2,1)S(1)}, bf16[1,128,4096]{2,1,0:T(8,128)(2,1)}, u32[]{:S(2)}) copy-start(bf16[1,128,4096]{2,1,0:T(8,128)(2,1)} %param.11) | copy-start | bytes 3145732
  149.5 7.2 %copy-start.4 = (f32[4096]{0:T(1024)S(1)}, f32[4096]{0:T(1024)}, u32[]{:S(2)}) copy-start(f32[4096]{0:T(1024)} %param.15) | copy-start | bytes 49156
  149.5 5.0 %collective-permute-start.1 = (f32[16,4,128]{2,1,0:T(4,128)S(1)}, f32[16,4,128]{2,1,0:T(4,128)S(1)}, u32[]{:S(2)}, u32[]{:S(2)}) collective-permute-start(f32[16,4,128]{2,1,0:T(4,128)S(1)} %fusion.1), channel_id=1, source_target_pairs={{0,32},{16,48},{32,0},{48,16},{64,96},{80,112},{96,64},{112,80},{1... | collective-permute-start | bytes 98312 | tf_op jit(solution)/shard_map/ppermute | solution.py:461
  154.5 5.5 %collective-permute-start.2 = (f32[16,4,128]{2,1,0:T(4,128)S(1)}, f32[16,4,128]{2,1,0:T(4,128)S(1)}, u32[]{:S(2)}, u32[]{:S(2)}) collective-permute-start(f32[16,4,128]{2,1,0:T(4,128)S(1)} %add.18), channel_id=1, source_target_pairs={{0,64},{16,80},{32,96},{48,112},{64,0},{80,16},{96,32},{112,48},{1... | collective-permute-start | bytes 98312 | tf_op jit(solution)/shard_map/ppermute | solution.py:461

commit v3 on v2

v3 whole, which is shorter than its diff:
```python
import functools
import math

import jax
import jax.numpy as jnp
import numpy as np
from jax import lax
from jax.experimental import pallas as pl
from jax.experimental.pallas import tpu as pltpu
from jax.sharding import PartitionSpec as P

HEAD_DIM = 128
HALF = HEAD_DIM // 2
EPSILON = 1e-06
APART = float(2**20)
QUERY_TILE = 256
KEY_STEP = 512
SLAB = 4 * HEAD_DIM
F32 = jnp.float32
BF16 = jnp.bfloat16


GRID = 64


def rotary_table():
    sixth = HEAD_DIM // 6
    first = HALF - 2 * sixth
    table = np.zeros((3, GRID, HEAD_DIM))
    begin = 0
    for section, count in enumerate((first, sixth, sixth)):
        freqs = 10000.0 ** (-np.arange(count) / count)
        angle = np.arange(GRID)[:, None] * freqs[None]
        table[section, :, begin : begin + count] = np.cos(angle)
        table[section, :, HALF + begin : HALF + begin + count] = np.sin(angle)
        begin += count
    rest = table.reshape(3 * GRID, HEAD_DIM)
    terms = []
    for _ in range(3):
        terms.append(rest.astype(np.float32).astype(jnp.bfloat16))
        rest = rest - terms[-1].astype(np.float64)
    return np.concatenate(terms, axis=1)


def dot(left, right, contract):
    return lax.dot_general(left, right, ((contract[0], contract[1]), ((), ())), preferred_element_type=F32)


def rotary(rows, table):
    tokens = rows[0].shape[1]
    terms = dot(picks_of(rows), table, ((0,), (0,)))
    both = terms[:, :HEAD_DIM] + terms[:, HEAD_DIM : 2 * HEAD_DIM] + terms[:, 2 * HEAD_DIM :]
    other = pltpu.roll(both, HALF, 1)
    lower = lax.broadcasted_iota(jnp.int32, (tokens, HEAD_DIM), 1) < HALF
    return jnp.where(lower, both, other), jnp.where(lower, -other, both)


def double_table():
    sixth = HEAD_DIM // 6
    first = HALF - 2 * sixth
    table = np.zeros((3, GRID, 2, 2, HALF))
    begin = 0
    for section, count in enumerate((first, sixth, sixth)):
        angle = 2 * np.arange(GRID)[:, None] * 10000.0 ** (-np.arange(count) / count)[None]
        at = slice(begin, begin + count)
        table[section, :, 0, 0, at], table[section, :, 0, 1, at] = np.cos(angle), -np.cos(angle)
        table[section, :, 1, 0, at] = table[section, :, 1, 1, at] = np.sin(angle)
        begin += count
    table = table.reshape(3 * GRID, 2 * HEAD_DIM)
    high = table.astype(np.float32).astype(jnp.bfloat16)
    return np.concatenate([high, (table - high.astype(np.float64)).astype(np.float32).astype(jnp.bfloat16)], axis=1)


def picks_of(rows):
    number = lax.broadcasted_iota(jnp.int32, (GRID, rows[0].shape[1]), 0).astype(F32)
    return jnp.concatenate([jnp.where(number == row, 1.0, 0.0) for row in rows], axis=0).astype(BF16)


def columns(block):
    return pl.ds(pl.multiple_of(block * HEAD_DIM, HEAD_DIM), HEAD_DIM)


def send_kernel(head, q_hbm, k_hbm, v_hbm, g_hbm, qg_hbm, kg_hbm, pos_hbm, table_hbm, *rest):
    if head == 0:
        out_hbm, aside_ref, raw, gains, pos_ref, table_ref, stage, in_sem, small_sem, out_sem = rest
    else:
        aside_ref, out_hbm, raw, gains, stage, in_sem, small_sem, out_sem = rest
    tokens, feature = q_hbm.shape
    members = out_hbm.shape[0]
    local = feature // members // HEAD_DIM
    sources = [(qg_hbm, gains.at[0]), (kg_hbm, gains.at[1])]
    if head == 0:
        sources += [(pos_hbm, pos_ref), (table_hbm, table_ref)]
    small = [pltpu.make_async_copy(source, target, small_sem.at[a]) for a, (source, target) in enumerate(sources)]
    reads = [pltpu.make_async_copy(ref, raw.at[a], in_sem.at[a]) for a, ref in enumerate((q_hbm, k_hbm, v_hbm, g_hbm))]
    for copy in small + reads:
        copy.start()
    for copy in small:
        copy.wait()
    if head == 0:
        rows = [pos_ref[a].astype(F32) for a in range(3)]
        aside_ref[0], aside_ref[1] = rotary(rows, table_ref[...])
        place = jnp.concatenate(rows + [jnp.zeros((13, tokens), F32)], axis=0).astype(BF16)
    for a in range(2):
        reads[a].wait()
        if head == 0:
            total = jnp.zeros((tokens, HEAD_DIM), F32)
            for h in range(feature // HEAD_DIM):
                part = raw[a, :, h * HEAD_DIM : (h + 1) * HEAD_DIM].astype(F32)
                total = total + part * part
            scale = lax.rsqrt(jnp.sum(total, axis=-1, keepdims=True) / feature + EPSILON)
            aside_ref[2 + a] = jnp.broadcast_to(scale, (tokens, HEAD_DIM))
    reads[2].wait()
    reads[3].wait()
    packets = []
    group = members // out_sem.shape[0]
    for j in range(members):
        at = slice((j * local + head) * HEAD_DIM, (j * local + head + 1) * HEAD_DIM)
        for a in range(2):
            x = raw[a, :, at].astype(F32) * aside_ref[2 + a] * gains[a, :, at]
            turned = x * aside_ref[0] + pltpu.roll(x, HALF, 1) * aside_ref[1]
            stage[j, a * tokens : (a + 1) * tokens, :] = turned.astype(BF16)
        for a in (2, 3):
            stage[j, a * tokens : (a + 1) * tokens, :] = raw[a, :, at]
        if head == 0:
            stage[j, SLAB:, :] = place
        if j % group == group - 1:
            some = slice(j + 1 - group, j + 1)
            packets.append(pltpu.make_async_copy(stage.at[some], out_hbm.at[some], out_sem.at[j // group]))
            packets[-1].start()
    for copy in packets:
        copy.wait()


def attention_kernel(head, len_ref, x_hbm, *rest):
    if head == 0:
        table_ref, out_hbm, sum_ref, angles_hbm, *rest = rest
    else:
        angles_hbm, before_ref, out_hbm, sum_ref, *rest = rest
    x_ref, out_ref, qt, kt, vt, gt, keymask, dk, dv, angles, in_sem, out_sem, angle_sem = rest
    members = x_ref.shape[0]
    tok = HEAD_DIM
    tokens = members * tok
    local = 1
    clips = len_ref.shape[0]
    scale = HEAD_DIM ** (-0.5)
    factor = scale * math.log2(math.e)

    group = members // in_sem.shape[0]

    def read(n):
        some = pl.ds(n * group, group)
        return pltpu.make_async_copy(x_hbm.at[some], x_ref.at[some], in_sem.at[n])

    for n in range(members // group):
        read(n).start()
    if head == 0:
        hand = pltpu.make_async_copy(angles, angles_hbm, angle_sem)
    else:
        hand = pltpu.make_async_copy(angles_hbm, angles, angle_sem)
        hand.start()
    ends = []
    so_far = 0
    for c in range(clips):
        so_far = so_far + len_ref[c]
        ends.append(so_far)

    def masks(i, carry):
        token = lax.broadcasted_iota(jnp.int32, (tok, HEAD_DIM), 0) + i * tok
        lane = lax.broadcasted_iota(jnp.int32, (tok, HEAD_DIM), 1)
        clip = jnp.zeros((tok, HEAD_DIM), jnp.int32)
        for c in range(clips):
            clip = clip + (token >= ends[c]).astype(jnp.int32)
        own = clip == lane
        at = pl.ds(pl.multiple_of(i * tok, tok), tok)
        keymask[at, :] = jnp.where(own, -APART, 0.0).astype(BF16)
        token = lax.broadcasted_iota(jnp.int32, (HEAD_DIM, tok), 1) + i * tok
        lane = lax.broadcasted_iota(jnp.int32, (HEAD_DIM, tok), 0)
        clip = jnp.zeros((HEAD_DIM, tok), jnp.int32)
        for c in range(clips):
            clip = clip + (token >= ends[c]).astype(jnp.int32)
        apart = jnp.where(clip == lane, 0.0, 1.0).astype(BF16)

        @pl.when(lax.rem(i, group) == 0)
        def _():
            read(i // group).wait()

        if head == 0:
            rows = x_ref[i, SLAB:, :].astype(F32)
            terms = dot(picks_of([rows[a : a + 1] for a in range(3)]), table_ref[...], ((0,), (0,)))
            angles[at, :] = terms[:, : 2 * HEAD_DIM] + terms[:, 2 * HEAD_DIM :]
        for h in range(local):
            qt[h, :HEAD_DIM, at] = x_ref[i, h * SLAB : h * SLAB + tok, :].T
            qt[h, HEAD_DIM:, at] = apart
            gt[h, :, at] = x_ref[i, h * SLAB + 3 * tok : h * SLAB + 4 * tok, :].T
            kt[h, :, at] = x_ref[i, h * SLAB + tok : h * SLAB + 2 * tok, :].T
            vt[h, :, at] = x_ref[i, h * SLAB + 2 * tok : h * SLAB + 3 * tok, :].T
            dk[h, at, :] = jnp.zeros((tok, HEAD_DIM), F32)
            dv[h, at, :] = jnp.zeros((tok, HEAD_DIM), F32)
        return carry

    lax.fori_loop(0, members, masks, 0)
    if head == 0:
        hand.start()

    per = QUERY_TILE // tok
    step = KEY_STEP // tok

    def window(i):
        first, last = jnp.int32(0), jnp.int32(tokens)
        for c in range(clips):
            first = jnp.where(ends[c] <= i * QUERY_TILE, ends[c], first)
        for c in reversed(range(clips)):
            last = jnp.where(ends[c] >= (i + 1) * QUERY_TILE, ends[c], last)
        low = first // tok
        return low, (last - low * tok + KEY_STEP - 1) // KEY_STEP

    def block(a, start, number):
        return x_ref[pl.ds(start, number), a * tok : (a + 1) * tok, :].reshape(number * tok, HEAD_DIM)

    def pair(i, carry):
        tiles = (2 * i, 2 * i + 1)
        windows = [window(t) for t in tiles]
        count = jnp.maximum(windows[0][1], windows[1][1])
        q_at = [pl.ds(pl.multiple_of(t * QUERY_TILE, QUERY_TILE), QUERY_TILE) for t in tiles]

        def whole(number):
            both = range(2)
            k0 = [[jnp.minimum(windows[t][0], members - number * step) + j * step for j in range(number)] for t in both]
            k_at = [[pl.ds(pl.multiple_of(k * tok, tok), KEY_STEP) for k in k0[t]] for t in both]
            s, highest = {}, {}
            for j in range(number):
                for t in both:
                    keys = jnp.concatenate([block(1, k0[t][j], step), keymask[k_at[t][j], :]], axis=1)
                    s[t, j] = dot(keys, qt[0, :, q_at[t]], ((1,), (0,)))
                    m = jnp.max(s[t, j].reshape(KEY_STEP // 8, 8, QUERY_TILE), axis=0)
                    highest[t] = m if j == 0 else jnp.maximum(highest[t], m)
            e, total, out = {}, {}, {}
            for t in both:
                top = jnp.max(highest[t], axis=0, keepdims=True)
                for j in range(number):
                    e[t, j] = jnp.exp2((s[t, j] - top) * factor)
                    n = jnp.sum(e[t, j].reshape(KEY_STEP // 8, 8, QUERY_TILE), axis=0)
                    o = dot(vt[0, :, k_at[t][j]], e[t, j].astype(BF16), ((1,), (0,)))
                    total[t] = n if j == 0 else total[t] + n
                    out[t] = o if j == 0 else out[t] + o
            for t in both:
                rows = pl.ds(tiles[t] * per, per)
                inv = 1.0 / jnp.sum(total[t], axis=0, keepdims=True)
                attended = (out[t] * inv).astype(BF16)
                delta = jnp.sum(attended.astype(F32) * gt[0, :, q_at[t]].astype(F32), axis=0, keepdims=True)
                out_ref[rows, :tok, :] = attended.T.reshape(per, tok, HEAD_DIM)
                query, cot = block(0, tiles[t] * per, per), block(3, tiles[t] * per, per)
                for j in range(number):
                    prob = e[t, j] * inv
                    dprob = dot(block(2, k0[t][j], step), gt[0, :, q_at[t]], ((1,), (0,)))
                    dscore = (prob * (dprob - delta)).astype(BF16)
                    dv[0, k_at[t][j], :] += dot(prob.astype(BF16), cot, ((1,), (0,)))
                    dk[0, k_at[t][j], :] += dot(dscore, query, ((1,), (0,)))
                    d = dot(kt[0, :, k_at[t][j]], dscore, ((1,), (0,)))
                    dq = d if j == 0 else dq + d
                out_ref[rows, tok : 2 * tok, :] = (dq * scale).astype(BF16).T.reshape(per, tok, HEAD_DIM)

        for number in range(1, tokens // KEY_STEP + 1):

            @pl.when(count == number)
            def _():
                whole(number)

        return carry

    lax.fori_loop(0, tokens // QUERY_TILE // 2, pair, 0)

    hand.wait()

    def write(n):
        some = pl.ds(n * group, group)
        return pltpu.make_async_copy(out_ref.at[some], out_hbm.at[some, :SLAB, :], out_sem.at[n])

    def finish(i, sums):
        at = pl.ds(pl.multiple_of(i * tok, tok), tok)
        cosine, sine = angles[at, :HEAD_DIM], angles[at, HEAD_DIM:]
        new = []
        for h in range(local):
            dk_tile = (dk[h, at, :] * scale).astype(BF16)
            out_ref[i, h * SLAB + 2 * tok : h * SLAB + 3 * tok, :] = dk_tile
            out_ref[i, h * SLAB + 3 * tok : h * SLAB + 4 * tok, :] = dv[h, at, :].astype(BF16)

        @pl.when(lax.rem(i, group) == group - 1)
        def _():
            write(i // group).start()

        for h in range(local):
            for a, row in ((0, 1), (1, 2)):
                g = out_ref[i, h * SLAB + row * tok : h * SLAB + (row + 1) * tok, :].astype(F32)
                p = x_ref[i, h * SLAB + a * tok : h * SLAB + (a + 1) * tok, :].astype(F32)
                straight = g * p
                across = straight * cosine + g * pltpu.roll(p, HALF, 1) * sine
                plain, turned = sums[2 * h + a]
                new.append(
                    (
                        plain + jnp.sum(straight.reshape(tok // 8, 8, HEAD_DIM), axis=0),
                        turned + jnp.sum(across.reshape(tok // 8, 8, HEAD_DIM), axis=0),
                    )
                )
        return tuple(new)

    zero = jnp.zeros((8, HEAD_DIM), F32)
    sums = lax.fori_loop(0, members, finish, ((zero, zero),) * (2 * local))
    fill = [jnp.zeros((8 - 2, HEAD_DIM), F32)]
    plain, turned = (
        jnp.concatenate([jnp.sum(s[n], axis=0, keepdims=True) for s in sums] + fill, axis=0) for n in range(2)
    )
    plain = plain + pltpu.roll(plain, HALF, 1)
    turned = turned + pltpu.roll(turned, HALF, 1)
    lower = lax.broadcasted_iota(jnp.int32, plain.shape, 1) < HALF
    sums = 0.5 * (plain + jnp.where(lower, turned, -turned))
    if head > 0:
        sums = jnp.concatenate([before_ref[: 2 * head], sums[: 8 - 2 * head]], axis=0)
    sum_ref[...] = sums
    for n in range(members // group):
        write(n).wait()


def insert_kernel(sum_ref, y_hbm, out_hbm, rows_ref, sem):
    del y_hbm
    rest = sum_ref[:4]
    terms = []
    for _ in range(3):
        terms.append(rest.astype(BF16).astype(F32))
        rest = rest - terms[-1]
    rows_ref[...] = jnp.concatenate(terms + [jnp.zeros_like(rest)], axis=0).astype(BF16)
    number = rows_ref.shape[0]
    copies = [
        pltpu.make_async_copy(rows_ref, out_hbm.at[i, SLAB : SLAB + number, :], sem.at[i])
        for i in range(out_hbm.shape[0])
    ]
    for copy in copies:
        copy.start()
    for copy in copies:
        copy.wait()


def spread_copies(j, head, local, y_ref, att_hbm, gv_hbm, sem):
    tokens = att_hbm.shape[0]
    at = slice((j * local + head) * HEAD_DIM, (j * local + head + 1) * HEAD_DIM)
    return [
        pltpu.make_async_copy(y_ref.at[j, row * tokens : (row + 1) * tokens, :], ref.at[:, at], sem.at[j, a])
        for a, (ref, row) in enumerate(((att_hbm, 0), (gv_hbm, 3)))
    ]


def spread_kernel(head, local, y_ref, att_hbm, gv_hbm, sem):
    copies = []
    for j in range(y_ref.shape[0]):
        copies += spread_copies(j, head, local, y_ref, att_hbm, gv_hbm, sem)
    for copy in copies:
        copy.start()
    for copy in copies:
        copy.wait()


def receive_kernel(buckets, ya_hbm, yb_hbm, q_hbm, k_hbm, qg_hbm, kg_hbm, aside_hbm, att_in, gv_in, gq_hbm, gk_hbm, gqg_ref, gkg_ref, att_hbm, gv_hbm, ya, yb, raw, gains, aside, lift_ref, stage, small_sem, raw_sem, y_sem, spread_sem, sem):
    del att_in, gv_in
    tokens, feature = q_hbm.shape
    members = ya_hbm.shape[0]
    local = feature // members // HEAD_DIM
    groups = y_sem.shape[1]
    group = members // groups
    small = [
        pltpu.make_async_copy(source, target, small_sem.at[a])
        for a, (source, target) in enumerate(((qg_hbm, gains.at[0]), (kg_hbm, gains.at[1]), (aside_hbm, aside)))
    ]
    raws = [pltpu.make_async_copy(ref, raw.at[a], raw_sem.at[a]) for a, ref in enumerate((q_hbm, k_hbm))]

    def arrive(n):
        some = slice(n * group, (n + 1) * group)
        return [
            pltpu.make_async_copy(ya_hbm.at[some, tokens : 3 * tokens, :], ya.at[some], y_sem.at[0, n]),
            pltpu.make_async_copy(yb_hbm.at[some], yb.at[some], y_sem.at[1, n]),
        ]

    for copy in small + raws[:1]:
        copy.start()
    for n in range(groups):
        for copy in arrive(n):
            copy.start()
    raws[1].start()
    for copy in small:
        copy.wait()
    copies = []
    parts = sem.shape[1]
    width = feature // parts
    number = 2 * local
    for a, grad_hbm in enumerate((gq_hbm, gk_hbm)):
        raws[a].wait()
        total = jnp.zeros((tokens, HEAD_DIM), F32)
        for j in range(members):
            if a == 0 and j % group == 0:
                for copy in arrive(j // group):
                    copy.wait()
                for n in range(j, j + group):
                    spread = spread_copies(n, 1, local, yb, att_hbm, gv_hbm, spread_sem)
                    for copy in spread:
                        copy.start()
                    copies += spread
            for h, (y_ref, skip) in enumerate(((ya, 0), (yb, tokens))):
                at = slice((j * local + h) * HEAD_DIM, (j * local + h + 1) * HEAD_DIM)
                g = y_ref[j, skip + a * tokens : skip + (a + 1) * tokens, :].astype(F32)
                g = g * aside[0] - pltpu.roll(g, HALF, 1) * aside[1]
                lift = g * gains[a, :, at]
                lift_ref[a, :, at] = lift
                total = total + lift * (raw[a, :, at].astype(F32) * aside[2 + a])
        inner = jnp.sum(total, axis=-1, keepdims=True) / feature
        for part in range(parts):
            for block in range(part * width // HEAD_DIM, (part + 1) * width // HEAD_DIM):
                at = slice(block * HEAD_DIM, (block + 1) * HEAD_DIM)
                hat = raw[a, :, at].astype(F32) * aside[2 + a]
                stage[a, :, at] = (aside[2 + a] * (lift_ref[a, :, at] - hat * inner)).astype(BF16)
            at = slice(part * width, (part + 1) * width)
            copies.append(pltpu.make_async_copy(stage.at[a, :, at], grad_hbm.at[:, at], sem.at[a, part]))
            copies[-1].start()
    for j in range(members):
        rows = yb[j, SLAB:, :].astype(F32)
        total = rows[:number] + rows[number : 2 * number] + rows[2 * number : 3 * number]
        for h in range(local):
            at = slice((j * local + h) * HEAD_DIM, (j * local + h + 1) * HEAD_DIM)
            gqg_ref[:, at] = total[2 * h : 2 * h + 1] / (gains[0, :, at] * buckets)
            gkg_ref[:, at] = total[2 * h + 1 : 2 * h + 2] / (gains[1, :, at] * buckets)
    for copy in copies:
        copy.wait()


def on_device(q_raw, k_raw, values, grad_out, q_gain, k_gain, lengths, positions):
    members = lax.axis_size("seq")
    replicas = lax.axis_size("dp")
    _, tok, feature = q_raw.shape
    local = feature // members // HEAD_DIM
    tokens = tok * members
    vmem = pl.BlockSpec(memory_space=pltpu.VMEM)
    smem = pl.BlockSpec(memory_space=pltpu.SMEM)
    hbm = pl.BlockSpec(memory_space=pltpu.HBM)
    sems = pltpu.SemaphoreType.DMA
    table = jnp.asarray(rotary_table())
    doubled = jnp.asarray(double_table())
    shape = jax.ShapeDtypeStruct
    slabs = shape((members, SLAB, HEAD_DIM), BF16)
    longer = shape((members, SLAB + 16, HEAD_DIM), BF16)
    row_shape = shape((tok, feature), BF16)

    def send(head, aside):
        first = head == 0
        packet = longer if first else slabs
        scratch = [pltpu.VMEM((4, tok, feature), BF16), pltpu.VMEM((2, 1, feature), F32)]
        if first:
            scratch += [pltpu.VMEM((3, 1, tok), jnp.int32), pltpu.VMEM(table.shape, BF16)]
        return pl.pallas_call(
            functools.partial(send_kernel, head),
            out_shape=(packet, shape((4, tok, HEAD_DIM), F32)) if first else packet,
            in_specs=[hbm] * 8 + ([] if first else [vmem]),
            out_specs=(hbm, vmem) if first else hbm,
            scratch_shapes=scratch + [pltpu.VMEM(packet.shape, BF16), sems((4,)), sems((4,)), sems((4,))],
            compiler_params=pltpu.CompilerParams(vmem_limit_bytes=60 << 20),
            cost_estimate=pl.CostEstimate(flops=20 << 20, bytes_accessed=6 << 20, transcendentals=0),
            name="send",
        )(
            *(a[0] for a in (q_raw, k_raw, values, grad_out)),
            q_gain[None],
            k_gain[None],
            jnp.transpose(positions, (1, 0, 2)),
            table,
            *([] if first else [aside]),
        )

    def exchange(packet):
        return lax.all_to_all(packet, "seq", 0, 0, tiled=True)

    angle_shape = shape((tokens, 2 * HEAD_DIM), F32)

    def attend(head, got, *others):
        first = head == 0
        outs = (longer if head == local - 1 else slabs, shape((8, HEAD_DIM), F32))
        return pl.pallas_call(
            functools.partial(attention_kernel, head),
            out_shape=outs + ((angle_shape,) if first else ()),
            in_specs=[smem, hbm] + ([vmem] if first else [hbm, vmem]),
            out_specs=(hbm, vmem) + ((hbm,) if first else ()),
            scratch_shapes=[
                pltpu.VMEM(got.shape, BF16),
                pltpu.VMEM((members, SLAB, HEAD_DIM), BF16),
                pltpu.VMEM((1, 2 * HEAD_DIM, tokens), BF16),
                pltpu.VMEM((1, HEAD_DIM, tokens), BF16),
                pltpu.VMEM((1, HEAD_DIM, tokens), BF16),
                pltpu.VMEM((1, HEAD_DIM, tokens), BF16),
                pltpu.VMEM((tokens, HEAD_DIM), BF16),
                pltpu.VMEM((1, tokens, HEAD_DIM), F32),
                pltpu.VMEM((1, tokens, HEAD_DIM), F32),
                pltpu.VMEM(angle_shape.shape, F32),
                sems((4,)),
                sems((4,)),
                sems(()),
            ],
            compiler_params=pltpu.CompilerParams(vmem_limit_bytes=60 << 20),
            cost_estimate=pl.CostEstimate(flops=10 << 30, bytes_accessed=5 << 20, transcendentals=1 << 22),
            name="attention",
        )(lengths[0], got, *others)

    packet_a, aside = send(0, None)
    got_a = exchange(packet_a)
    packet_b = send(1, aside)
    got_b = exchange(packet_b)
    back_a, sum_a, angles = attend(0, got_a, doubled)
    y_a = exchange(back_a)
    back_b, sums = attend(1, got_b, angles, sum_a)
    for distance in (1, 2, 4):
        sums = sums + lax.ppermute(sums, "dp", [(i, i ^ distance) for i in range(replicas)])
    back_b = pl.pallas_call(
        insert_kernel,
        out_shape=longer,
        in_specs=[vmem, hbm],
        out_specs=hbm,
        scratch_shapes=[pltpu.VMEM((16, HEAD_DIM), BF16), sems((members,))],
        input_output_aliases={1: 0},
        name="insert",
    )(sums, back_b)
    y_b = exchange(back_b)
    attended, grad_v = pl.pallas_call(
        functools.partial(spread_kernel, 0, local),
        out_shape=(row_shape,) * 2,
        in_specs=[vmem],
        out_specs=(hbm, hbm),
        scratch_shapes=[sems((members, 2))],
        compiler_params=pltpu.CompilerParams(vmem_limit_bytes=24 << 20),
        cost_estimate=pl.CostEstimate(flops=0, bytes_accessed=4 << 20, transcendentals=0),
        name="receive_spread",
    )(y_a)
    grad_q, grad_k, q_sum, k_sum, attended, grad_v = pl.pallas_call(
        functools.partial(receive_kernel, replicas),
        out_shape=(row_shape, row_shape, shape((1, feature), F32), shape((1, feature), F32), row_shape, row_shape),
        in_specs=[hbm] * 9,
        out_specs=(hbm, hbm, vmem, vmem, hbm, hbm),
        scratch_shapes=[
            pltpu.VMEM((members, 2 * tok, HEAD_DIM), BF16),
            pltpu.VMEM(longer.shape, BF16),
            pltpu.VMEM((2, tok, feature), BF16),
            pltpu.VMEM((2, 1, feature), F32),
            pltpu.VMEM((4, tok, HEAD_DIM), F32),
            pltpu.VMEM((2, tok, feature), F32),
            pltpu.VMEM((2, tok, feature), BF16),
            sems((3,)),
            sems((2,)),
            sems((2, 4)),
            sems((members, 2)),
            sems((2, 4)),
        ],
        input_output_aliases={7: 4, 8: 5},
        compiler_params=pltpu.CompilerParams(vmem_limit_bytes=60 << 20),
        cost_estimate=pl.CostEstimate(flops=40 << 20, bytes_accessed=8 << 20, transcendentals=0),
        name="receive",
    )(y_a, y_b, q_raw[0], k_raw[0], q_gain[None], k_gain[None], aside, attended, grad_v)
    return tuple(o[None] for o in (attended, grad_q, grad_k, grad_v)) + (q_sum[0], k_sum[0])


def solution(mesh):
    tokens_split = P("dp", "seq", None)
    return jax.shard_map(
        on_device,
        mesh=mesh,
        in_specs=(tokens_split,) * 4 + (P(), P(), P("dp", None), P("dp", None, "seq")),
        out_specs=(tokens_split,) * 4 + (P(), P()),
        check_vma=False,
    )
```

time: 161 us -> 156 us (0.969)
  blocking collectives: 115 us -> 0 us
  waiting for transfers between devices: 0.9 us -> 68.7 us
  starting transfers between devices: 4.68 us -> 28.9 us
  Pallas kernels: 39.1 us -> 54.1 us
    all_to_all x2 -> x0, blocking collectives: 115 us -> none  [the longest x1 60.5 us: on_device(): got = lax.all_to_all(packet, 'seq', 0, 0, tiled=True)]
    all_to_all x0 -> x4, waiting for transfers between devices: none -> 63.4 us  [exchange(): return lax.all_to_all(packet, 'seq', 0, 0, tiled=True)]
    all_to_all x0 -> x4, starting transfers between devices: none -> 23.7 us  [exchange(): return lax.all_to_all(packet, 'seq', 0, 0, tiled=True)]
    pallas_call x5 -> x7, Pallas kernels: 39.1 us -> 54.1 us  [the longest x2 34.2 us: attend(): pl.pallas_call(functools.partial(attention_kernel, head), out_shape=outs...]
    ppermute x3, waiting for transfers between devices: 0.9 us -> 5.22 us  [on_device(): lax.ppermute(sums, 'dp', [(i, i ^ distance) for i in range(replicas)])]
  transfers between devices with their start and end apart: 3 -> 7, of which waited for: 1 -> 6; matrix products, arithmetic and copies ran while one was open for 0% -> 1% of each run, Pallas kernels for 4% -> 24%
where the time goes in v3:
time: 156 us; the launch traced here: 155 us
  waiting for transfers between devices  68.7 us (44%)
  Pallas kernels  54.1 us (35%)
  starting transfers between devices  28.9 us (19%)
    all_to_all x4, waiting for transfers between devices, exchange(): return lax.all_to_all(packet, 'seq', 0, 0, tiled=True)  63.4 us
    pallas_call x2, Pallas kernels, attend(): pl.pallas_call(functools.partial(attention_kernel, head), out_shape=outs...  34.2 us
    all_to_all x4, starting transfers between devices, exchange(): return lax.all_to_all(packet, 'seq', 0, 0, tiled=True)  23.7 us
    pallas_call x2, Pallas kernels, send(): pl.pallas_call(functools.partial(send_kernel, head), out_shape=(packet, s...  10.2 us
    pallas_call x1, Pallas kernels, on_device(): pl.pallas_call(functools.partial(receive_kernel, replicas), out_shape=(ro...  6.99 us
    ppermute x3, waiting for transfers between devices, on_device(): lax.ppermute(sums, 'dp', [(i, i ^ distance) for i in range(replicas)])  5.22 us
    ppermute x3, starting transfers between devices, on_device(): lax.ppermute(sums, 'dp', [(i, i ^ distance) for i in range(replicas)])  5.13 us
  transfers between devices with their start and end apart: 7, of which 6 were waited for; matrix products, arithmetic and copies ran while one was open for 1% of the time, Pallas kernels for 24%

profile of v3, /device:TPU:0, one launch (start us, length us, event | category | flops | bytes accessed | tf_op | source)
XLA Modules:
  0.0 155.2 jit_solution(12245645927163602940)
XLA Ops:
  0.6 5.3 %send.2 = (bf16[16,528,128]{2,1,0:T(8,128)(2,1)}, f32[4,128,128]{2,1,0:T(8,128)}) custom-call(bf16[128,4096]{1,0:T(8,128)(2,1)} %bitcast.14, bf16[128,4096]{1,0:T(8,128)(2,1)} %bitcast.17, bf16[128,4096]{1,0:T(8,128)(2,1)} %bitcast.20, bf16[128,4096]{1,0:T(8,128)(2,1)} %bitcast.22, f32[1,4096]{1,0:T(1,128)} %bitcast.26, f32[1,4096]{1,0:T(1,128)} %bitcast.29, ...), custom_call_target="tpu_custom_call" | custom-call | flops 20971520 | bytes 6291456 | tf_op jit(solution)/shard_map/send/pallas_call | solution.py:457
  5.9 8.2 %all-to-all-start = ((bf16[16,528,128]{2,1,0:T(8,128)(2,1)}), bf16[16,528,128]{2,1,0:T(8,128)(2,1)}, u32[]{:S(2)}, u32[]{:S(2)}) async-start(bf16[16,528,128]{2,1,0:T(8,128)(2,1)} %get-tuple-element.21), calls=%async_computation | async-start | bytes 4325376 | tf_op jit(solution)/shard_map/all_to_all | solution.py:476
  14.1 4.9 %send.3 = bf16[16,512,128]{2,1,0:T(8,128)(2,1)} custom-call(bf16[128,4096]{1,0:T(8,128)(2,1)} %bitcast.15, bf16[128,4096]{1,0:T(8,128)(2,1)} %bitcast.18, bf16[128,4096]{1,0:T(8,128)(2,1)} %bitcast.21, bf16[128,4096]{1,0:T(8,128)(2,1)} %bitcast.23, f32[1,4096]{1,0:T(1,128)} %bitcast.27, f32[1,4096]{1,0:T(1,128)} %bitcast.30, s32[3,1,128]{2,1,0:T(1,128)} %bitcast.33, ...), custom_call_target="tpu_custom_call" | custom-call | flops 20971520 | bytes 6291456 | tf_op jit(solution)/shard_map/send/pallas_call | solution.py:457
  19.0 26.3 %all-to-all-done.x_hbm = bf16[16,528,128]{2,1,0:T(8,128)(2,1)} async-done(((bf16[16,528,128]{2,1,0:T(8,128)(2,1)}), bf16[16,528,128]{2,1,0:T(8,128)(2,1)}, u32[]{:S(2)}, u32[]{:S(2)}) %all-to-all-start) | async-done | bytes 2162720 | tf_op jit(solution)/shard_map/all_to_all | solution.py:476
  45.4 3.9 %all-to-all-start.2 = ((bf16[16,512,128]{2,1,0:T(8,128)(2,1)}), bf16[16,512,128]{2,1,0:T(8,128)(2,1)S(1)}, u32[]{:S(2)}, u32[]{:S(2)}) async-start(bf16[16,512,128]{2,1,0:T(8,128)(2,1)} %send.3), calls=%async_computation.2 | async-start | bytes 4194304 | tf_op jit(solution)/shard_map/all_to_all | solution.py:476
  49.3 18.3 %attention.2 = (bf16[16,512,128]{2,1,0:T(8,128)(2,1)}, f32[8,128]{1,0:T(8,128)}, f32[2048,256]{1,0:T(8,128)}) custom-call(s32[6]{0:T(128)} %bitcast.38, bf16[16,528,128]{2,1,0:T(8,128)(2,1)} %all-to-all-done.x_hbm, bf16[192,512]{1,0:T(8,128)(2,1)} %constant.5.clone.rest_0_), custom_call_target="tpu_custom_call" | custom-call | flops 10737418240 | bytes 5242880 | tf_op jit(solution)/shard_map/attention/pallas_call | solution.py:483
  67.6 9.2 %all-to-all-done.2.x_hbm = bf16[16,512,128]{2,1,0:T(8,128)(2,1)S(1)} async-done(((bf16[16,512,128]{2,1,0:T(8,128)(2,1)}), bf16[16,512,128]{2,1,0:T(8,128)(2,1)S(1)}, u32[]{:S(2)}, u32[]{:S(2)}) %all-to-all-start.2) | async-done | bytes 2097184 | tf_op jit(solution)/shard_map/all_to_all | solution.py:476
  76.8 0.0 copy-start.1
  76.8 1.3 copy-done.1
  78.1 4.4 %all-to-all-start.1 = ((bf16[16,512,128]{2,1,0:T(8,128)(2,1)}), bf16[16,512,128]{2,1,0:T(8,128)(2,1)S(1)}, u32[]{:S(2)}, u32[]{:S(2)}) async-start(bf16[16,512,128]{2,1,0:T(8,128)(2,1)} %get-tuple-element.22), calls=%async_computation.1 | async-start | bytes 4194304 | tf_op jit(solution)/shard_map/all_to_all | solution.py:476
  82.5 16.0 %attention.3 = (bf16[16,528,128]{2,1,0:T(8,128)(2,1)}, f32[8,128]{1,0:T(8,128)}) custom-call(s32[6]{0:T(128)} %bitcast.39, bf16[16,512,128]{2,1,0:T(8,128)(2,1)} %copy-done.1, f32[2048,256]{1,0:T(8,128)} %get-tuple-element.24.rest_0_, f32[8,128]{1,0:T(8,128)} %get-tuple-element.25.rest_1_), custom_call_target="tpu_custom_call" | custom-call | flops 10737418240 | bytes 5242880 | tf_op jit(solution)/shard_map/attention/pallas_call | solution.py:483
  98.4 0.1 collective-permute-start
  98.5 1.4 collective-permute-done
  99.9 0.7 add.9
  100.6 2.2 %collective-permute-start.1 = (f32[8,128]{1,0:T(8,128)S(1)}, f32[8,128]{1,0:T(8,128)S(1)}, u32[]{:S(2)}, u32[]{:S(2)}) collective-permute-start(f32[8,128]{1,0:T(8,128)S(1)} %add.9), channel_id=1, source_target_pairs={{0,32},{16,48},{32,0},{48,16},{64,96},{80,112},{96,64},{112,80},{1... | collective-permute-start | bytes 12296 | tf_op jit(solution)/shard_map/ppermute | solution.py:516
  102.8 1.6 %collective-permute-done.1 = f32[8,128]{1,0:T(8,128)S(1)} collective-permute-done((f32[8,128]{1,0:T(8,128)S(1)}, f32[8,128]{1,0:T(8,128)S(1)}, u32[]{:S(2)}, u32[]{:S(2)}) %collective-permute-start.1) | collective-permute-done | bytes 4128 | tf_op jit(solution)/shard_map/ppermute | solution.py:516
  104.4 2.8 %collective-permute-start.2 = (f32[8,128]{1,0:T(8,128)S(1)}, f32[8,128]{1,0:T(8,128)S(1)}, u32[]{:S(2)}, u32[]{:S(2)}) collective-permute-start(f32[8,128]{1,0:T(8,128)S(1)} %add.10), channel_id=1, source_target_pairs={{0,64},{16,80},{32,96},{48,112},{64,0},{80,16},{96,32},{112,48},{1... | collective-permute-start | bytes 12296 | tf_op jit(solution)/shard_map/ppermute | solution.py:516
  107.2 2.3 %collective-permute-done.2 = f32[8,128]{1,0:T(8,128)S(1)} collective-permute-done((f32[8,128]{1,0:T(8,128)S(1)}, f32[8,128]{1,0:T(8,128)S(1)}, u32[]{:S(2)}, u32[]{:S(2)}) %collective-permute-start.2) | collective-permute-done | bytes 4128 | tf_op jit(solution)/shard_map/ppermute | solution.py:516
  109.5 0.6 add.11.sum_ref
  110.1 1.5 insert.1
  111.6 0.0 all-to-all-done.1.y_ref.ya_hbm
  111.6 0.0 copy-start
  111.6 7.3 %all-to-all-start.3 = ((bf16[16,528,128]{2,1,0:T(8,128)(2,1)}), bf16[16,528,128]{2,1,0:T(8,128)(2,1)}, u32[]{:S(2)}, u32[]{:S(2)}) async-start(bf16[16,528,128]{2,1,0:T(8,128)(2,1)} %insert.1), calls=%async_computation.3 | async-start | bytes 4325376 | tf_op jit(solution)/shard_map/all_to_all | solution.py:476
  118.9 0.0 copy-done
  118.9 1.2 receive_spread.1
  120.1 27.9 %all-to-all-done.3.yb_hbm = bf16[16,528,128]{2,1,0:T(8,128)(2,1)} async-done(((bf16[16,528,128]{2,1,0:T(8,128)(2,1)}), bf16[16,528,128]{2,1,0:T(8,128)(2,1)}, u32[]{:S(2)}, u32[]{:S(2)}) %all-to-all-start.3) | async-done | bytes 2162720 | tf_op jit(solution)/shard_map/all_to_all | solution.py:476
  148.0 7.0 %receive.1 = (bf16[128,4096]{1,0:T(8,128)(2,1)}, bf16[128,4096]{1,0:T(8,128)(2,1)}, f32[1,4096]{1,0:T(1,128)}, f32[1,4096]{1,0:T(1,128)}, bf16[128,4096]{1,0:T(8,128)(2,1)}, /*index=5*/bf16[128,4096]{1,0:T(8,128)(2,1)}) custom-call(bf16[16,512,128]{2,1,0:T(8,128)(2,1)} %copy-done, ...), custom_call_target="tpu_custom_call", output_to_operand_aliasing={{4}: (7, {}), {5}: (8, {})} | custom-call | flops 41943040 | bytes 8388608 | tf_op jit(solution)/shard_map/receive/pallas_call | solution.py:537
  (1 shorter events, 0.0 us)
Async XLA Ops:
  5.9 39.5 %all-to-all-start = ((bf16[16,528,128]{2,1,0:T(8,128)(2,1)}), bf16[16,528,128]{2,1,0:T(8,128)(2,1)}, u32[]{:S(2)}, u32[]{:S(2)}) async-start(bf16[16,528,128]{2,1,0:T(8,128)(2,1)} %get-tuple-element.21), calls=%async_computation | async-start | bytes 4325376 | tf_op jit(solution)/shard_map/all_to_all | solution.py:476
  45.4 31.4 %all-to-all-start.2 = ((bf16[16,512,128]{2,1,0:T(8,128)(2,1)}), bf16[16,512,128]{2,1,0:T(8,128)(2,1)S(1)}, u32[]{:S(2)}, u32[]{:S(2)}) async-start(bf16[16,512,128]{2,1,0:T(8,128)(2,1)} %send.3), calls=%async_computation.2 | async-start | bytes 4194304 | tf_op jit(solution)/shard_map/all_to_all | solution.py:476
  76.8 1.3 copy-start.1
  78.1 33.5 %all-to-all-start.1 = ((bf16[16,512,128]{2,1,0:T(8,128)(2,1)}), bf16[16,512,128]{2,1,0:T(8,128)(2,1)S(1)}, u32[]{:S(2)}, u32[]{:S(2)}) async-start(bf16[16,512,128]{2,1,0:T(8,128)(2,1)} %get-tuple-element.22), calls=%async_computation.1 | async-start | bytes 4194304 | tf_op jit(solution)/shard_map/all_to_all | solution.py:476
  98.4 1.5 collective-permute-start
  100.6 3.8 %collective-permute-start.1 = (f32[8,128]{1,0:T(8,128)S(1)}, f32[8,128]{1,0:T(8,128)S(1)}, u32[]{:S(2)}, u32[]{:S(2)}) collective-permute-start(f32[8,128]{1,0:T(8,128)S(1)} %add.9), channel_id=1, source_target_pairs={{0,32},{16,48},{32,0},{48,16},{64,96},{80,112},{96,64},{112,80},{1... | collective-permute-start | bytes 12296 | tf_op jit(solution)/shard_map/ppermute | solution.py:516
  104.4 5.1 %collective-permute-start.2 = (f32[8,128]{1,0:T(8,128)S(1)}, f32[8,128]{1,0:T(8,128)S(1)}, u32[]{:S(2)}, u32[]{:S(2)}) collective-permute-start(f32[8,128]{1,0:T(8,128)S(1)} %add.10), channel_id=1, source_target_pairs={{0,64},{16,80},{32,96},{48,112},{64,0},{80,16},{96,32},{112,48},{1... | collective-permute-start | bytes 12296 | tf_op jit(solution)/shard_map/ppermute | solution.py:516
  111.6 7.3 %copy-start = (bf16[16,512,128]{2,1,0:T(8,128)(2,1)}, bf16[16,512,128]{2,1,0:T(8,128)(2,1)S(1)}, u32[]{:S(2)}) copy-start(bf16[16,512,128]{2,1,0:T(8,128)(2,1)S(1)} %all-to-all-done.1.y_ref.ya_hbm) | copy-start | bytes 6291460
  111.6 36.4 %all-to-all-start.3 = ((bf16[16,528,128]{2,1,0:T(8,128)(2,1)}), bf16[16,528,128]{2,1,0:T(8,128)(2,1)}, u32[]{:S(2)}, u32[]{:S(2)}) async-start(bf16[16,528,128]{2,1,0:T(8,128)(2,1)} %insert.1), calls=%async_computation.3 | async-start | bytes 4325376 | tf_op jit(solution)/shard_map/all_to_all | solution.py:476

commit v4 on v3

--- a/solution.py
+++ b/solution.py
@@ -132,12 +132,12 @@
         copy.wait()
 
 
-def attention_kernel(head, len_ref, x_hbm, *rest):
+def attention_kernel(head, len_ref, x_ref, *rest):
     if head == 0:
         table_ref, out_hbm, sum_ref, angles_hbm, *rest = rest
     else:
         angles_hbm, before_ref, out_hbm, sum_ref, *rest = rest
-    x_ref, out_ref, qt, kt, vt, gt, keymask, dk, dv, angles, in_sem, out_sem, angle_sem = rest
+    out_ref, qt, kt, vt, gt, keymask, dk, dv, angles, out_sem, angle_sem = rest
     members = x_ref.shape[0]
     tok = HEAD_DIM
     tokens = members * tok
@@ -146,14 +146,7 @@
     scale = HEAD_DIM ** (-0.5)
     factor = scale * math.log2(math.e)
 
-    group = members // in_sem.shape[0]
-
-    def read(n):
-        some = pl.ds(n * group, group)
-        return pltpu.make_async_copy(x_hbm.at[some], x_ref.at[some], in_sem.at[n])
-
-    for n in range(members // group):
-        read(n).start()
+    group = members // out_sem.shape[0]
     if head == 0:
         hand = pltpu.make_async_copy(angles, angles_hbm, angle_sem)
     else:
@@ -180,11 +173,6 @@
         for c in range(clips):
             clip = clip + (token >= ends[c]).astype(jnp.int32)
         apart = jnp.where(clip == lane, 0.0, 1.0).astype(BF16)
-
-        @pl.when(lax.rem(i, group) == 0)
-        def _():
-            read(i // group).wait()
-
         if head == 0:
             rows = x_ref[i, SLAB:, :].astype(F32)
             terms = dot(picks_of([rows[a : a + 1] for a in range(3)]), table_ref[...], ((0,), (0,)))
@@ -350,42 +338,52 @@
     ]
 
 
-def spread_kernel(head, local, y_ref, att_hbm, gv_hbm, sem):
+def early_kernel(local, y_ref, q_ref, k_ref, qg_ref, kg_ref, aside_ref, att_hbm, gv_hbm, lift_hbm, total_ref, lift_ref, spread_sem, lift_sem):
+    tokens = q_ref.shape[0]
+    members = y_ref.shape[0]
     copies = []
-    for j in range(y_ref.shape[0]):
-        copies += spread_copies(j, head, local, y_ref, att_hbm, gv_hbm, sem)
+    for j in range(members):
+        copies += spread_copies(j, 0, local, y_ref, att_hbm, gv_hbm, spread_sem)
     for copy in copies:
         copy.start()
+    for a, (raw_ref, gain_ref) in enumerate(((q_ref, qg_ref), (k_ref, kg_ref))):
+        total = jnp.zeros((tokens, HEAD_DIM), F32)
+        for j in range(members):
+            at = slice(j * local * HEAD_DIM, (j * local + 1) * HEAD_DIM)
+            g = y_ref[j, (a + 1) * tokens : (a + 2) * tokens, :].astype(F32)
+            g = g * aside_ref[0] - pltpu.roll(g, HALF, 1) * aside_ref[1]
+            lift = g * gain_ref[:, at]
+            lift_ref[a, :, j * HEAD_DIM : (j + 1) * HEAD_DIM] = lift
+            total = total + lift * (raw_ref[:, at].astype(F32) * aside_ref[2 + a])
+        total_ref[a] = total
+        copies.append(pltpu.make_async_copy(lift_ref.at[a], lift_hbm.at[a], lift_sem.at[a]))
+        copies[-1].start()
     for copy in copies:
         copy.wait()
 
 
-def receive_kernel(buckets, ya_hbm, yb_hbm, q_hbm, k_hbm, qg_hbm, kg_hbm, aside_hbm, att_in, gv_in, gq_hbm, gk_hbm, gqg_ref, gkg_ref, att_hbm, gv_hbm, ya, yb, raw, gains, aside, lift_ref, stage, small_sem, raw_sem, y_sem, spread_sem, sem):
+def receive_kernel(buckets, yb_hbm, q_hbm, k_hbm, qg_hbm, kg_hbm, aside_hbm, lift_hbm, total_hbm, att_in, gv_in, gq_hbm, gk_hbm, gqg_ref, gkg_ref, att_hbm, gv_hbm, yb, raw, gains, aside, before, totals, lift_ref, stage, small_sem, raw_sem, lift_sem, y_sem, spread_sem, sem):
     del att_in, gv_in
     tokens, feature = q_hbm.shape
-    members = ya_hbm.shape[0]
+    members = yb_hbm.shape[0]
     local = feature // members // HEAD_DIM
-    groups = y_sem.shape[1]
+    groups = y_sem.shape[0]
     group = members // groups
-    small = [
-        pltpu.make_async_copy(source, target, small_sem.at[a])
-        for a, (source, target) in enumerate(((qg_hbm, gains.at[0]), (kg_hbm, gains.at[1]), (aside_hbm, aside)))
-    ]
+    sources = ((aside_hbm, aside), (total_hbm, totals), (qg_hbm, gains.at[0]), (kg_hbm, gains.at[1]))
+    small = [pltpu.make_async_copy(source, target, small_sem.at[a]) for a, (source, target) in enumerate(sources)]
     raws = [pltpu.make_async_copy(ref, raw.at[a], raw_sem.at[a]) for a, ref in enumerate((q_hbm, k_hbm))]
+    lifts = [pltpu.make_async_copy(lift_hbm.at[a], before.at[a], lift_sem.at[a]) for a in range(2)]
 
     def arrive(n):
         some = slice(n * group, (n + 1) * group)
-        return [
-            pltpu.make_async_copy(ya_hbm.at[some, tokens : 3 * tokens, :], ya.at[some], y_sem.at[0, n]),
-            pltpu.make_async_copy(yb_hbm.at[some], yb.at[some], y_sem.at[1, n]),
-        ]
+        return pltpu.make_async_copy(yb_hbm.at[some], yb.at[some], y_sem.at[n])
 
     for copy in small + raws[:1]:
         copy.start()
     for n in range(groups):
-        for copy in arrive(n):
-            copy.start()
-    raws[1].start()
+        arrive(n).start()
+    for copy in lifts[:1] + raws[1:] + lifts[1:]:
+        copy.start()
     for copy in small:
         copy.wait()
     copies = []
@@ -394,29 +392,30 @@
     number = 2 * local
     for a, grad_hbm in enumerate((gq_hbm, gk_hbm)):
         raws[a].wait()
-        total = jnp.zeros((tokens, HEAD_DIM), F32)
+        total = totals[a]
         for j in range(members):
             if a == 0 and j % group == 0:
-                for copy in arrive(j // group):
-                    copy.wait()
+                arrive(j // group).wait()
                 for n in range(j, j + group):
                     spread = spread_copies(n, 1, local, yb, att_hbm, gv_hbm, spread_sem)
                     for copy in spread:
                         copy.start()
                     copies += spread
-            for h, (y_ref, skip) in enumerate(((ya, 0), (yb, tokens))):
-                at = slice((j * local + h) * HEAD_DIM, (j * local + h + 1) * HEAD_DIM)
-                g = y_ref[j, skip + a * tokens : skip + (a + 1) * tokens, :].astype(F32)
-                g = g * aside[0] - pltpu.roll(g, HALF, 1) * aside[1]
-                lift = g * gains[a, :, at]
-                lift_ref[a, :, at] = lift
-                total = total + lift * (raw[a, :, at].astype(F32) * aside[2 + a])
+            at = slice((j * local + 1) * HEAD_DIM, (j * local + 2) * HEAD_DIM)
+            g = yb[j, (a + 1) * tokens : (a + 2) * tokens, :].astype(F32)
+            g = g * aside[0] - pltpu.roll(g, HALF, 1) * aside[1]
+            lift = g * gains[a, :, at]
+            lift_ref[a, :, j * HEAD_DIM : (j + 1) * HEAD_DIM] = lift
+            total = total + lift * (raw[a, :, at].astype(F32) * aside[2 + a])
         inner = jnp.sum(total, axis=-1, keepdims=True) / feature
+        lean = jnp.broadcast_to(inner, (tokens, HEAD_DIM)) * aside[2 + a]
+        lifts[a].wait()
         for part in range(parts):
             for block in range(part * width // HEAD_DIM, (part + 1) * width // HEAD_DIM):
                 at = slice(block * HEAD_DIM, (block + 1) * HEAD_DIM)
-                hat = raw[a, :, at].astype(F32) * aside[2 + a]
-                stage[a, :, at] = (aside[2 + a] * (lift_ref[a, :, at] - hat * inner)).astype(BF16)
+                j, h = divmod(block, local)
+                lift = (before, lift_ref)[h][a, :, j * HEAD_DIM : (j + 1) * HEAD_DIM]
+                stage[a, :, at] = (aside[2 + a] * (lift - raw[a, :, at].astype(F32) * lean)).astype(BF16)
             at = slice(part * width, (part + 1) * width)
             copies.append(pltpu.make_async_copy(stage.at[a, :, at], grad_hbm.at[:, at], sem.at[a, part]))
             copies[-1].start()
@@ -483,10 +482,9 @@
         return pl.pallas_call(
             functools.partial(attention_kernel, head),
             out_shape=outs + ((angle_shape,) if first else ()),
-            in_specs=[smem, hbm] + ([vmem] if first else [hbm, vmem]),
+            in_specs=[smem, vmem] + ([vmem] if first else [hbm, vmem]),
             out_specs=(hbm, vmem) + ((hbm,) if first else ()),
             scratch_shapes=[
-                pltpu.VMEM(got.shape, BF16),
                 pltpu.VMEM((members, SLAB, HEAD_DIM), BF16),
                 pltpu.VMEM((1, 2 * HEAD_DIM, tokens), BF16),
                 pltpu.VMEM((1, HEAD_DIM, tokens), BF16),
@@ -497,10 +495,9 @@
                 pltpu.VMEM((1, tokens, HEAD_DIM), F32),
                 pltpu.VMEM(angle_shape.shape, F32),
                 sems((4,)),
-                sems((4,)),
                 sems(()),
             ],
-            compiler_params=pltpu.CompilerParams(vmem_limit_bytes=60 << 20),
+            compiler_params=pltpu.CompilerParams(vmem_limit_bytes=50 << 20),
             cost_estimate=pl.CostEstimate(flops=10 << 30, bytes_accessed=5 << 20, transcendentals=1 << 22),
             name="attention",
         )(lengths[0], got, *others)
@@ -524,40 +521,44 @@
         name="insert",
     )(sums, back_b)
     y_b = exchange(back_b)
-    attended, grad_v = pl.pallas_call(
-        functools.partial(spread_kernel, 0, local),
-        out_shape=(row_shape,) * 2,
-        in_specs=[vmem],
-        out_specs=(hbm, hbm),
-        scratch_shapes=[sems((members, 2))],
+    half_shape = shape((2, tok, feature // local), F32)
+    total_shape = shape((2, tok, HEAD_DIM), F32)
+    attended, grad_v, lift, totals = pl.pallas_call(
+        functools.partial(early_kernel, local),
+        out_shape=(row_shape, row_shape, half_shape, total_shape),
+        in_specs=[vmem] * 6,
+        out_specs=(hbm, hbm, hbm, vmem),
+        scratch_shapes=[pltpu.VMEM(half_shape.shape, F32), sems((members, 2)), sems((2,))],
         compiler_params=pltpu.CompilerParams(vmem_limit_bytes=24 << 20),
-        cost_estimate=pl.CostEstimate(flops=0, bytes_accessed=4 << 20, transcendentals=0),
-        name="receive_spread",
-    )(y_a)
+        cost_estimate=pl.CostEstimate(flops=20 << 20, bytes_accessed=6 << 20, transcendentals=0),
+        name="early",
+    )(y_a, q_raw[0], k_raw[0], q_gain[None], k_gain[None], aside)
     grad_q, grad_k, q_sum, k_sum, attended, grad_v = pl.pallas_call(
         functools.partial(receive_kernel, replicas),
         out_shape=(row_shape, row_shape, shape((1, feature), F32), shape((1, feature), F32), row_shape, row_shape),
-        in_specs=[hbm] * 9,
+        in_specs=[hbm] * 10,
         out_specs=(hbm, hbm, vmem, vmem, hbm, hbm),
         scratch_shapes=[
-            pltpu.VMEM((members, 2 * tok, HEAD_DIM), BF16),
             pltpu.VMEM(longer.shape, BF16),
             pltpu.VMEM((2, tok, feature), BF16),
             pltpu.VMEM((2, 1, feature), F32),
             pltpu.VMEM((4, tok, HEAD_DIM), F32),
-            pltpu.VMEM((2, tok, feature), F32),
+            pltpu.VMEM(half_shape.shape, F32),
+            pltpu.VMEM(total_shape.shape, F32),
+            pltpu.VMEM(half_shape.shape, F32),
             pltpu.VMEM((2, tok, feature), BF16),
-            sems((3,)),
+            sems((4,)),
             sems((2,)),
-            sems((2, 4)),
+            sems((2,)),
+            sems((4,)),
             sems((members, 2)),
             sems((2, 4)),
         ],
-        input_output_aliases={7: 4, 8: 5},
+        input_output_aliases={8: 4, 9: 5},
         compiler_params=pltpu.CompilerParams(vmem_limit_bytes=60 << 20),
         cost_estimate=pl.CostEstimate(flops=40 << 20, bytes_accessed=8 << 20, transcendentals=0),
         name="receive",
-    )(y_a, y_b, q_raw[0], k_raw[0], q_gain[None], k_gain[None], aside, attended, grad_v)
+    )(y_b, q_raw[0], k_raw[0], q_gain[None], k_gain[None], aside, lift, totals, attended, grad_v)
     return tuple(o[None] for o in (attended, grad_q, grad_k, grad_v)) + (q_sum[0], k_sum[0])
 
 

time: 156 us -> 151 us (0.968)
  Pallas kernels: 54.1 us -> 51.1 us
  starting transfers between devices: 28.9 us -> 26.7 us
    pallas_call x2, Pallas kernels: 34.2 us -> 30.8 us  [attend(): pl.pallas_call(functools.partial(attention_kernel, head), out_shape=outs...]
    pallas_call x1, Pallas kernels: 1.23 us -> 2.85 us  [on_device(): pl.pallas_call(functools.partial(early_kernel, local), out_shape=(row_sha...]
  transfers between devices with their start and end apart: 7 -> 7, of which waited for: 6 -> 7; matrix products, arithmetic and copies ran while one was open for 1% -> 0% of each run, Pallas kernels for 24% -> 23%
where the time goes in v4:
time: 151 us; the launch traced here: 150 us
  waiting for transfers between devices  68.5 us (45%)
  Pallas kernels  51.1 us (34%)
  starting transfers between devices  26.7 us (18%)
  local copies, waits for them, and re-layouts  2.02 us (1%)
    all_to_all x4, waiting for transfers between devices, exchange(): return lax.all_to_all(packet, 'seq', 0, 0, tiled=True)  62.8 us
    pallas_call x2, Pallas kernels, attend(): pl.pallas_call(functools.partial(attention_kernel, head), out_shape=outs...  30.8 us
    all_to_all x4, starting transfers between devices, exchange(): return lax.all_to_all(packet, 'seq', 0, 0, tiled=True)  22.2 us
    pallas_call x2, Pallas kernels, send(): pl.pallas_call(functools.partial(send_kernel, head), out_shape=(packet, s...  10.3 us
    ppermute x3, waiting for transfers between devices, on_device(): lax.ppermute(sums, 'dp', [(i, i ^ distance) for i in range(replicas)])  5.74 us
    pallas_call x1, Pallas kernels, on_device(): pl.pallas_call(functools.partial(receive_kernel, replicas), out_shape=(ro...  5.72 us
    ppermute x3, starting transfers between devices, on_device(): lax.ppermute(sums, 'dp', [(i, i ^ distance) for i in range(replicas)])  4.45 us
  transfers between devices with their start and end apart: 7, of which 7 were waited for; matrix products, arithmetic and copies ran while one was open for 0% of the time, Pallas kernels for 23%

profile of v4, /device:TPU:0, one launch (start us, length us, event | category | flops | bytes accessed | tf_op | source)
XLA Modules:
  0.0 150.0 jit_solution(7199265402367406189)
XLA Ops:
  0.6 5.4 %send.2 = (bf16[16,528,128]{2,1,0:T(8,128)(2,1)}, f32[4,128,128]{2,1,0:T(8,128)}) custom-call(bf16[128,4096]{1,0:T(8,128)(2,1)} %bitcast.14, bf16[128,4096]{1,0:T(8,128)(2,1)} %bitcast.18, bf16[128,4096]{1,0:T(8,128)(2,1)} %bitcast.32, bf16[128,4096]{1,0:T(8,128)(2,1)} %bitcast.34, f32[1,4096]{1,0:T(1,128)} %bitcast.22, f32[1,4096]{1,0:T(1,128)} %bitcast.26, ...), custom_call_target="tpu_custom_call" | custom-call | flops 20971520 | bytes 6291456 | tf_op jit(solution)/shard_map/send/pallas_call | solution.py:456
  6.0 8.2 %all-to-all-start.1 = ((bf16[16,528,128]{2,1,0:T(8,128)(2,1)}), bf16[16,528,128]{2,1,0:T(8,128)(2,1)}, u32[]{:S(2)}, u32[]{:S(2)}) async-start(bf16[16,528,128]{2,1,0:T(8,128)(2,1)} %get-tuple-element.24), calls=%async_computation.1 | async-start | bytes 4325376 | tf_op jit(solution)/shard_map/all_to_all | solution.py:475
  14.2 4.9 %send.3 = bf16[16,512,128]{2,1,0:T(8,128)(2,1)} custom-call(bf16[128,4096]{1,0:T(8,128)(2,1)} %bitcast.15, bf16[128,4096]{1,0:T(8,128)(2,1)} %bitcast.19, bf16[128,4096]{1,0:T(8,128)(2,1)} %bitcast.33, bf16[128,4096]{1,0:T(8,128)(2,1)} %bitcast.35, f32[1,4096]{1,0:T(1,128)} %bitcast.23, f32[1,4096]{1,0:T(1,128)} %bitcast.27, s32[3,1,128]{2,1,0:T(1,128)} %bitcast.39, ...), custom_call_target="tpu_custom_call" | custom-call | flops 20971520 | bytes 6291456 | tf_op jit(solution)/shard_map/send/pallas_call | solution.py:456
  19.1 0.0 copy-start.7
  19.1 0.0 copy-start.8
  19.2 26.3 %all-to-all-done.1.x_ref = bf16[16,528,128]{2,1,0:T(8,128)(2,1)} async-done(((bf16[16,528,128]{2,1,0:T(8,128)(2,1)}), bf16[16,528,128]{2,1,0:T(8,128)(2,1)}, u32[]{:S(2)}, u32[]{:S(2)}) %all-to-all-start.1) | async-done | bytes 2162720 | tf_op jit(solution)/shard_map/all_to_all | solution.py:475
  45.5 3.9 %all-to-all-start = ((bf16[16,512,128]{2,1,0:T(8,128)(2,1)}), bf16[16,512,128]{2,1,0:T(8,128)(2,1)S(1)}, u32[]{:S(2)}, u32[]{:S(2)}) async-start(bf16[16,512,128]{2,1,0:T(8,128)(2,1)} %send.3), calls=%async_computation | async-start | bytes 4194304 | tf_op jit(solution)/shard_map/all_to_all | solution.py:475
  49.4 0.0 copy-done.7
  49.4 0.0 copy-done.8
  49.4 17.2 %attention.2 = (bf16[16,512,128]{2,1,0:T(8,128)(2,1)}, f32[8,128]{1,0:T(8,128)S(1)}, f32[2048,256]{1,0:T(8,128)}) custom-call(s32[6]{0:T(128)S(1)} %bitcast.30, bf16[16,528,128]{2,1,0:T(8,128)(2,1)} %all-to-all-done.1.x_ref, bf16[192,512]{1,0:T(8,128)(2,1)S(1)} %copy-done.8), custom_call_target="tpu_custom_call" | custom-call | flops 10737418240 | bytes 5242880 | tf_op jit(solution)/shard_map/attention/pallas_call | solution.py:482
  66.6 10.2 %all-to-all-done.x_ref = bf16[16,512,128]{2,1,0:T(8,128)(2,1)S(1)} async-done(((bf16[16,512,128]{2,1,0:T(8,128)(2,1)}), bf16[16,512,128]{2,1,0:T(8,128)(2,1)S(1)}, u32[]{:S(2)}, u32[]{:S(2)}) %all-to-all-start) | async-done | bytes 2097184 | tf_op jit(solution)/shard_map/all_to_all | solution.py:475
  76.8 4.7 %all-to-all-start.3 = ((bf16[16,512,128]{2,1,0:T(8,128)(2,1)}), bf16[16,512,128]{2,1,0:T(8,128)(2,1)}, u32[]{:S(2)}, u32[]{:S(2)}) async-start(bf16[16,512,128]{2,1,0:T(8,128)(2,1)} %get-tuple-element.29), calls=%async_computation.3 | async-start | bytes 4194304 | tf_op jit(solution)/shard_map/all_to_all | solution.py:475
  81.5 13.5 %attention.3 = (bf16[16,528,128]{2,1,0:T(8,128)(2,1)}, f32[8,128]{1,0:T(8,128)S(1)}) custom-call(s32[6]{0:T(128)S(1)} %bitcast.31, bf16[16,512,128]{2,1,0:T(8,128)(2,1)S(1)} %all-to-all-done.x_ref, f32[2048,256]{1,0:T(8,128)} %get-tuple-element.25.rest_0_, f32[8,128]{1,0:T(8,128)S(1)} %get-tuple-element.26.rest_1_), custom_call_target="tpu_custom_call" | custom-call | flops 10737418240 | bytes 5242880 | tf_op jit(solution)/shard_map/attention/pallas_call | solution.py:482
  95.0 0.1 collective-permute-start
  95.1 1.2 collective-permute-done
  96.3 0.6 collective-permute-start.1
  96.9 3.0 %collective-permute-done.1 = f32[8,128]{1,0:T(8,128)S(1)} collective-permute-done((f32[8,128]{1,0:T(8,128)S(1)}, f32[8,128]{1,0:T(8,128)S(1)}, u32[]{:S(2)}, u32[]{:S(2)}) %collective-permute-start.1) | collective-permute-done | bytes 4128 | tf_op jit(solution)/shard_map/ppermute | solution.py:513
  99.9 3.8 %collective-permute-start.2 = (f32[8,128]{1,0:T(8,128)S(1)}, f32[8,128]{1,0:T(8,128)S(1)}, u32[]{:S(2)}, u32[]{:S(2)}) collective-permute-start(f32[8,128]{1,0:T(8,128)S(1)} %add.10), channel_id=1, source_target_pairs={{0,64},{16,80},{32,96},{48,112},{64,0},{80,16},{96,32},{112,48},{1... | collective-permute-start | bytes 12296 | tf_op jit(solution)/shard_map/ppermute | solution.py:513
  103.7 1.6 %collective-permute-done.2 = f32[8,128]{1,0:T(8,128)S(1)} collective-permute-done((f32[8,128]{1,0:T(8,128)S(1)}, f32[8,128]{1,0:T(8,128)S(1)}, u32[]{:S(2)}, u32[]{:S(2)}) %collective-permute-start.2) | collective-permute-done | bytes 4128 | tf_op jit(solution)/shard_map/ppermute | solution.py:513
  105.3 0.6 add.11.sum_ref
  105.8 1.5 insert.1
  107.3 0.0 copy-start
  107.3 0.0 copy-start.1
  107.4 0.0 copy-start.4
  107.4 0.0 copy-start.5
  107.4 1.7 %all-to-all-done.3.y_ref = bf16[16,512,128]{2,1,0:T(8,128)(2,1)} async-done(((bf16[16,512,128]{2,1,0:T(8,128)(2,1)}), bf16[16,512,128]{2,1,0:T(8,128)(2,1)}, u32[]{:S(2)}, u32[]{:S(2)}) %all-to-all-start.3) | async-done | bytes 2097184 | tf_op jit(solution)/shard_map/all_to_all | solution.py:475
  109.0 5.5 %all-to-all-start.2 = ((bf16[16,528,128]{2,1,0:T(8,128)(2,1)}), bf16[16,528,128]{2,1,0:T(8,128)(2,1)}, u32[]{:S(2)}, u32[]{:S(2)}) async-start(bf16[16,528,128]{2,1,0:T(8,128)(2,1)} %insert.1), calls=%async_computation.2 | async-start | bytes 4325376 | tf_op jit(solution)/shard_map/all_to_all | solution.py:475
  114.6 2.9 %early.1 = (bf16[128,4096]{1,0:T(8,128)(2,1)}, bf16[128,4096]{1,0:T(8,128)(2,1)}, f32[2,128,2048]{2,1,0:T(8,128)S(1)}, f32[2,128,128]{2,1,0:T(8,128)S(1)}) custom-call(bf16[16,512,128]{2,1,0:T(8,128)(2,1)} %all-to-all-done.3.y_ref, bf16[128,4096]{1,0:T(8,128)(2,1)S(1)} %bitcast.17, bf16[128,4096]{1,0:T(8,128)(2,1)S(1)} %bitcast.21, f32[1,4096]{1,0:T(1,128)S(1)} %bitcast.25, ...), custom_call_target="tpu_custom_call" | custom-call | flops 20971520 | bytes 6291456 | tf_op jit(solution)/shard_map/early/pallas_call | solution.py:526
  117.4 1.3 copy-done.3
  118.7 0.7 copy-done.6
  119.4 24.6 %all-to-all-done.2.yb_hbm = bf16[16,528,128]{2,1,0:T(8,128)(2,1)} async-done(((bf16[16,528,128]{2,1,0:T(8,128)(2,1)}), bf16[16,528,128]{2,1,0:T(8,128)(2,1)}, u32[]{:S(2)}, u32[]{:S(2)}) %all-to-all-start.2) | async-done | bytes 2162720 | tf_op jit(solution)/shard_map/all_to_all | solution.py:475
  144.0 5.7 %receive.1 = (bf16[128,4096]{1,0:T(8,128)(2,1)}, bf16[128,4096]{1,0:T(8,128)(2,1)}, f32[1,4096]{1,0:T(1,128)}, f32[1,4096]{1,0:T(1,128)}, bf16[128,4096]{1,0:T(8,128)(2,1)}, /*index=5*/bf16[128,4096]{1,0:T(8,128)(2,1)}) custom-call(bf16[16,528,128]{2,1,0:T(8,128)(2,1)} %all-to-all-done.2.yb_hbm, ...), custom_call_target="tpu_custom_call", output_to_operand_aliasing={{4}: (8, {}), {5}: (9, {})} | custom-call | flops 41943040 | bytes 8388608 | tf_op jit(solution)/shard_map/receive/pallas_call | solution.py:536
  (10 shorter events, 0.0 us)
Async XLA Ops:
  6.0 39.5 %all-to-all-start.1 = ((bf16[16,528,128]{2,1,0:T(8,128)(2,1)}), bf16[16,528,128]{2,1,0:T(8,128)(2,1)}, u32[]{:S(2)}, u32[]{:S(2)}) async-start(bf16[16,528,128]{2,1,0:T(8,128)(2,1)} %get-tuple-element.24), calls=%async_computation.1 | async-start | bytes 4325376 | tf_op jit(solution)/shard_map/all_to_all | solution.py:475
  19.1 30.2 %copy-start.7 = (s32[1,6]{1,0:T(1,128)S(1)}, s32[1,6]{1,0:T(1,128)}, u32[]{:S(2)}) copy-start(s32[1,6]{1,0:T(1,128)} %param.16) | copy-start | bytes 76
  19.1 30.2 %copy-start.8 = (bf16[192,512]{1,0:T(8,128)(2,1)S(1)}, bf16[192,512]{1,0:T(8,128)(2,1)}, u32[]{:S(2)}) copy-start(bf16[192,512]{1,0:T(8,128)(2,1)} %constant.5.clone.rest_0_) | copy-start | bytes 589828
  45.5 31.4 %all-to-all-start = ((bf16[16,512,128]{2,1,0:T(8,128)(2,1)}), bf16[16,512,128]{2,1,0:T(8,128)(2,1)S(1)}, u32[]{:S(2)}, u32[]{:S(2)}) async-start(bf16[16,512,128]{2,1,0:T(8,128)(2,1)} %send.3), calls=%async_computation | async-start | bytes 4194304 | tf_op jit(solution)/shard_map/all_to_all | solution.py:475
  76.8 32.2 %all-to-all-start.3 = ((bf16[16,512,128]{2,1,0:T(8,128)(2,1)}), bf16[16,512,128]{2,1,0:T(8,128)(2,1)}, u32[]{:S(2)}, u32[]{:S(2)}) async-start(bf16[16,512,128]{2,1,0:T(8,128)(2,1)} %get-tuple-element.29), calls=%async_computation.3 | async-start | bytes 4194304 | tf_op jit(solution)/shard_map/all_to_all | solution.py:475
  95.0 1.2 collective-permute-start
  96.3 3.6 %collective-permute-start.1 = (f32[8,128]{1,0:T(8,128)S(1)}, f32[8,128]{1,0:T(8,128)S(1)}, u32[]{:S(2)}, u32[]{:S(2)}) collective-permute-start(f32[8,128]{1,0:T(8,128)S(1)} %add.9), channel_id=1, source_target_pairs={{0,32},{16,48},{32,0},{48,16},{64,96},{80,112},{96,64},{112,80},{1... | collective-permute-start | bytes 12296 | tf_op jit(solution)/shard_map/ppermute | solution.py:513
  99.9 5.3 %collective-permute-start.2 = (f32[8,128]{1,0:T(8,128)S(1)}, f32[8,128]{1,0:T(8,128)S(1)}, u32[]{:S(2)}, u32[]{:S(2)}) collective-permute-start(f32[8,128]{1,0:T(8,128)S(1)} %add.10), channel_id=1, source_target_pairs={{0,64},{16,80},{32,96},{48,112},{64,0},{80,16},{96,32},{112,48},{1... | collective-permute-start | bytes 12296 | tf_op jit(solution)/shard_map/ppermute | solution.py:513
  107.3 7.2 %copy-start = (bf16[1,128,4096]{2,1,0:T(8,128)(2,1)S(1)}, bf16[1,128,4096]{2,1,0:T(8,128)(2,1)}, u32[]{:S(2)}) copy-start(bf16[1,128,4096]{2,1,0:T(8,128)(2,1)} %param.10) | copy-start | bytes 3145732
  107.3 7.2 %copy-start.1 = (bf16[1,128,4096]{2,1,0:T(8,128)(2,1)S(1)}, bf16[1,128,4096]{2,1,0:T(8,128)(2,1)}, u32[]{:S(2)}) copy-start(bf16[1,128,4096]{2,1,0:T(8,128)(2,1)} %param.11) | copy-start | bytes 3145732
  107.4 7.2 %copy-start.2 = (f32[4,128,128]{2,1,0:T(8,128)S(1)}, f32[4,128,128]{2,1,0:T(8,128)}, u32[]{:S(2)}) copy-start(f32[4,128,128]{2,1,0:T(8,128)} %get-tuple-element.23.rest_0_.aside_ref.aside_hbm) | copy-start | bytes 786436
  107.4 7.2 %copy-start.4 = (f32[4096]{0:T(1024)S(1)}, f32[4096]{0:T(1024)}, u32[]{:S(2)}) copy-start(f32[4096]{0:T(1024)} %param.14) | copy-start | bytes 49156
  107.4 7.2 %copy-start.5 = (f32[4096]{0:T(1024)S(1)}, f32[4096]{0:T(1024)}, u32[]{:S(2)}) copy-start(f32[4096]{0:T(1024)} %param.15) | copy-start | bytes 49156
  109.0 35.0 %all-to-all-start.2 = ((bf16[16,528,128]{2,1,0:T(8,128)(2,1)}), bf16[16,528,128]{2,1,0:T(8,128)(2,1)}, u32[]{:S(2)}, u32[]{:S(2)}) async-start(bf16[16,528,128]{2,1,0:T(8,128)(2,1)} %insert.1), calls=%async_computation.2 | async-start | bytes 4325376 | tf_op jit(solution)/shard_map/all_to_all | solution.py:475
  117.4 1.3 copy-start.3
  118.7 0.7 copy-start.6

commit v5 on v4

--- a/solution.py
+++ b/solution.py
@@ -362,36 +362,28 @@
         copy.wait()
 
 
-def receive_kernel(buckets, yb_hbm, q_hbm, k_hbm, qg_hbm, kg_hbm, aside_hbm, lift_hbm, total_hbm, att_in, gv_in, gq_hbm, gk_hbm, gqg_ref, gkg_ref, att_hbm, gv_hbm, yb, raw, gains, aside, before, totals, lift_ref, stage, small_sem, raw_sem, lift_sem, y_sem, spread_sem, sem):
+def receive_kernel(buckets, yb_hbm, q_ref, k_ref, qg_ref, kg_ref, aside, lift_hbm, totals, att_in, gv_in, gq_hbm, gk_hbm, gqg_ref, gkg_ref, att_hbm, gv_hbm, yb, before, lift_ref, stage, lift_sem, y_sem, spread_sem, sem):
     del att_in, gv_in
-    tokens, feature = q_hbm.shape
+    raw, gains = (q_ref, k_ref), (qg_ref, kg_ref)
+    tokens, feature = q_ref.shape
     members = yb_hbm.shape[0]
     local = feature // members // HEAD_DIM
     groups = y_sem.shape[0]
     group = members // groups
-    sources = ((aside_hbm, aside), (total_hbm, totals), (qg_hbm, gains.at[0]), (kg_hbm, gains.at[1]))
-    small = [pltpu.make_async_copy(source, target, small_sem.at[a]) for a, (source, target) in enumerate(sources)]
-    raws = [pltpu.make_async_copy(ref, raw.at[a], raw_sem.at[a]) for a, ref in enumerate((q_hbm, k_hbm))]
-    lifts = [pltpu.make_async_copy(lift_hbm.at[a], before.at[a], lift_sem.at[a]) for a in range(2)]
-
     def arrive(n):
         some = slice(n * group, (n + 1) * group)
         return pltpu.make_async_copy(yb_hbm.at[some], yb.at[some], y_sem.at[n])
 
-    for copy in small + raws[:1]:
-        copy.start()
     for n in range(groups):
         arrive(n).start()
-    for copy in lifts[:1] + raws[1:] + lifts[1:]:
+    lifts = [pltpu.make_async_copy(lift_hbm.at[a], before.at[a], lift_sem.at[a]) for a in range(2)]
+    for copy in lifts:
         copy.start()
-    for copy in small:
-        copy.wait()
     copies = []
     parts = sem.shape[1]
     width = feature // parts
     number = 2 * local
     for a, grad_hbm in enumerate((gq_hbm, gk_hbm)):
-        raws[a].wait()
         total = totals[a]
         for j in range(members):
             if a == 0 and j % group == 0:
@@ -404,18 +396,18 @@
             at = slice((j * local + 1) * HEAD_DIM, (j * local + 2) * HEAD_DIM)
             g = yb[j, (a + 1) * tokens : (a + 2) * tokens, :].astype(F32)
             g = g * aside[0] - pltpu.roll(g, HALF, 1) * aside[1]
-            lift = g * gains[a, :, at]
+            lift = g * gains[a][:, at]
             lift_ref[a, :, j * HEAD_DIM : (j + 1) * HEAD_DIM] = lift
-            total = total + lift * (raw[a, :, at].astype(F32) * aside[2 + a])
+            total = total + lift * (raw[a][:, at].astype(F32) * aside[2 + a])
         inner = jnp.sum(total, axis=-1, keepdims=True) / feature
+        lifts[a].wait()
         lean = jnp.broadcast_to(inner, (tokens, HEAD_DIM)) * aside[2 + a]
-        lifts[a].wait()
         for part in range(parts):
             for block in range(part * width // HEAD_DIM, (part + 1) * width // HEAD_DIM):
                 at = slice(block * HEAD_DIM, (block + 1) * HEAD_DIM)
                 j, h = divmod(block, local)
                 lift = (before, lift_ref)[h][a, :, j * HEAD_DIM : (j + 1) * HEAD_DIM]
-                stage[a, :, at] = (aside[2 + a] * (lift - raw[a, :, at].astype(F32) * lean)).astype(BF16)
+                stage[a, :, at] = (aside[2 + a] * (lift - raw[a][:, at].astype(F32) * lean)).astype(BF16)
             at = slice(part * width, (part + 1) * width)
             copies.append(pltpu.make_async_copy(stage.at[a, :, at], grad_hbm.at[:, at], sem.at[a, part]))
             copies[-1].start()
@@ -424,8 +416,8 @@
         total = rows[:number] + rows[number : 2 * number] + rows[2 * number : 3 * number]
         for h in range(local):
             at = slice((j * local + h) * HEAD_DIM, (j * local + h + 1) * HEAD_DIM)
-            gqg_ref[:, at] = total[2 * h : 2 * h + 1] / (gains[0, :, at] * buckets)
-            gkg_ref[:, at] = total[2 * h + 1 : 2 * h + 2] / (gains[1, :, at] * buckets)
+            gqg_ref[:, at] = total[2 * h : 2 * h + 1] / (gains[0][:, at] * buckets)
+            gkg_ref[:, at] = total[2 * h + 1 : 2 * h + 2] / (gains[1][:, at] * buckets)
     for copy in copies:
         copy.wait()
 
@@ -529,33 +521,27 @@
         in_specs=[vmem] * 6,
         out_specs=(hbm, hbm, hbm, vmem),
         scratch_shapes=[pltpu.VMEM(half_shape.shape, F32), sems((members, 2)), sems((2,))],
-        compiler_params=pltpu.CompilerParams(vmem_limit_bytes=24 << 20),
+        compiler_params=pltpu.CompilerParams(vmem_limit_bytes=60 << 20),
         cost_estimate=pl.CostEstimate(flops=20 << 20, bytes_accessed=6 << 20, transcendentals=0),
         name="early",
     )(y_a, q_raw[0], k_raw[0], q_gain[None], k_gain[None], aside)
     grad_q, grad_k, q_sum, k_sum, attended, grad_v = pl.pallas_call(
         functools.partial(receive_kernel, replicas),
         out_shape=(row_shape, row_shape, shape((1, feature), F32), shape((1, feature), F32), row_shape, row_shape),
-        in_specs=[hbm] * 10,
+        in_specs=[hbm] + [vmem] * 5 + [hbm, vmem] + [hbm] * 2,
         out_specs=(hbm, hbm, vmem, vmem, hbm, hbm),
         scratch_shapes=[
             pltpu.VMEM(longer.shape, BF16),
-            pltpu.VMEM((2, tok, feature), BF16),
-            pltpu.VMEM((2, 1, feature), F32),
-            pltpu.VMEM((4, tok, HEAD_DIM), F32),
             pltpu.VMEM(half_shape.shape, F32),
-            pltpu.VMEM(total_shape.shape, F32),
             pltpu.VMEM(half_shape.shape, F32),
             pltpu.VMEM((2, tok, feature), BF16),
-            sems((4,)),
-            sems((2,)),
             sems((2,)),
             sems((4,)),
             sems((members, 2)),
             sems((2, 4)),
         ],
         input_output_aliases={8: 4, 9: 5},
-        compiler_params=pltpu.CompilerParams(vmem_limit_bytes=60 << 20),
+        compiler_params=pltpu.CompilerParams(vmem_limit_bytes=24 << 20),
         cost_estimate=pl.CostEstimate(flops=40 << 20, bytes_accessed=8 << 20, transcendentals=0),
         name="receive",
     )(y_b, q_raw[0], k_raw[0], q_gain[None], k_gain[None], aside, lift, totals, attended, grad_v)

time: 151 us -> 153 us (1.013)
  Pallas kernels: 51.1 us -> 55.7 us
  waiting for transfers between devices: 68.5 us -> 66.6 us
    all_to_all x4, waiting for transfers between devices: 62.8 us -> 59 us  [exchange(): return lax.all_to_all(packet, 'seq', 0, 0, tiled=True)]
    pallas_call x2, Pallas kernels: 30.8 us -> 33.8 us  [attend(): pl.pallas_call(functools.partial(attention_kernel, head), out_shape=outs...]
    pallas_call x1, Pallas kernels: 2.85 us -> 5.46 us  [on_device(): pl.pallas_call(functools.partial(early_kernel, local), out_shape=(row_sha...]
    ppermute x3, starting transfers between devices: 4.45 us -> 2.32 us  [on_device(): lax.ppermute(sums, 'dp', [(i, i ^ distance) for i in range(replicas)])]
    ppermute x3, waiting for transfers between devices: 5.74 us -> 7.64 us  [on_device(): lax.ppermute(sums, 'dp', [(i, i ^ distance) for i in range(replicas)])]
  transfers between devices with their start and end apart: 7 -> 7, of which waited for: 7 -> 7; matrix products, arithmetic and copies ran while one was open for 0% -> 0% of each run, Pallas kernels for 23% -> 27%
where the time goes in v5:
time: 153 us; the launch traced here: 152 us
  waiting for transfers between devices  66.6 us (44%)
  Pallas kernels  55.7 us (36%)
  starting transfers between devices  25.6 us (17%)
  local copies, waits for them, and re-layouts  2.53 us (2%)
    all_to_all x4, waiting for transfers between devices, exchange(): return lax.all_to_all(packet, 'seq', 0, 0, tiled=True)  59 us
    pallas_call x2, Pallas kernels, attend(): pl.pallas_call(functools.partial(attention_kernel, head), out_shape=outs...  33.8 us
    all_to_all x4, starting transfers between devices, exchange(): return lax.all_to_all(packet, 'seq', 0, 0, tiled=True)  23.3 us
    pallas_call x2, Pallas kernels, send(): pl.pallas_call(functools.partial(send_kernel, head), out_shape=(packet, s...  10.2 us
    ppermute x3, waiting for transfers between devices, on_device(): lax.ppermute(sums, 'dp', [(i, i ^ distance) for i in range(replicas)])  7.64 us
    pallas_call x1, Pallas kernels, on_device(): pl.pallas_call(functools.partial(early_kernel, local), out_shape=(row_sha...  5.46 us
    pallas_call x1, Pallas kernels, on_device(): pl.pallas_call(functools.partial(receive_kernel, replicas), out_shape=(ro...  4.75 us
  transfers between devices with their start and end apart: 7, of which 7 were waited for; matrix products, arithmetic and copies ran while one was open for 0% of the time, Pallas kernels for 27%

profile of v5, /device:TPU:0, one launch (start us, length us, event | category | flops | bytes accessed | tf_op | source)
XLA Modules:
  0.0 152.1 jit_solution(2653983314886572363)
XLA Ops:
  0.6 5.3 %send.2 = (bf16[16,528,128]{2,1,0:T(8,128)(2,1)}, f32[4,128,128]{2,1,0:T(8,128)}) custom-call(bf16[128,4096]{1,0:T(8,128)(2,1)} %bitcast.14, bf16[128,4096]{1,0:T(8,128)(2,1)} %bitcast.18, bf16[128,4096]{1,0:T(8,128)(2,1)} %bitcast.32, bf16[128,4096]{1,0:T(8,128)(2,1)} %bitcast.34, f32[1,4096]{1,0:T(1,128)} %bitcast.22, f32[1,4096]{1,0:T(1,128)} %bitcast.26, ...), custom_call_target="tpu_custom_call" | custom-call | flops 20971520 | bytes 6291456 | tf_op jit(solution)/shard_map/send/pallas_call | solution.py:448
  5.9 8.2 %all-to-all-start.1 = ((bf16[16,528,128]{2,1,0:T(8,128)(2,1)}), bf16[16,528,128]{2,1,0:T(8,128)(2,1)}, u32[]{:S(2)}, u32[]{:S(2)}) async-start(bf16[16,528,128]{2,1,0:T(8,128)(2,1)} %get-tuple-element.24), calls=%async_computation.1 | async-start | bytes 4325376 | tf_op jit(solution)/shard_map/all_to_all | solution.py:467
  14.1 4.9 %send.3 = bf16[16,512,128]{2,1,0:T(8,128)(2,1)} custom-call(bf16[128,4096]{1,0:T(8,128)(2,1)} %bitcast.15, bf16[128,4096]{1,0:T(8,128)(2,1)} %bitcast.19, bf16[128,4096]{1,0:T(8,128)(2,1)} %bitcast.33, bf16[128,4096]{1,0:T(8,128)(2,1)} %bitcast.35, f32[1,4096]{1,0:T(1,128)} %bitcast.23, f32[1,4096]{1,0:T(1,128)} %bitcast.27, s32[3,1,128]{2,1,0:T(1,128)} %bitcast.39, ...), custom_call_target="tpu_custom_call" | custom-call | flops 20971520 | bytes 6291456 | tf_op jit(solution)/shard_map/send/pallas_call | solution.py:448
  19.0 0.0 copy-start.7
  19.1 0.0 copy-start.8
  19.1 26.3 %all-to-all-done.1.x_ref = bf16[16,528,128]{2,1,0:T(8,128)(2,1)} async-done(((bf16[16,528,128]{2,1,0:T(8,128)(2,1)}), bf16[16,528,128]{2,1,0:T(8,128)(2,1)}, u32[]{:S(2)}, u32[]{:S(2)}) %all-to-all-start.1) | async-done | bytes 2162720 | tf_op jit(solution)/shard_map/all_to_all | solution.py:467
  45.4 3.9 %all-to-all-start = ((bf16[16,512,128]{2,1,0:T(8,128)(2,1)}), bf16[16,512,128]{2,1,0:T(8,128)(2,1)S(1)}, u32[]{:S(2)}, u32[]{:S(2)}) async-start(bf16[16,512,128]{2,1,0:T(8,128)(2,1)} %send.3), calls=%async_computation | async-start | bytes 4194304 | tf_op jit(solution)/shard_map/all_to_all | solution.py:467
  49.3 18.8 %attention.2 = (bf16[16,512,128]{2,1,0:T(8,128)(2,1)}, f32[8,128]{1,0:T(8,128)S(1)}, f32[2048,256]{1,0:T(8,128)}) custom-call(s32[6]{0:T(128)S(1)} %bitcast.30, bf16[16,528,128]{2,1,0:T(8,128)(2,1)} %all-to-all-done.1.x_ref, bf16[192,512]{1,0:T(8,128)(2,1)S(1)} %copy-done.8), custom_call_target="tpu_custom_call" | custom-call | flops 10737418240 | bytes 5242880 | tf_op jit(solution)/shard_map/attention/pallas_call | solution.py:474
  68.1 8.7 %all-to-all-done.x_ref = bf16[16,512,128]{2,1,0:T(8,128)(2,1)S(1)} async-done(((bf16[16,512,128]{2,1,0:T(8,128)(2,1)}), bf16[16,512,128]{2,1,0:T(8,128)(2,1)S(1)}, u32[]{:S(2)}, u32[]{:S(2)}) %all-to-all-start) | async-done | bytes 2097184 | tf_op jit(solution)/shard_map/all_to_all | solution.py:467
  76.8 4.7 %all-to-all-start.3 = ((bf16[16,512,128]{2,1,0:T(8,128)(2,1)}), bf16[16,512,128]{2,1,0:T(8,128)(2,1)}, u32[]{:S(2)}, u32[]{:S(2)}) async-start(bf16[16,512,128]{2,1,0:T(8,128)(2,1)} %get-tuple-element.29), calls=%async_computation.3 | async-start | bytes 4194304 | tf_op jit(solution)/shard_map/all_to_all | solution.py:467
  81.5 15.0 %attention.3 = (bf16[16,528,128]{2,1,0:T(8,128)(2,1)}, f32[8,128]{1,0:T(8,128)S(1)}) custom-call(s32[6]{0:T(128)S(1)} %bitcast.31, bf16[16,512,128]{2,1,0:T(8,128)(2,1)S(1)} %all-to-all-done.x_ref, f32[2048,256]{1,0:T(8,128)} %get-tuple-element.25.rest_0_, f32[8,128]{1,0:T(8,128)S(1)} %get-tuple-element.26.rest_1_), custom_call_target="tpu_custom_call" | custom-call | flops 10737418240 | bytes 5242880 | tf_op jit(solution)/shard_map/attention/pallas_call | solution.py:474
  96.5 0.1 collective-permute-start
  96.6 1.2 collective-permute-done
  97.7 0.0 collective-permute-start.1
  97.7 3.6 %collective-permute-done.1 = f32[8,128]{1,0:T(8,128)S(1)} collective-permute-done((f32[8,128]{1,0:T(8,128)S(1)}, f32[8,128]{1,0:T(8,128)S(1)}, u32[]{:S(2)}, u32[]{:S(2)}) %collective-permute-start.1) | collective-permute-done | bytes 4128 | tf_op jit(solution)/shard_map/ppermute | solution.py:505
  101.4 2.2 %collective-permute-start.2 = (f32[8,128]{1,0:T(8,128)S(1)}, f32[8,128]{1,0:T(8,128)S(1)}, u32[]{:S(2)}, u32[]{:S(2)}) collective-permute-start(f32[8,128]{1,0:T(8,128)S(1)} %add.10), channel_id=1, source_target_pairs={{0,64},{16,80},{32,96},{48,112},{64,0},{80,16},{96,32},{112,48},{1... | collective-permute-start | bytes 12296 | tf_op jit(solution)/shard_map/ppermute | solution.py:505
  103.6 2.9 %collective-permute-done.2 = f32[8,128]{1,0:T(8,128)S(1)} collective-permute-done((f32[8,128]{1,0:T(8,128)S(1)}, f32[8,128]{1,0:T(8,128)S(1)}, u32[]{:S(2)}, u32[]{:S(2)}) %collective-permute-start.2) | collective-permute-done | bytes 4128 | tf_op jit(solution)/shard_map/ppermute | solution.py:505
  106.5 0.6 add.11.sum_ref
  107.1 1.5 insert.1
  108.6 0.4 all-to-all-done.3.y_ref
  109.0 6.6 %all-to-all-start.2 = ((bf16[16,528,128]{2,1,0:T(8,128)(2,1)}), bf16[16,528,128]{2,1,0:T(8,128)(2,1)}, u32[]{:S(2)}, u32[]{:S(2)}) async-start(bf16[16,528,128]{2,1,0:T(8,128)(2,1)} %insert.1), calls=%async_computation.2 | async-start | bytes 4325376 | tf_op jit(solution)/shard_map/all_to_all | solution.py:467
  115.6 0.0 copy-start
  115.6 0.0 copy-start.1
  115.6 0.0 copy-start.2
  115.6 0.0 copy-start.4
  115.6 0.0 copy-start.5
  115.6 5.5 %early.1 = (bf16[128,4096]{1,0:T(8,128)(2,1)}, bf16[128,4096]{1,0:T(8,128)(2,1)}, f32[2,128,2048]{2,1,0:T(8,128)}, f32[2,128,128]{2,1,0:T(8,128)}) custom-call(bf16[16,512,128]{2,1,0:T(8,128)(2,1)} %all-to-all-done.3.y_ref, bf16[128,4096]{1,0:T(8,128)(2,1)} %bitcast.16, bf16[128,4096]{1,0:T(8,128)(2,1)} %bitcast.20, f32[1,4096]{1,0:T(1,128)} %bitcast.24, ...), custom_call_target="tpu_custom_call" | custom-call | flops 20971520 | bytes 6291456 | tf_op jit(solution)/shard_map/early/pallas_call | solution.py:518
  121.1 23.6 %all-to-all-done.2.yb_hbm = bf16[16,528,128]{2,1,0:T(8,128)(2,1)} async-done(((bf16[16,528,128]{2,1,0:T(8,128)(2,1)}), bf16[16,528,128]{2,1,0:T(8,128)(2,1)}, u32[]{:S(2)}, u32[]{:S(2)}) %all-to-all-start.2) | async-done | bytes 2162720 | tf_op jit(solution)/shard_map/all_to_all | solution.py:467
  144.7 0.0 copy-done.4
  144.7 1.6 %copy-done.3 = f32[2,128,2048]{2,1,0:T(8,128)S(1)} copy-done((f32[2,128,2048]{2,1,0:T(8,128)S(1)}, f32[2,128,2048]{2,1,0:T(8,128)}, u32[]{:S(2)}) %copy-start.3) | copy-done | bytes 2097176
  146.3 0.9 copy-done.6
  147.2 4.7 %receive.1 = (bf16[128,4096]{1,0:T(8,128)(2,1)}, bf16[128,4096]{1,0:T(8,128)(2,1)}, f32[1,4096]{1,0:T(1,128)}, f32[1,4096]{1,0:T(1,128)}, bf16[128,4096]{1,0:T(8,128)(2,1)}, /*index=5*/bf16[128,4096]{1,0:T(8,128)(2,1)}) custom-call(bf16[16,528,128]{2,1,0:T(8,128)(2,1)} %all-to-all-done.2.yb_hbm, ...), custom_call_target="tpu_custom_call", output_to_operand_aliasing={{4}: (8, {}), {5}: (9, {})} | custom-call | flops 41943040 | bytes 8388608 | tf_op jit(solution)/shard_map/receive/pallas_call | solution.py:528
  (10 shorter events, 0.0 us)
Async XLA Ops:
  5.9 39.5 %all-to-all-start.1 = ((bf16[16,528,128]{2,1,0:T(8,128)(2,1)}), bf16[16,528,128]{2,1,0:T(8,128)(2,1)}, u32[]{:S(2)}, u32[]{:S(2)}) async-start(bf16[16,528,128]{2,1,0:T(8,128)(2,1)} %get-tuple-element.24), calls=%async_computation.1 | async-start | bytes 4325376 | tf_op jit(solution)/shard_map/all_to_all | solution.py:467
  19.0 30.3 %copy-start.7 = (s32[1,6]{1,0:T(1,128)S(1)}, s32[1,6]{1,0:T(1,128)}, u32[]{:S(2)}) copy-start(s32[1,6]{1,0:T(1,128)} %param.16) | copy-start | bytes 76
  19.1 30.3 %copy-start.8 = (bf16[192,512]{1,0:T(8,128)(2,1)S(1)}, bf16[192,512]{1,0:T(8,128)(2,1)}, u32[]{:S(2)}) copy-start(bf16[192,512]{1,0:T(8,128)(2,1)} %constant.5.clone.rest_0_) | copy-start | bytes 589828
  45.4 31.4 %all-to-all-start = ((bf16[16,512,128]{2,1,0:T(8,128)(2,1)}), bf16[16,512,128]{2,1,0:T(8,128)(2,1)S(1)}, u32[]{:S(2)}, u32[]{:S(2)}) async-start(bf16[16,512,128]{2,1,0:T(8,128)(2,1)} %send.3), calls=%async_computation | async-start | bytes 4194304 | tf_op jit(solution)/shard_map/all_to_all | solution.py:467
  76.8 32.2 %all-to-all-start.3 = ((bf16[16,512,128]{2,1,0:T(8,128)(2,1)}), bf16[16,512,128]{2,1,0:T(8,128)(2,1)}, u32[]{:S(2)}, u32[]{:S(2)}) async-start(bf16[16,512,128]{2,1,0:T(8,128)(2,1)} %get-tuple-element.29), calls=%async_computation.3 | async-start | bytes 4194304 | tf_op jit(solution)/shard_map/all_to_all | solution.py:467
  96.5 1.2 collective-permute-start
  97.7 3.6 %collective-permute-start.1 = (f32[8,128]{1,0:T(8,128)S(1)}, f32[8,128]{1,0:T(8,128)S(1)}, u32[]{:S(2)}, u32[]{:S(2)}) collective-permute-start(f32[8,128]{1,0:T(8,128)S(1)} %add.9), channel_id=1, source_target_pairs={{0,32},{16,48},{32,0},{48,16},{64,96},{80,112},{96,64},{112,80},{1... | collective-permute-start | bytes 12296 | tf_op jit(solution)/shard_map/ppermute | solution.py:505
  101.4 5.1 %collective-permute-start.2 = (f32[8,128]{1,0:T(8,128)S(1)}, f32[8,128]{1,0:T(8,128)S(1)}, u32[]{:S(2)}, u32[]{:S(2)}) collective-permute-start(f32[8,128]{1,0:T(8,128)S(1)} %add.10), channel_id=1, source_target_pairs={{0,64},{16,80},{32,96},{48,112},{64,0},{80,16},{96,32},{112,48},{1... | collective-permute-start | bytes 12296 | tf_op jit(solution)/shard_map/ppermute | solution.py:505
  109.0 35.7 %all-to-all-start.2 = ((bf16[16,528,128]{2,1,0:T(8,128)(2,1)}), bf16[16,528,128]{2,1,0:T(8,128)(2,1)}, u32[]{:S(2)}, u32[]{:S(2)}) async-start(bf16[16,528,128]{2,1,0:T(8,128)(2,1)} %insert.1), calls=%async_computation.2 | async-start | bytes 4325376 | tf_op jit(solution)/shard_map/all_to_all | solution.py:467
  115.6 29.1 %copy-start = (bf16[1,128,4096]{2,1,0:T(8,128)(2,1)S(1)}, bf16[1,128,4096]{2,1,0:T(8,128)(2,1)}, u32[]{:S(2)}) copy-start(bf16[1,128,4096]{2,1,0:T(8,128)(2,1)} %param.10) | copy-start | bytes 3145732
  115.6 29.1 %copy-start.1 = (bf16[1,128,4096]{2,1,0:T(8,128)(2,1)S(1)}, bf16[1,128,4096]{2,1,0:T(8,128)(2,1)}, u32[]{:S(2)}) copy-start(bf16[1,128,4096]{2,1,0:T(8,128)(2,1)} %param.11) | copy-start | bytes 3145732
  115.6 29.1 %copy-start.2 = (f32[4,128,128]{2,1,0:T(8,128)S(1)}, f32[4,128,128]{2,1,0:T(8,128)}, u32[]{:S(2)}) copy-start(f32[4,128,128]{2,1,0:T(8,128)} %get-tuple-element.23.rest_0_.aside_ref.aside) | copy-start | bytes 786436
  115.6 29.1 %copy-start.4 = (f32[4096]{0:T(1024)S(1)}, f32[4096]{0:T(1024)}, u32[]{:S(2)}) copy-start(f32[4096]{0:T(1024)} %param.14) | copy-start | bytes 49156
  115.6 29.1 %copy-start.5 = (f32[4096]{0:T(1024)S(1)}, f32[4096]{0:T(1024)}, u32[]{:S(2)}) copy-start(f32[4096]{0:T(1024)} %param.15) | copy-start | bytes 49156
  144.7 1.6 %copy-start.3 = (f32[2,128,2048]{2,1,0:T(8,128)S(1)}, f32[2,128,2048]{2,1,0:T(8,128)}, u32[]{:S(2)}) copy-start(f32[2,128,2048]{2,1,0:T(8,128)} %get-tuple-element.30.lift_hbm) | copy-start | bytes 6291460
  146.3 0.9 copy-start.6
